TPU v7x, 32 devices: a whole 2x2x4 slice. The times are simulated.
32 devices in a mesh: dp: 16 (over z, x, core), tensor: 2 (over y).
Axes of the slice: x: 2, y: 2, z: 4, core: 2. Of those that a mesh axis runs over, the one named last changes fastest.
Arguments:
- tokens: bfloat16 [1024, 16, 1152], P('tensor', 'dp'), may hold values from -6 to 6
- cond: bfloat16 [16, 1152], P('dp'), may hold values from -6 to 6
- mod_weight: bfloat16 [1152, 6912], P('dp'), may hold values from -0.1875 to 0.1875
- mod_bias: bfloat16 [6912], replicated, may hold values from -3 to 3
- query_key_value_weight: bfloat16 [1152, 3, 1152], P('dp', None, 'tensor'), may hold values from -0.1875 to 0.1875
- qkv_bias: bfloat16 [2, 1152], P(None, 'tensor'), may hold values from -3 to 3
- attention_out_weight: bfloat16 [1152, 1152], P('tensor', 'dp'), may hold values from -1.5 to 1.5
- attention_out_bias: bfloat16 [1152], replicated, may hold values from -3 to 3
- first_hidden_weight: bfloat16 [1152, 4608], P('dp', 'tensor'), may hold values from -0.1875 to 0.1875
- first_hidden_bias: bfloat16 [4608], P('tensor'), may hold values from -3 to 3
- second_hidden_weight: bfloat16 [4608, 1152], P('tensor', 'dp'), may hold values from -0.09375 to 0.09375
- second_hidden_bias: bfloat16 [1152], replicated, may hold values from -3 to 3
- out_grad: bfloat16 [1024, 16, 1152], P('tensor', 'dp'), may hold values from -6 to 6
Outputs:
- output: bfloat16 [1024, 16, 1152], P('tensor', 'dp')
- tokens_grad: bfloat16 [1024, 16, 1152], P('tensor', 'dp')
- cond_grad: float32 [16, 1152], P('dp')
- mod_weight_grad: float32 [1152, 6912], P('dp')
- mod_bias_grad: float32 [6912], replicated
- qkv_weight_grad: float32 [1152, 3, 1152], P('dp', None, 'tensor')
- qkv_bias_grad: float32 [2, 1152], P(None, 'tensor')
- proj_weight_grad: float32 [1152, 1152], P('tensor', 'dp')
- proj_bias_grad: float32 [1152], replicated
- fc1_weight_grad: float32 [1152, 4608], P('dp', 'tensor')
- fc1_bias_grad: float32 [4608], P('tensor')
- fc2_weight_grad: float32 [4608, 1152], P('tensor', 'dp')
- fc2_bias_grad: float32 [1152], replicated
All inputs are finite; a program needn't handle non-finite values.
Results may differ from a plain program's by a relative error of at most 0.02.
The roundings to bfloat16 on the way count: a program that leaves them out, or rounds other values in their place, can miss the bound.
Values may be sent and summed in bfloat16 or wider, within the bound.
A program may use at most 256 MiB of HBM per device.

v0:
```python
import jax
import jax.numpy as jnp
from jax import lax
from jax.sharding import PartitionSpec as P

HEADS = 16


def modulate(hidden, shifts, scales):
    center = hidden - jnp.mean(hidden, axis=-1, keepdims=True)
    spread = jnp.mean(center * center, axis=-1, keepdims=True)
    return center * lax.rsqrt(spread + 1e-06) * (1.0 + scales) + shifts


def gelu_tanh(values):
    return jax.nn.gelu(values, approximate=True)


def attend_forward(packed):
    queries = packed[:, 0]
    keys_all = packed[:, 1]
    values_all = packed[:, 2]
    seq_len = packed.shape[0]
    scaling = packed.shape[3] ** (-0.5)
    block_rows = min(512, seq_len)
    results = []
    log_parts = []
    for offset in range(0, seq_len, block_rows):
        query_block = queries[offset : offset + block_rows]
        scores = (
            jnp.einsum("qhe,khe->hqk", query_block, keys_all, preferred_element_type=jnp.float32)
            * scaling
        )
        highest = jnp.max(scores, axis=-1, keepdims=True)
        weights = jnp.exp(scores - highest)
        row_total = jnp.sum(weights, axis=-1, keepdims=True)
        prob_low = (weights / row_total).astype(jnp.bfloat16)
        mixture = jnp.einsum(
            "hqk,khe->qhe", prob_low, values_all, preferred_element_type=jnp.float32
        )
        results.append(mixture.reshape(block_rows, -1))
        log_parts.append((highest + jnp.log(row_total))[..., 0])
    return (jnp.concatenate(results, 0).astype(jnp.bfloat16), jnp.concatenate(log_parts, 1))


def attend_backward(inputs):
    packed, grad_out, log_totals = inputs
    queries = packed[:, 0]
    keys_all = packed[:, 1]
    values_all = packed[:, 2]
    seq_len = packed.shape[0]
    scaling = packed.shape[3] ** (-0.5)
    block_rows = min(512, seq_len)
    query_grads = []
    key_grad = jnp.zeros(keys_all.shape, jnp.float32)
    value_grad = jnp.zeros(values_all.shape, jnp.float32)
    for offset in range(0, seq_len, block_rows):
        query_block = queries[offset : offset + block_rows]
        grad_block = grad_out[offset : offset + block_rows]
        scores = (
            jnp.einsum("qhe,khe->hqk", query_block, keys_all, preferred_element_type=jnp.float32)
            * scaling
        )
        probs = jnp.exp(scores - log_totals[:, offset : offset + block_rows, None])
        prob_low = probs.astype(jnp.bfloat16)
        prob_grad = jnp.einsum(
            "qhe,khe->hqk", grad_block, values_all, preferred_element_type=jnp.float32
        )
        inner = jnp.sum(probs * prob_grad, axis=-1, keepdims=True)
        score_grad = (probs * (prob_grad - inner)).astype(jnp.bfloat16)
        query_grads.append(
            jnp.einsum("hqk,khe->qhe", score_grad, keys_all, preferred_element_type=jnp.float32)
            * scaling
        )
        key_grad = (
            key_grad
            + jnp.einsum(
                "hqk,qhe->khe", score_grad, query_block, preferred_element_type=jnp.float32
            )
            * scaling
        )
        value_grad = value_grad + jnp.einsum(
            "hqk,qhe->khe", prob_low, grad_block, preferred_element_type=jnp.float32
        )
    return jnp.stack([jnp.concatenate(query_grads, 0), key_grad, value_grad], 1).astype(
        jnp.bfloat16
    )


def on_device(
    tokens,
    cond,
    mod_weight,
    mod_bias,
    query_key_value_weight,
    qkv_bias,
    attention_out_weight,
    attention_out_bias,
    first_hidden_weight,
    first_hidden_bias,
    second_hidden_weight,
    second_hidden_bias,
    out_grad,
):
    w_mod, w_qkv, w_proj, w_fc1, w_fc2 = (
        lax.all_gather(mod_weight, "dp", axis=0, tiled=True),
        lax.all_gather(query_key_value_weight, "dp", axis=0, tiled=True),
        lax.all_gather(attention_out_weight, "dp", axis=1, tiled=True),
        lax.all_gather(first_hidden_weight, "dp", axis=0, tiled=True),
        lax.all_gather(second_hidden_weight, "dp", axis=1, tiled=True),
    )
    seq_local, latents, width = tokens.shape
    columns = query_key_value_weight.shape[2]
    head_size = width // HEADS
    heads_here = columns // head_size
    local_rows = seq_local * latents
    cond_wide = cond.astype(jnp.float32)
    silu_cond, silu_back = jax.vjp(jax.nn.silu, cond_wide)
    silu_low = silu_cond.astype(jnp.bfloat16)
    modulation = jnp.dot(silu_low, w_mod, preferred_element_type=jnp.float32) + mod_bias.astype(
        jnp.float32
    )
    pieces = modulation.reshape(latents, 6, width)
    hidden_in = tokens.astype(jnp.float32)
    attention_normalized, norm_a_back = jax.vjp(modulate, hidden_in, pieces[:, 0], pieces[:, 1])
    gathered_a = lax.all_gather(
        attention_normalized.astype(jnp.bfloat16), "tensor", axis=0, tiled=True
    )
    seq_len = gathered_a.shape[0]
    total_rows = seq_len * latents
    rows_a = gathered_a.reshape(total_rows, width)
    qkv_flat = w_qkv.reshape(width, 3 * columns)
    zero_row = jnp.zeros((columns,), jnp.float32)
    query_key_value_shift = jnp.stack(
        [qkv_bias[0].astype(jnp.float32), zero_row, qkv_bias[1].astype(jnp.float32)]
    )
    projected_output = (
        jnp.dot(rows_a, qkv_flat, preferred_element_type=jnp.float32).reshape(
            seq_len, latents, 3, columns
        )
        + query_key_value_shift
    )
    packed = jnp.moveaxis(projected_output.astype(jnp.bfloat16), 1, 0).reshape(
        latents, seq_len, 3, heads_here, head_size
    )
    attention_result, log_totals = lax.map(attend_forward, packed)
    attended_rows = jnp.moveaxis(attention_result, 0, 1).reshape(total_rows, columns)
    summed_a = lax.psum_scatter(
        jnp.dot(attended_rows, w_proj, preferred_element_type=jnp.float32).astype(jnp.bfloat16),
        "tensor",
        scatter_dimension=0,
        tiled=True,
    ).astype(jnp.float32)
    attention_branch = summed_a.reshape(seq_local, latents, width) + attention_out_bias.astype(
        jnp.float32
    )
    resid_mid = hidden_in + pieces[:, 2] * attention_branch
    feedforward_normalized, norm_m_back = jax.vjp(modulate, resid_mid, pieces[:, 3], pieces[:, 4])
    gathered_m = lax.all_gather(
        feedforward_normalized.astype(jnp.bfloat16), "tensor", axis=0, tiled=True
    )
    rows_m = gathered_m.reshape(total_rows, width)
    before_activation = jnp.dot(
        rows_m, w_fc1, preferred_element_type=jnp.float32
    ) + first_hidden_bias.astype(jnp.float32)
    gelu_activated, gelu_back = jax.vjp(gelu_tanh, before_activation)
    act_low = gelu_activated.astype(jnp.bfloat16)
    summed_m = lax.psum_scatter(
        jnp.dot(act_low, w_fc2, preferred_element_type=jnp.float32).astype(jnp.bfloat16),
        "tensor",
        scatter_dimension=0,
        tiled=True,
    ).astype(jnp.float32)
    feedforward_branch = summed_m.reshape(seq_local, latents, width) + second_hidden_bias.astype(
        jnp.float32
    )
    output = (resid_mid + pieces[:, 5] * feedforward_branch).astype(jnp.bfloat16)
    grad_out = out_grad.astype(jnp.float32)
    gate_m_grad = jnp.sum(grad_out * feedforward_branch, axis=0)
    grad_m_low = (grad_out * pieces[:, 5]).astype(jnp.bfloat16)
    grad_m_rows = lax.all_gather(grad_m_low, "tensor", axis=0, tiled=True).reshape(
        total_rows, width
    )
    fc2_bias_grad = jnp.sum(grad_m_rows, axis=0, dtype=jnp.float32)
    fc2_weight_grad = jnp.einsum(
        "rf,rd->fd", act_low, grad_m_rows, preferred_element_type=jnp.float32
    )
    act_grad = jnp.einsum("rd,fd->rf", grad_m_rows, w_fc2, preferred_element_type=jnp.float32)
    pre_grad = gelu_back(act_grad)[0].astype(jnp.bfloat16)
    fc1_bias_grad = jnp.sum(pre_grad, axis=0, dtype=jnp.float32)
    fc1_weight_grad = jnp.einsum("rd,rf->df", rows_m, pre_grad, preferred_element_type=jnp.float32)
    normed_m_grad = (
        lax.psum_scatter(
            jnp.einsum("rf,df->rd", pre_grad, w_fc1, preferred_element_type=jnp.float32).astype(
                jnp.bfloat16
            ),
            "tensor",
            scatter_dimension=0,
            tiled=True,
        )
        .astype(jnp.float32)
        .reshape(seq_local, latents, width)
    )
    resid_part, shift_m_grad, scale_m_grad = norm_m_back(normed_m_grad)
    resid_grad = grad_out + resid_part
    gate_a_grad = jnp.sum(resid_grad * attention_branch, axis=0)
    grad_a_low = (resid_grad * pieces[:, 2]).astype(jnp.bfloat16)
    grad_a_flat = grad_a_low.reshape(local_rows, width)
    proj_bias_part = jnp.sum(grad_a_flat, axis=0, dtype=jnp.float32)
    grad_a_rows = lax.all_gather(grad_a_low, "tensor", axis=0, tiled=True).reshape(
        total_rows, width
    )
    proj_weight_grad = jnp.einsum(
        "rc,rd->cd", attended_rows, grad_a_rows, preferred_element_type=jnp.float32
    )
    attended_grad = jnp.einsum(
        "rd,cd->rc", grad_a_rows, w_proj, preferred_element_type=jnp.float32
    ).astype(jnp.bfloat16)
    grad_packed = jnp.moveaxis(attended_grad.reshape(seq_len, latents, heads_here, head_size), 1, 0)
    qkv_grad_packed = lax.map(attend_backward, (packed, grad_packed, log_totals))
    qkv_grad_rows = jnp.moveaxis(qkv_grad_packed, 0, 1).reshape(total_rows, 3 * columns)
    bias_sums = jnp.sum(qkv_grad_rows.reshape(total_rows, 3, columns), axis=0, dtype=jnp.float32)
    qkv_bias_grad = jnp.stack([bias_sums[0], bias_sums[2]])
    qkv_weight_grad = jnp.einsum(
        "rd,rc->dc", rows_a, qkv_grad_rows, preferred_element_type=jnp.float32
    ).reshape(width, 3, columns)
    normed_a_grad = (
        lax.psum_scatter(
            jnp.einsum(
                "rc,dc->rd", qkv_grad_rows, qkv_flat, preferred_element_type=jnp.float32
            ).astype(jnp.bfloat16),
            "tensor",
            scatter_dimension=0,
            tiled=True,
        )
        .astype(jnp.float32)
        .reshape(seq_local, latents, width)
    )
    input_part, shift_a_grad, scale_a_grad = norm_a_back(normed_a_grad)
    tokens_grad = (resid_grad + input_part).astype(jnp.bfloat16)
    partial_mod = jnp.stack(
        [shift_a_grad, scale_a_grad, gate_a_grad, shift_m_grad, scale_m_grad, gate_m_grad], 1
    ).reshape(latents, 6 * width)
    mod_summed, proj_bias_grad = (
        lax.psum(partial_mod.astype(jnp.bfloat16), "tensor").astype(jnp.float32),
        lax.psum(proj_bias_part.astype(jnp.bfloat16), "tensor").astype(jnp.float32),
    )
    mod_grad_low = mod_summed.astype(jnp.bfloat16)
    silu_grad = jnp.einsum("le,de->ld", mod_grad_low, w_mod, preferred_element_type=jnp.float32)
    cond_grad = silu_back(silu_grad)[0]
    silu_every, mod_every = (
        lax.all_gather(silu_low, "dp", axis=0, tiled=True),
        lax.all_gather(mod_grad_low, "dp", axis=0, tiled=True),
    )
    owned_rows = mod_weight.shape[0]
    silu_owned = lax.dynamic_slice_in_dim(
        silu_every, lax.axis_index("dp") * owned_rows, owned_rows, 1
    )
    mod_weight_grad = jnp.einsum(
        "ld,le->de", silu_owned, mod_every, preferred_element_type=jnp.float32
    )
    mod_bias_grad = jnp.sum(mod_every, axis=0, dtype=jnp.float32)
    qkv_weight_grad, proj_weight_grad, fc1_weight_grad, fc2_weight_grad = (
        lax.psum_scatter(
            qkv_weight_grad.astype(jnp.bfloat16), "dp", scatter_dimension=0, tiled=True
        ).astype(jnp.float32),
        lax.psum_scatter(
            proj_weight_grad.astype(jnp.bfloat16), "dp", scatter_dimension=1, tiled=True
        ).astype(jnp.float32),
        lax.psum_scatter(
            fc1_weight_grad.astype(jnp.bfloat16), "dp", scatter_dimension=0, tiled=True
        ).astype(jnp.float32),
        lax.psum_scatter(
            fc2_weight_grad.astype(jnp.bfloat16), "dp", scatter_dimension=1, tiled=True
        ).astype(jnp.float32),
    )
    qkv_bias_grad, proj_bias_grad, fc1_bias_grad, fc2_bias_grad = lax.psum(
        (qkv_bias_grad, proj_bias_grad, fc1_bias_grad, fc2_bias_grad), "dp"
    )
    return (
        output,
        tokens_grad,
        cond_grad,
        mod_weight_grad,
        mod_bias_grad,
        qkv_weight_grad,
        qkv_bias_grad,
        proj_weight_grad,
        proj_bias_grad,
        fc1_weight_grad,
        fc1_bias_grad,
        fc2_weight_grad,
        fc2_bias_grad,
    )


def solution(mesh):
    return jax.shard_map(
        on_device,
        mesh=mesh,
        in_specs=(
            P("tensor", "dp", None),
            P("dp", None),
            P("dp", None),
            P(),
            P("dp", None, "tensor"),
            P(None, "tensor"),
            P("tensor", "dp"),
            P(),
            P("dp", "tensor"),
            P("tensor"),
            P("tensor", "dp"),
            P(),
            P("tensor", "dp", None),
        ),
        out_specs=(
            P("tensor", "dp", None),
            P("tensor", "dp", None),
            P("dp", None),
            P("dp", None),
            P(),
            P("dp", None, "tensor"),
            P(None, "tensor"),
            P("tensor", "dp"),
            P(),
            P("dp", "tensor"),
            P("tensor"),
            P("tensor", "dp"),
            P(),
        ),
        check_vma=False,
    )
```

profile of v0, /device:TPU:1, one launch (start us, length us, event | category | flops | bytes accessed | tf_op | source)
XLA Modules:
  0.0 1025.5 jit_solution(3620825164057800775)
XLA Ops:
  10.7 123.5 %all-gather.12.cloned.1.call-done = bf16[1152,6912]{1,0:T(8,128)(2,1)} async-done(((bf16[72,6912]{1,0:T(8,128)(2,1)}), bf16[1152,6912]{1,0:T(8,128)(2,1)}) %all-gather.12.cloned.1.call-update) | async-done | bytes 15925264 | tf_op jit(solution)/shard_map/all_gather | solution.py:106
  134.3 7.7 convolution_reduce_fusion
  145.4 41.1 %all-gather.16.cloned.1.call-done = bf16[1152,3,576]{2,0,1:T(8,128)(2,1)} async-done(((bf16[72,3,576]{2,0,1:T(8,128)(2,1)}), bf16[1152,3,576]{2,0,1:T(8,128)(2,1)}) %all-gather.16.cloned.1.call-update) | async-done | bytes 3981328 | tf_op jit(solution)/shard_map/all_gather | solution.py:107
  186.4 6.5 copy.29
  192.9 29.8 %all-gather.14.cloned.1.call-done = bf16[1024,1,1152]{2,0,1:T(8,128)(2,1)} async-done(((bf16[512,1,1152]{2,0,1:T(8,128)(2,1)}), bf16[1024,1,1152]{2,0,1:T(8,128)(2,1)}) %all-gather.14.cloned.1.call-update) | async-done | bytes 2359312 | tf_op jit(solution)/shard_map/all_gather | solution.py:126
  222.7 7.6 add_convert_fusion
  230.4 8.1 multiply_reduce_fusion.2
  241.0 13.6 %fusion.1 = f32[8,512]{1,0:T(8,128)S(1)} fusion(f32[8,512,1024]{2,1,0:T(8,128)} %get-tuple-element.73, f32[8,512]{1,0:T(8,128)S(1)} %get-tuple-element.72), kind=kLoop, calls=%fused_computation.11 | loop fusion | flops 12578816 | bytes 16809984 | tf_op jit(solution)/shard_map/while/body/eval_jaxpr/reduce_sum | solution.py:36
  254.7 7.9 fusion.75
  262.5 4.2 fusion
  267.4 4.7 fusion.76
  272.1 5.2 convolution_convert_fusion.6
  278.0 34.3 %reduce-scatter.13.cloned.1.call-done = bf16[512,1152]{1,0:T(8,128)(2,1)} async-done(((bf16[1024,1152]{1,0:T(8,128)(2,1)}), bf16[512,1152]{1,0:T(8,128)(2,1)}) %reduce-scatter.13.cloned.1.call-update) | async-done | bytes 1179664 | tf_op jit(solution)/shard_map/reduce_scatter | solution.py:148
  321.4 49.9 %all-gather.22.cloned.1.call-done = bf16[1152,2304]{1,0:T(8,128)(2,1)} async-done(((bf16[72,2304]{1,0:T(8,128)(2,1)}), bf16[1152,2304]{1,0:T(8,128)(2,1)}) %all-gather.22.cloned.1.call-update) | async-done | bytes 5308432 | tf_op jit(solution)/shard_map/all_gather | solution.py:109
  371.4 36.4 %all-gather.20.cloned.1.call-done = bf16[1024,1,1152]{2,0,1:T(8,128)(2,1)} async-done(((bf16[512,1,1152]{2,0,1:T(8,128)(2,1)}), bf16[1024,1,1152]{2,0,1:T(8,128)(2,1)}) %all-gather.20.cloned.1.call-update) | async-done | bytes 2359312 | tf_op jit(solution)/shard_map/all_gather | solution.py:159
  407.8 11.6 %fusion.57 = f32[1024,2304]{1,0:T(8,128)} fusion(bf16[1152,2304]{1,0:T(8,128)(2,1)} %all-gather.22.cloned.1.call-done, bf16[1024,1,1152]{2,0,1:T(8,128)(2,1)} %all-gather.20.cloned.1.call-done), kind=kOutput, calls=%fused_computation.98 | convolution fusion | flops 5435817984 | bytes 17104896 | tf_op jit(solution)/shard_map/dot_general | solution.py:163
  419.4 47.6 %all-gather.24.cloned.1.call-done = bf16[2304,1152]{0,1:T(8,128)(2,1)} async-done(((bf16[2304,72]{0,1:T(8,128)(2,1)}), bf16[2304,1152]{0,1:T(8,128)(2,1)}) %all-gather.24.cloned.1.call-update) | async-done | bytes 5308432 | tf_op jit(solution)/shard_map/all_gather | solution.py:110
  467.0 36.4 %all-gather.26.cloned.1.call-done = bf16[1024,1,1152]{2,0,1:T(8,128)(2,1)} async-done(((bf16[512,1,1152]{2,0,1:T(8,128)(2,1)}), bf16[1024,1,1152]{2,0,1:T(8,128)(2,1)}) %all-gather.26.cloned.1.call-update) | async-done | bytes 2359312 | tf_op jit(solution)/shard_map/all_gather | solution.py:181
  503.5 15.4 %convert_reduce_fusion = (f32[2304]{0:T(1024)}, bf16[1024,2304]{1,0:T(8,128)(2,1)S(1)}) fusion(f32[1024,2304]{1,0:T(8,128)} %fusion.57, f32[2304]{0:T(1024)} %convert_element_type.198, bf16[2304,1152]{0,1:T(8,128)(2,1)} %all-gather.24.cloned.1.call-done, bf16[1024,1,1152]{2,0,1:T(8,128)(2,1)} %all-gather.26.cloned.1.call-done), kind=kOutput, calls=%fused_computation.27 | convolution fusion | flops 5490079744 | bytes 21841920 | tf_op jit(solution)/shard_map/rd,fd->rf/dot_general | solution.py:188
  521.1 10.0 convolution_convert_fusion.3
  531.4 34.6 %reduce-scatter.17.cloned.1.call-done = bf16[512,1152]{1,0:T(8,128)(2,1)} async-done(((bf16[1024,1152]{1,0:T(8,128)(2,1)}), bf16[512,1152]{1,0:T(8,128)(2,1)}) %reduce-scatter.17.cloned.1.call-update) | async-done | bytes 1179664 | tf_op jit(solution)/shard_map/reduce_scatter | solution.py:193
  573.4 10.9 %convolution_convert_fusion = bf16[2304,1152]{0,1:T(8,128)(2,1)} fusion(bf16[1024,1,1152]{2,0,1:T(8,128)(2,1)S(1)} %copy-done.24, f32[1024,2304]{1,0:T(8,128)} %fusion.57, f32[2304]{0:T(1024)} %convert_element_type.198), kind=kOutput, calls=%fused_computation.16 | convolution fusion | flops 5462065152 | bytes 17114112 | tf_op jit(solution)/shard_map/rf,rd->fd/dot_general | solution.py:185
  586.0 9.7 convolution_convert_fusion.1
  595.8 13.1 %all-gather.28.cloned.1.call-done = bf16[1024,1,1152]{2,0,1:T(8,128)(2,1)} async-done(((bf16[512,1,1152]{2,0,1:T(8,128)(2,1)}), bf16[1024,1,1152]{2,0,1:T(8,128)(2,1)}) %all-gather.28.cloned.1.call-update) | async-done | bytes 2359312 | tf_op jit(solution)/shard_map/all_gather | solution.py:210
  613.2 15.6 %multiply_reduce_fusion.1 = (f32[8,512]{1,0:T(8,128)S(1)}, f32[8,512,1024]{2,1,0:T(8,128)}) fusion(f32[8,512,1024]{2,1,0:T(8,128)} %copy-done, f32[8,512]{1,0:T(8,128)S(1)} %log_add_fusion.1, bf16[512,8,72]{0,2,1:T(8,128)(2,1)S(1)} %bitcast.230, bf16[1024,3,8,72]{0,3,2,1:T(8,128)(2,1)} %bitcast.220), kind=kOutput, calls=%fused_computation.4 | convolution fusion | flops 620752896 | bytes 35356672 | tf_op jit(solution)/shard_map/while/body/eval_jaxpr/qhe,khe->hqk/dot_general | solution.py:66
  631.4 11.1 %multiply_convert_fusion.1 = bf16[8,512,1024]{2,1,0:T(8,128)(2,1)} fusion(f32[8,512,1024]{2,1,0:T(8,128)} %get-tuple-element.77, f32[8,512,1024]{2,1,0:T(8,128)S(1)} %bitcast.213, f32[8,512]{1,0:T(8,128)S(1)} %get-tuple-element.76, f32[8,512]{1,0:T(8,128)S(1)} %log_add_fusion.1), kind=kLoop, calls=%fused_computation.3 | loop fusion | flops 20971520 | bytes 41975808 | tf_op jit(solution)/shard_map/while/body/eval_jaxpr/convert_element_type | solution.py:70
  645.8 6.5 fusion.82
  655.8 12.1 %multiply_reduce_fusion = (f32[8,512]{1,0:T(8,128)}, f32[8,512,1024]{2,1,0:T(8,128)}) fusion(f32[8,512,1024]{2,1,0:T(8,128)} %get-tuple-element.73, f32[8,512]{1,0:T(8,128)S(1)} %copy-done.29, bf16[512,8,72]{0,2,1:T(8,128)(2,1)S(1)} %bitcast.232, bf16[1024,3,8,72]{0,3,2,1:T(8,128)(2,1)S(1)} %bitcast.225), kind=kOutput, calls=%fused_computation.1 | convolution fusion | flops 620752896 | bytes 35356672 | tf_op jit(solution)/shard_map/while/body/eval_jaxpr/qhe,khe->hqk/dot_general | solution.py:66
  667.9 13.0 %multiply_convert_fusion = bf16[8,512,1024]{2,1,0:T(8,128)(2,1)S(1)} fusion(f32[8,512,1024]{2,1,0:T(8,128)} %get-tuple-element.79, f32[8,512,1024]{2,1,0:T(8,128)} %get-tuple-element.73, f32[8,512]{1,0:T(8,128)} %get-tuple-element.78, f32[8,512]{1,0:T(8,128)} %log_add_fusion), kind=kLoop, calls=%fused_computation | loop fusion | flops 20971520 | bytes 41975808 | tf_op jit(solution)/shard_map/while/body/eval_jaxpr/convert_element_type | solution.py:70
  680.9 3.6 copy-done.3
  684.5 4.1 fusion.74
  688.6 7.6 fusion.11
  696.3 4.3 fusion.67
  702.8 5.8 add_multiply_fusion
  712.3 6.3 convolution_convert_fusion.5
  719.3 13.6 %convolution_convert_fusion.4 = bf16[1024,1152]{1,0:T(8,128)(2,1)} fusion(bf16[2304,1152]{0,1:T(8,128)(2,1)} %all-gather.24.cloned.1.call-done, f32[1024,2304]{1,0:T(8,128)} %fusion.57, f32[2304]{0:T(1024)S(1)} %copy-done.59), kind=kOutput, calls=%fused_computation.45 | convolution fusion | flops 5460590592 | bytes 17114112 | tf_op jit(solution)/shard_map/dot_general | solution.py:169
  734.6 7.6 convolution_convert_fusion.2
  742.2 18.2 %copy.34 = bf16[1152,3,576]{2,1,0:T(4,128)(2,1)} copy(bf16[1152,3,576]{2,0,1:T(8,128)(2,1)S(1)} %convolution_convert_fusion.2) | data formatting | bytes 7962624
  760.5 12.3 %reshape.346 = bf16[1152,1728]{1,0:T(8,128)(2,1)} reshape(bf16[1152,3,576]{2,1,0:T(4,128)(2,1)} %copy.34) | data formatting | bytes 7962624
  774.1 21.9 %all-gather = bf16[16,1,1152]{2,1,0:T(2,128)(2,1)S(1)} all-gather(bf16[1,1,1152]{2,1,0:T(2,128)(2,1)S(1)} %convert_bitcast_fusion.2), channel_id=1, replica_groups=mesh['dp'=16,'tensor'=2] {'dp'}, dimensions={0}, use_global_device_ids=true | all-gather | bytes 39168 | tf_op jit(solution)/shard_map/all_gather | solution.py:252
  807.2 28.4 %reduce-scatter.27.cloned.1.call-done = bf16[576,72]{0,1:T(8,128)(2,1)} async-done(((bf16[576,1152]{0,1:T(8,128)(2,1)}), bf16[576,72]{0,1:T(8,128)(2,1)}) %reduce-scatter.27.cloned.1.call-update) | async-done | bytes 82960
  837.2 35.9 %reduce-scatter.19.cloned.1.call-done = bf16[512,1152]{1,0:T(8,128)(2,1)} async-done(((bf16[1024,1152]{1,0:T(8,128)(2,1)}), bf16[512,1152]{1,0:T(8,128)(2,1)}) %reduce-scatter.19.cloned.1.call-update) | async-done | bytes 1179664 | tf_op jit(solution)/shard_map/reduce_scatter | solution.py:228
  881.6 28.4 %reduce-scatter.15.cloned.1.call-done = bf16[512,1152]{1,0:T(8,128)(2,1)} async-done(((bf16[1024,1152]{1,0:T(8,128)(2,1)}), bf16[512,1152]{1,0:T(8,128)(2,1)}) %reduce-scatter.15.cloned.1.call-update) | async-done | bytes 1179664 | tf_op jit(solution)/shard_map/reduce_scatter | solution.py:168
  910.0 5.1 fusion.45
  915.9 6.0 all-reduce.2
  922.0 58.4 %all-reduce.1 = (f32[2,576]{1,0:T(2,128)}, f32[1152]{0:T(1024)}, f32[2304]{0:T(1024)}, f32[1152]{0:T(1024)}) all-reduce(f32[2,576]{1,0:T(2,128)} %pad_maximum_fusion.5, bf16[1152]{0:T(1024)(128)(2,1)S(1)} %get-tuple-element.57, f32[2304]{0:T(1024)} %get-tuple-element.80, ...), channel_id=1, replica_groups=mesh['dp'=16,'tensor'=2] {'dp'}, use_global_device_ids=true, to_apply=%region_28.29 | all-reduce | flops 5760 | bytes 43776 | tf_op jit(solution)/shard_map/psum | solution.py:277
  980.3 23.0 %all-gather.1 = bf16[16,1,6912]{2,1,0:T(2,128)(2,1)S(1)} all-gather(bf16[1,1,6912]{2,1,0:T(2,128)(2,1)S(1)} %bitcast.239), channel_id=1, replica_groups=mesh['dp'=16,'tensor'=2] {'dp'}, dimensions={0}, use_global_device_ids=true | all-gather | bytes 235008 | tf_op jit(solution)/shard_map/all_gather | solution.py:253
  1006.4 10.3 %fusion.89 = f32[1,1152]{1,0:T(1,128)} fusion(bf16[1152,6912]{1,0:T(8,128)(2,1)} %all-gather.12.cloned.1.call-done, bf16[1,6912]{1,0:T(2,128)(2,1)S(1)} %get-tuple-element.56, bf16[1,1152]{1,0:T(2,128)(2,1)S(1)} %copy-done.48), kind=kOutput, calls=%fused_computation.145 | convolution fusion | flops 15936768 | bytes 15945984 | tf_op jit(solution)/shard_map/le,de->ld/dot_general | solution.py:249
  (260 shorter events, 81.7 us)
Async XLA Ops:
  7.2 127.1 %copy-start.46 = (bf16[1,1152]{1,0:T(2,128)(2,1)S(1)}, bf16[1,1152]{1,0:T(2,128)(2,1)}, u32[]{:S(2)}) copy-start(bf16[1,1152]{1,0:T(2,128)(2,1)} %param.14) | copy-start | bytes 6916
  7.2 127.1 %all-gather.12.cloned.1.call-start = ((), (), s32[]{:S(2)}) async-start(), calls=%async_computation.8 | async-start | bytes 16920576 | tf_op jit(solution)/shard_map/all_gather | solution.py:106
  7.9 178.5 %all-gather.16.cloned.1.call-start = ((), (), s32[]{:S(2)}) async-start(), calls=%async_computation.10 | async-start | bytes 4700160 | tf_op jit(solution)/shard_map/all_gather | solution.py:107
  8.7 214.0 %all-gather.14.cloned.1.call-start = ((), (), s32[]{:S(2)}) async-start(), calls=%async_computation.9 | async-start | bytes 3538944 | tf_op jit(solution)/shard_map/all_gather | solution.py:126
  10.2 132.5 %copy-start.38 = (f32[512]{0:T(512)}, f32[512]{0:T(512)S(1)}, u32[]{:S(2)}) copy-start(f32[512]{0:T(512)S(1)} %broadcast_multiply_fusion.1) | copy-start | bytes 6148
  10.7 123.6 %copy-start.53 = (f32[512]{0:T(512)}, f32[512]{0:T(512)S(1)}, u32[]{:S(2)}) copy-start(f32[512]{0:T(512)S(1)} %fusion.42) | copy-start | bytes 6148
  10.7 132.0 %copy-start.43 = (f32[512]{0:T(512)}, f32[512]{0:T(512)S(1)}, u32[]{:S(2)}) copy-start(f32[512]{0:T(512)S(1)} %fusion.96) | copy-start | bytes 6148
  10.7 131.3 %copy-start.58 = (bf16[6912]{0:T(1024)(128)(2,1)S(1)}, bf16[6912]{0:T(1024)(128)(2,1)}, u32[]{:S(2)}) copy-start(bf16[6912]{0:T(1024)(128)(2,1)} %param.16) | copy-start | bytes 41476
  142.7 50.2 %copy-start.31 = (f32[1152]{0:T(1024)}, f32[1152]{0:T(1024)S(1)}, u32[]{:S(2)}) copy-start(f32[1152]{0:T(1024)S(1)} %get-tuple-element.50) | copy-start | bytes 13828
  142.7 427.8 %copy-start.25 = (f32[1152]{0:T(1024)}, f32[1152]{0:T(1024)S(1)}, u32[]{:S(2)}) copy-start(f32[1152]{0:T(1024)S(1)} %get-tuple-element.51) | copy-start | bytes 13828
  144.3 127.9 %all-gather.18.cloned.1.call-start = ((), (), s32[]{:S(2)}) async-start(), calls=%async_computation.11 | async-start | bytes 1566720 | tf_op jit(solution)/shard_map/all_gather | solution.py:108
  144.8 167.5 %reduce-scatter.13.cloned.1.call-start = ((), (), s32[]{:S(2)}) async-start(), calls=%async_computation.12 | async-start | bytes 3538944 | tf_op jit(solution)/shard_map/reduce_scatter | solution.py:148
  230.4 36.4 %copy-start.7 = (bf16[1024,3,576]{0,2,1:T(8,128)(2,1)}, bf16[1024,3,576]{0,2,1:T(8,128)(2,1)S(1)}, u32[]{:S(2)}) copy-start(bf16[1024,3,576]{0,2,1:T(8,128)(2,1)S(1)} %add_convert_fusion) | copy-start | bytes 10616836
  238.5 16.1 %copy-start.32 = (f32[8,512]{1,0:T(8,128)}, f32[8,512]{1,0:T(8,128)S(1)}, u32[]{:S(2)}) copy-start(f32[8,512]{1,0:T(8,128)S(1)} %get-tuple-element.72) | copy-start | bytes 49156
  241.0 25.7 %copy-start = (f32[8,512,1024]{2,1,0:T(8,128)}, f32[8,512,1024]{2,1,0:T(8,128)S(1)}, u32[]{:S(2)}) copy-start(f32[8,512,1024]{2,1,0:T(8,128)S(1)} %get-tuple-element.75) | copy-start | bytes 50331652
  241.0 25.7 %copy-start.34 = (f32[8,512]{1,0:T(8,128)}, f32[8,512]{1,0:T(8,128)S(1)}, u32[]{:S(2)}) copy-start(f32[8,512]{1,0:T(8,128)S(1)} %get-tuple-element.74) | copy-start | bytes 49156
  277.4 94.0 %all-gather.22.cloned.1.call-start = ((), (), s32[]{:S(2)}) async-start(), calls=%async_computation.14 | async-start | bytes 5640192 | tf_op jit(solution)/shard_map/all_gather | solution.py:109
  277.9 129.9 %all-gather.20.cloned.1.call-start = ((), (), s32[]{:S(2)}) async-start(), calls=%async_computation.13 | async-start | bytes 3538944 | tf_op jit(solution)/shard_map/all_gather | solution.py:159
  278.0 291.2 %copy-start.27 = (f32[1152]{0:T(1024)}, f32[1152]{0:T(1024)S(1)}, u32[]{:S(2)}) copy-start(f32[1152]{0:T(1024)S(1)} %convert_element_type.196) | copy-start | bytes 13828
  317.4 149.7 %all-gather.24.cloned.1.call-start = ((), (), s32[]{:S(2)}) async-start(), calls=%async_computation.15 | async-start | bytes 5640192 | tf_op jit(solution)/shard_map/all_gather | solution.py:110
  318.1 185.4 %all-gather.26.cloned.1.call-start = ((), (), s32[]{:S(2)}) async-start(), calls=%async_computation.17 | async-start | bytes 3538944 | tf_op jit(solution)/shard_map/all_gather | solution.py:181
  320.1 245.9 %reduce-scatter.17.cloned.1.call-start = ((), (), s32[]{:S(2)}) async-start(), calls=%async_computation.18 | async-start | bytes 3538944 | tf_op jit(solution)/shard_map/reduce_scatter | solution.py:193
  531.1 77.8 %all-gather.28.cloned.1.call-start = ((), (), s32[]{:S(2)}) async-start(), calls=%async_computation.19 | async-start | bytes 3538944 | tf_op jit(solution)/shard_map/all_gather | solution.py:210
  572.7 230.7 %reduce-scatter.23.cloned.1.call-start = ((), (), s32[]{:S(2)}) async-start(), calls=%async_computation.22 | async-start | bytes 5640192 | tf_op jit(solution)/shard_map/reduce_scatter | solution.py:273
  584.3 220.9 %reduce-scatter.21.cloned.1.call-start = ((), (), s32[]{:S(2)}) async-start(), calls=%async_computation.21 | async-start | bytes 5640192 | tf_op jit(solution)/shard_map/reduce_scatter | solution.py:270
  595.7 13.2 %copy-start.66 = (bf16[576,1152]{0,1:T(8,128)(2,1)S(1)}, bf16[576,1152]{0,1:T(8,128)(2,1)}, u32[]{:S(2)}) copy-start(bf16[576,1152]{0,1:T(8,128)(2,1)} %all-gather.18.cloned.1.call-done) | copy-start | bytes 3981316
  595.7 239.9 %reduce-scatter.27.cloned.1.call-start = ((), (), s32[]{:S(2)}) async-start(), calls=%async_computation.24 | async-start | bytes 1566720
  613.2 15.6 %copy-start.17 = (bf16[512,576]{0,1:T(8,128)(2,1)}, bf16[512,576]{0,1:T(8,128)(2,1)S(1)}, u32[]{:S(2)}) copy-start(bf16[512,576]{0,1:T(8,128)(2,1)S(1)} %get-tuple-element.66) | copy-start | bytes 1769476
  613.2 15.6 %slice-start = ((s8[16777216]{0:T(1024)(128)(4,1)}), s8[4194304]{0:T(1024)(128)(4,1)S(1)}, s32[]{:S(2)}) async-start(s8[16777216]{0:T(1024)(128)(4,1)} %bitcast.212), calls=%async_computation.25 | async-start | bytes 8388608
  613.2 15.6 %slice-start.1 = ((s8[16777216]{0:T(1024)(128)(4,1)}), s8[4194304]{0:T(1024)(128)(4,1)S(1)}, s32[]{:S(2)}) async-start(s8[16777216]{0:T(1024)(128)(4,1)} %bitcast.212), calls=%async_computation.26 | async-start | bytes 8388608
  613.2 16.7 %slice-start.2 = ((s8[16777216]{0:T(1024)(128)(4,1)}), s8[4194304]{0:T(1024)(128)(4,1)S(1)}, s32[]{:S(2)}) async-start(s8[16777216]{0:T(1024)(128)(4,1)} %bitcast.212), calls=%async_computation.27 | async-start | bytes 8388608
  613.2 18.2 %slice-start.3 = ((s8[16777216]{0:T(1024)(128)(4,1)}), s8[4194304]{0:T(1024)(128)(4,1)S(1)}, s32[]{:S(2)}) async-start(s8[16777216]{0:T(1024)(128)(4,1)} %bitcast.212), calls=%async_computation.28 | async-start | bytes 8388608
  631.4 11.1 %copy-start.68 = (bf16[8,72,512]{2,1,0:T(8,128)(2,1)S(1)}, bf16[8,72,512]{2,1,0:T(8,128)(2,1)}, u32[]{:S(2)}) copy-start(bf16[8,72,512]{2,1,0:T(8,128)(2,1)} %copy-done.67) | copy-start | bytes 1769476
  631.4 11.1 %copy-start.70 = (bf16[8,72,512]{2,1,0:T(8,128)(2,1)S(1)}, bf16[8,72,512]{2,1,0:T(8,128)(2,1)}, u32[]{:S(2)}) copy-start(bf16[8,72,512]{2,1,0:T(8,128)(2,1)} %copy-done.69) | copy-start | bytes 1769476
  667.9 28.3 %slice-start.4 = ((s8[16777216]{0:T(1024)(128)(4,1)}), s8[4194304]{0:T(1024)(128)(4,1)S(1)}, s32[]{:S(2)}) async-start(s8[16777216]{0:T(1024)(128)(4,1)} %bitcast.214), calls=%async_computation.29 | async-start | bytes 8388608
  667.9 28.3 %slice-start.5 = ((s8[16777216]{0:T(1024)(128)(4,1)}), s8[4194304]{0:T(1024)(128)(4,1)S(1)}, s32[]{:S(2)}) async-start(s8[16777216]{0:T(1024)(128)(4,1)} %bitcast.214), calls=%async_computation.30 | async-start | bytes 8388608
  667.9 28.3 %slice-start.6 = ((s8[16777216]{0:T(1024)(128)(4,1)}), s8[4194304]{0:T(1024)(128)(4,1)S(1)}, s32[]{:S(2)}) async-start(s8[16777216]{0:T(1024)(128)(4,1)} %bitcast.214), calls=%async_computation.31 | async-start | bytes 8388608
  700.6 172.5 %reduce-scatter.19.cloned.1.call-start = ((), (), s32[]{:S(2)}) async-start(), calls=%async_computation.20 | async-start | bytes 3538944 | tf_op jit(solution)/shard_map/reduce_scatter | solution.py:228
  718.6 191.4 %reduce-scatter.15.cloned.1.call-start = ((), (), s32[]{:S(2)}) async-start(), calls=%async_computation.16 | async-start | bytes 3538944 | tf_op jit(solution)/shard_map/reduce_scatter | solution.py:168
  733.0 283.8 %reduce-scatter.25.cloned.1.call-start = ((), (), s32[]{:S(2)}) async-start(), calls=%async_computation.23 | async-start | bytes 4386816
  772.7 26.6 %copy-start.16 = (bf16[512,1152]{1,0:T(8,128)(2,1)S(1)}, bf16[512,1152]{1,0:T(8,128)(2,1)}, u32[]{:S(2)}) copy-start(bf16[512,1152]{1,0:T(8,128)(2,1)} %reduce-scatter.17.cloned.1.call-done) | copy-start | bytes 3538948
  772.8 27.4 %copy-start.57 = (bf16[1152]{0:T(1024)(128)(2,1)S(1)}, bf16[1152]{0:T(1024)(128)(2,1)}, u32[]{:S(2)}) copy-start(bf16[1152]{0:T(1024)(128)(2,1)} %get-tuple-element.40) | copy-start | bytes 6916
  772.8 28.0 %copy-start.13 = (bf16[8,72,1024]{2,1,0:T(8,128)(2,1)S(1)}, bf16[8,72,1024]{2,1,0:T(8,128)(2,1)}, u32[]{:S(2)}) copy-start(bf16[8,72,1024]{2,1,0:T(8,128)(2,1)} %fusion.67) | copy-start | bytes 3538948
  802.8 72.5 %copy-start.2 = (bf16[512,1,1152]{2,0,1:T(8,128)(2,1)S(1)}, bf16[512,1,1152]{2,0,1:T(8,128)(2,1)}, u32[]{:S(2)}) copy-start(bf16[512,1,1152]{2,0,1:T(8,128)(2,1)} %param.13) | copy-start | bytes 3538948
  875.2 34.8 %copy-start.6 = (bf16[512,1152]{1,0:T(8,128)(2,1)S(1)}, bf16[512,1152]{1,0:T(8,128)(2,1)}, u32[]{:S(2)}) copy-start(bf16[512,1152]{1,0:T(8,128)(2,1)} %reduce-scatter.13.cloned.1.call-done) | copy-start | bytes 3538948
  875.2 34.8 %copy-start.26 = (f32[1152]{0:T(1024)S(1)}, f32[1152]{0:T(1024)}, u32[]{:S(2)}) copy-start(f32[1152]{0:T(1024)} %copy-done.25) | copy-start | bytes 13828
  875.2 34.8 %copy-start.28 = (f32[1152]{0:T(1024)S(1)}, f32[1152]{0:T(1024)}, u32[]{:S(2)}) copy-start(f32[1152]{0:T(1024)} %copy-done.27) | copy-start | bytes 13828
  915.1 91.3 %copy-start.48 = (bf16[1,1152]{1,0:T(2,128)(2,1)S(1)}, bf16[1,1152]{1,0:T(2,128)(2,1)}, u32[]{:S(2)}) copy-start(bf16[1,1152]{1,0:T(2,128)(2,1)} %param.14) | copy-start | bytes 6916
  (49 other events, 159.0 us)
Sparse Core Ops, SparseCore 0:
  10.2 124.0 all-gather.11
  136.5 49.8 all-gather.15
  188.5 34.1 all-gather.13
  224.7 39.7 all-gather.17
  277.5 34.7 reduce-scatter.12
  314.5 56.7 all-gather.21
  373.6 34.2 all-gather.19
  410.2 56.7 all-gather.23
  469.2 34.2 all-gather.25
  531.2 34.6 reduce-scatter.16
  572.8 36.0 all-gather.27
  612.8 78.5 reduce-scatter.22
  695.4 78.7 reduce-scatter.20
  778.3 57.2 reduce-scatter.26
  837.7 35.3 reduce-scatter.18
  875.2 34.7 reduce-scatter.14
  913.8 71.2 reduce-scatter.24
where the time goes:
time: 1030 us
  waiting for transfers between devices  543 us (53%)
  matrix products  208 us (20%)
  blocking collectives  109 us (11%)
  other arithmetic  87.4 us (8%)
  local copies, waits for them, and re-layouts  62.2 us (6%)
  between operations  15 us (1%)
    all_gather x1, waiting for transfers between devices, on_device(): lax.all_gather(mod_weight, 'dp', axis=0, tiled=True)  124 us
    psum x1, blocking collectives, on_device(): lax.psum((qkv_bias_grad, proj_bias_grad, fc1_bias_grad, fc2_bias_grad), '...  58.4 us
    unnamed x164, local copies, waits for them, and re-layouts  50.9 us
    all_gather x1, waiting for transfers between devices, on_device(): lax.all_gather(first_hidden_weight, 'dp', axis=0, tiled=True)  49.9 us
    all_gather x1, waiting for transfers between devices, on_device(): lax.all_gather(second_hidden_weight, 'dp', axis=1, tiled=True)  47.6 us
    all_gather x1, waiting for transfers between devices, on_device(): lax.all_gather(query_key_value_weight, 'dp', axis=0, tiled=True)  41.1 us
    all_gather x1, waiting for transfers between devices, on_device(): lax.all_gather(grad_m_low, 'tensor', axis=0, tiled=True)  36.4 us
    all_gather x1, waiting for transfers between devices, on_device(): lax.all_gather(feedforward_normalized.astype(jnp.bfloat16), 'tensor', axi...  36.4 us
  transfers between devices with their start and end apart: 17, of which 13 were waited for; matrix products, arithmetic and copies ran while one was open for 29% of the time, Pallas kernels for 0%

commit v1 on v0

--- a/solution.py
+++ b/solution.py
@@ -1,9 +1,17 @@
+import functools
+
 import jax
 import jax.numpy as jnp
 from jax import lax
+from jax.experimental import pallas as pl
+from jax.experimental.pallas import tpu as pltpu
 from jax.sharding import PartitionSpec as P
 
 HEADS = 16
+MESH = pl.DeviceIdType.MESH
+AXES = ("dp", "tensor")
+F32 = jnp.float32
+BF16 = jnp.bfloat16
 
 
 def modulate(hidden, shifts, scales):
@@ -87,7 +95,7 @@
     )
 
 
-def on_device(
+def on_device_general(
     tokens,
     cond,
     mod_weight,
@@ -294,9 +302,826 @@
     )
 
 
+def place():
+    d = lax.axis_index("dp")
+    y = lax.axis_index("tensor")
+    return d, d // 4, (d // 2) % 2, d % 2, y
+
+
+def neighbours(pos):
+    d, z, x, c, y = pos
+    sib = (z * 4 + x * 2 + (1 - c), y)
+    xn = (z * 4 + (1 - x) * 2 + c, y)
+    yn = (d, 1 - y)
+    return sib, xn, yn
+
+
+def z_peer(pos, k):
+    d, z, x, c, y = pos
+    return (((z + k) % 4) * 4 + x * 2 + c, y)
+
+
+def greet(peers):
+    sem = pltpu.get_barrier_semaphore()
+    for peer in peers:
+        pl.semaphore_signal(sem, inc=1, device_id=peer, device_id_type=MESH)
+    pl.semaphore_wait(sem, len(peers))
+
+
+def chip_peers(pos):
+    return list(neighbours(pos)) + [z_peer(pos, k) for k in (1, 2, 3)]
+
+
+def remote(src, dst, send, recv, peer):
+    return pltpu.make_async_remote_copy(
+        src_ref=src, dst_ref=dst, send_sem=send, recv_sem=recv, device_id=peer, device_id_type=MESH
+    )
+
+
+GATHER_RECV = 17
+GATHER_SEND = 17
+
+
+class Gather:
+    def __init__(self, shard, full, cols, recv, send, pos):
+        self.shard, self.full, self.cols = shard, full, cols
+        self.recv, self.send, self.pos = recv, send, pos
+        self.sib, self.xn, self.yn = neighbours(pos)
+        self.home = pos[3] == pos[4]
+        self.away = pos[3] != pos[4]
+
+    def rows(self, b, n):
+        if self.cols is None:
+            return self.full.at[pl.ds(b, n)]
+        return self.full.at[pl.ds(b, n), :, pl.ds(*self.cols)]
+
+    def own(self):
+        if self.cols is None:
+            return self.shard
+        return self.shard.at[:, :, pl.ds(*self.cols)]
+
+    def copy(self, b, n, peer, s, r):
+        ref = self.rows(b, n)
+        return remote(ref, ref, self.send.at[s], self.recv.at[r], peer)
+
+    def stay(self):
+        return pltpu.make_async_copy(self.own(), self.rows(self.pos[0], 1), self.send.at[16])
+
+    def join(self):
+        d = self.pos[0]
+
+        @pl.when(self.away)
+        def _():
+            remote(
+                self.own(), self.rows(d, 1), self.send.at[15], self.recv.at[16], self.sib
+            ).start()
+
+        @pl.when(self.home)
+        def _():
+            self.stay().start()
+
+    def spread(self):
+        d, z, x, c, y = self.pos
+        q = z * 2 + x
+
+        @pl.when(self.home)
+        def _():
+            self.stay().wait()
+            self.copy(2 * q + 1 - c, 1, self.sib, 15, 16).wait_recv()
+            for k in (2, 1, 3):
+                self.copy(2 * q, 2, z_peer(self.pos, k), k - 1, q).start()
+            self.copy(2 * q, 2, self.xn, 3, q).start()
+            self.copy(2 * q, 2, self.yn, 4, q).start()
+
+    def from_z(self, k):
+        d, z, x, c, y = self.pos
+        q = ((z + k) % 4) * 2 + x
+
+        @pl.when(self.home)
+        def _():
+            self.copy(2 * q, 2, self.xn, 0, q).wait_recv()
+            self.copy(2 * q, 2, self.xn, 3 + 2 * k, q).start()
+            self.copy(2 * q, 2, self.yn, 4 + 2 * k, q).start()
+
+    def cross(self, k):
+        d, z, x, c, y = self.pos
+        zz = (z + k) % 4
+
+        @pl.when(self.home)
+        def _():
+            q = zz * 2 + 1 - x
+            self.copy(2 * q, 2, self.xn, 0, q).wait_recv()
+            self.copy(2 * q, 1, self.yn, 11 + k, 8 + zz).start()
+
+        @pl.when(self.away)
+        def _():
+            q = zz * 2 + x
+            self.copy(2 * q, 2, self.xn, 0, q).wait_recv()
+            self.copy(2 * q + 1, 1, self.xn, 11 + k, 12 + zz).start()
+
+    def finish(self):
+        d, z, x, c, y = self.pos
+
+        @pl.when(self.home)
+        def _():
+            for i in range(11):
+                self.copy(0, 2, self.xn, i, 0).wait_send()
+            for k in range(4):
+                self.copy(0, 1, self.yn, 11 + k, 8).wait_send()
+
+        @pl.when(self.away)
+        def _():
+            for k in range(4):
+                zz = (z + k) % 4
+                q = zz * 2 + 1 - x
+                self.copy(2 * q, 1, self.yn, 0, 8 + zz).wait_recv()
+                self.copy(2 * q + 1, 1, self.xn, 0, 12 + zz).wait_recv()
+            self.copy(0, 1, self.sib, 15, 16).wait_send()
+            for k in range(4):
+                self.copy(0, 1, self.xn, 11 + k, 12).wait_send()
+
+
+def gather_events(parts):
+    events = [p.join for p in parts] + [p.spread for p in parts]
+    for p in parts:
+        events += [functools.partial(p.from_z, k) for k in (1, 2, 3)]
+    for p in parts:
+        events += [functools.partial(p.cross, k) for k in range(4)]
+    return events + [p.finish for p in parts]
+
+
+def gather_parts(shards, fulls, chunks, recv, send, pos):
+    return [
+        Gather(shards[g], fulls[g], cols, recv.at[i], send.at[i], pos)
+        for i, (g, cols) in enumerate(chunks)
+    ]
+
+
+def gather_kernel(chunks, count, *refs):
+    shards, fulls = refs[:count], refs[count : 2 * count]
+    recv, send = refs[2 * count :]
+    pos = place()
+    greet(chip_peers(pos))
+    for event in gather_events(gather_parts(shards, fulls, chunks, recv, send, pos)):
+        event()
+
+
+def gather_sems(chunks):
+    n = len(chunks)
+    return [
+        pltpu.SemaphoreType.DMA((n, GATHER_RECV)),
+        pltpu.SemaphoreType.DMA((n, GATHER_SEND)),
+    ]
+
+
+def gather_weights(shards, chunks, collective_id):
+    count = len(shards)
+    anywhere = pl.BlockSpec(memory_space=pl.ANY)
+    return pl.pallas_call(
+        functools.partial(gather_kernel, chunks, count),
+        out_shape=[jax.ShapeDtypeStruct((16,) + s.shape[1:], s.dtype) for s in shards],
+        in_specs=[anywhere] * count,
+        out_specs=[anywhere] * count,
+        scratch_shapes=gather_sems(chunks),
+        compiler_params=pltpu.CompilerParams(
+            collective_id=collective_id, has_side_effects=True
+        ),
+    )(*shards)
+
+
+REDUCE_RECV = 24
+REDUCE_SEND = 17
+
+
+class Reduce:
+    def __init__(self, grad, land, spare, out, recv, send, pos, cols):
+        self.grad, self.land, self.spare, self.out = grad, land, spare, out
+        self.recv, self.send, self.pos, self.cols = recv, send, pos, pl.ds(*cols)
+        self.sib, self.xn, self.yn = neighbours(pos)
+        self.home = pos[3] == pos[4]
+        self.away = pos[3] != pos[4]
+
+    def rows(self, b, n=1):
+        return self.grad.at[pl.ds(b, n), :, self.cols]
+
+    def copy(self, src, slot, n, r, s, peer):
+        return remote(src, self.land.at[pl.ds(slot, n)], self.send.at[s], self.recv.at[r], peer)
+
+    def arrive(self, slot, n, r):
+        self.copy(self.land.at[pl.ds(slot, n)], slot, n, r, 0, self.xn).wait_recv()
+
+    def add(self, b, *slots):
+        total = self.grad[b, :, self.cols].astype(F32)
+        for slot in slots:
+            total = total + self.land[slot].astype(F32)
+        self.grad[b, :, self.cols] = total.astype(BF16)
+
+    def first(self):
+        d, z, x, c, y = self.pos
+
+        def over_y(column, sem):
+            def step(k, _):
+                zz = lax.rem(z + 1 + k, 4)
+                q = zz * 2 + column
+                self.copy(self.rows(2 * q), q, 1, q, sem + k, self.yn).start()
+                return 0
+
+            lax.fori_loop(0, 4, step, 0)
+
+        def over_x(k, _):
+            zz = lax.rem(z + 1 + k, 4)
+            b = zz * 4 + (1 - x) * 2 + 1
+            self.copy(self.rows(b), 8 + zz, 1, 8 + zz, 8 + k, self.xn).start()
+            return 0
+
+        @pl.when(self.away)
+        def _():
+            over_y(1 - x, 0)
+
+        lax.fori_loop(0, 4, over_x, 0)
+
+        @pl.when(self.away)
+        def _():
+            over_y(x, 4)
+
+    def second(self):
+        d, z, x, c, y = self.pos
+
+        @pl.when(self.home)
+        def _():
+            def step(k, _):
+                zz = lax.rem(z + 1 + k, 4)
+                q = zz * 2 + 1 - x
+                self.arrive(q, 1, q)
+                self.add(2 * q, q)
+                self.copy(self.rows(2 * q), 12 + zz, 1, 12 + zz, k, self.xn).start()
+                return 0
+
+            lax.fori_loop(0, 4, step, 0)
+
+        def step(k, _):
+            zz = lax.rem(z + 1 + k, 4)
+            q = zz * 2 + x
+            self.arrive(8 + zz, 1, 8 + zz)
+            self.add(2 * q + 1, 8 + zz)
+
+            @pl.when(self.away)
+            def _():
+                self.copy(self.rows(2 * q + 1), 16 + zz, 1, 16 + zz, 12 + k, self.yn).start()
+
+            return 0
+
+        lax.fori_loop(0, 4, step, 0)
+
+    def third(self):
+        d, z, x, c, y = self.pos
+
+        @pl.when(self.home)
+        def _():
+            def step(k, _):
+                zz = lax.rem(z + 1 + k, 4)
+                q = zz * 2 + x
+                self.arrive(q, 1, q)
+                self.arrive(12 + zz, 1, 12 + zz)
+                self.add(2 * q, q, 12 + zz)
+                self.arrive(16 + zz, 1, 16 + zz)
+                self.add(2 * q + 1, 16 + zz)
+                peer = (zz * 4 + x * 2 + c, y)
+                self.copy(self.rows(2 * q, 2), 20 + 2 * k, 2, 20 + k, 4 + k, peer).start()
+                return 0
+
+            lax.fori_loop(0, 3, step, 0)
+
+    def hand_over(self):
+        return remote(
+            self.spare, self.out.at[:, self.cols], self.send.at[16], self.recv.at[23], self.sib
+        )
+
+    def fourth(self):
+        d, z, x, c, y = self.pos
+
+        @pl.when(self.home)
+        def _():
+            q = z * 2 + x
+            self.arrive(q, 1, q)
+            self.arrive(12 + z, 1, 12 + z)
+            self.arrive(16 + z, 1, 16 + z)
+            for k in range(3):
+                self.arrive(20 + 2 * k, 2, 20 + k)
+            low = self.grad[2 * q, :, self.cols].astype(F32)
+            for slot in (q, 12 + z, 20, 22, 24):
+                low = low + self.land[slot].astype(F32)
+            high = self.grad[2 * q + 1, :, self.cols].astype(F32)
+            for slot in (16 + z, 21, 23, 25):
+                high = high + self.land[slot].astype(F32)
+
+            @pl.when(c == 0)
+            def _():
+                self.out[:, self.cols] = low
+                self.spare[...] = high
+
+            @pl.when(c == 1)
+            def _():
+                self.out[:, self.cols] = high
+                self.spare[...] = low
+
+            self.hand_over().start()
+
+    def finish(self):
+        one, two = self.rows(0), self.rows(0, 2)
+
+        @pl.when(self.home)
+        def _():
+            for k in range(4):
+                self.copy(one, 0, 1, 0, k, self.xn).wait_send()
+            for k in range(3):
+                self.copy(two, 0, 2, 0, 4 + k, self.xn).wait_send()
+            self.hand_over().wait_send()
+
+        @pl.when(self.away)
+        def _():
+            for k in range(8):
+                self.copy(one, 0, 1, 0, k, self.yn).wait_send()
+            for k in range(4):
+                self.copy(one, 0, 1, 0, 12 + k, self.yn).wait_send()
+            self.hand_over().wait_recv()
+
+        for k in range(4):
+            self.copy(one, 0, 1, 0, 8 + k, self.xn).wait_send()
+
+
+def reduce_events(parts):
+    n = len(parts)
+    events = [parts[0].first]
+    for i in range(n + 2):
+        if i + 1 < n:
+            events.append(parts[i + 1].first)
+        if i < n:
+            events.append(parts[i].second)
+        if 0 <= i - 1 < n:
+            events.append(parts[i - 1].third)
+        if 0 <= i - 2 < n:
+            events.append(parts[i - 2].fourth)
+    return events + [p.finish for p in parts]
+
+
+def reduce_kernel(chunks, count, *refs):
+    n = len(chunks)
+    grads, outs = refs[:count], refs[count : 2 * count]
+    lands, spares = refs[2 * count : 2 * count + n], refs[2 * count + n : 2 * count + 2 * n]
+    recv, send = refs[2 * count + 2 * n :]
+    pos = place()
+    greet(chip_peers(pos))
+    parts = [
+        Reduce(grads[g], lands[i], spares[i], outs[g], recv.at[i], send.at[i], pos, cols)
+        for i, (g, cols) in enumerate(chunks)
+    ]
+    for event in reduce_events(parts):
+        event()
+
+
+def reduce_scratch(chunks):
+    n = len(chunks)
+    return (
+        [pltpu.VMEM((26, 72, cols[1]), BF16) for _, cols in chunks]
+        + [pltpu.VMEM((72, cols[1]), F32) for _, cols in chunks]
+        + [pltpu.SemaphoreType.DMA((n, REDUCE_RECV)), pltpu.SemaphoreType.DMA((n, REDUCE_SEND))]
+    )
+
+
+def reduce_grads(grads, chunks, collective_id):
+    count = len(grads)
+    vmem = pl.BlockSpec(memory_space=pltpu.VMEM)
+    return pl.pallas_call(
+        functools.partial(reduce_kernel, chunks, count),
+        out_shape=[jax.ShapeDtypeStruct(g.shape[1:], F32) for g in grads],
+        in_specs=[vmem] * count,
+        out_specs=[vmem] * count,
+        scratch_shapes=reduce_scratch(chunks),
+        compiler_params=pltpu.CompilerParams(
+            collective_id=collective_id, has_side_effects=True, vmem_limit_bytes=63000 * 1024
+        ),
+    )(*grads)
+
+
+def mod_forward_kernel(
+    piece_ref, w_ref, bias_ref, mod_ref, silu_ref, part, land, mine, other, s1, r1, s2, r2, s3
+):
+    pos = place()
+    d, z, x, c, y = pos
+    sib = neighbours(pos)[0]
+    greet([((d + k) % 16, y) for k in range(1, 16)])
+
+    def piece(k):
+        to = (d + k) % 16
+        return remote(piece_ref.at[to], silu_ref.at[d], s1.at[k], r1.at[d], (to, y))
+
+    def piece_in(k):
+        src = (d + k) % 16
+        return remote(piece_ref.at[src], silu_ref.at[src], s1.at[k], r1.at[src], (src, y))
+
+    for k in range(1, 16):
+        piece(k).start()
+    silu_ref[d] = piece_ref[d]
+    for k in range(1, 16):
+        piece_in(k).wait_recv()
+    rows = jnp.concatenate(
+        [silu_ref[2 * q + y].astype(F32)[0:1, :] for q in range(8)], axis=0
+    ).astype(BF16)[:, :72]
+    width = w_ref.shape[1] // 6
+    for j in range(6):
+        cols = slice(j * width, (j + 1) * width)
+        value = jnp.dot(rows, w_ref[:, cols], preferred_element_type=F32)
+        for q in range(8):
+            part[q, :, cols] = value[q : q + 1, :]
+    me = z * 2 + x
+
+    def send_part(k):
+        q = (me + k) % 8
+        return remote(part.at[q], land.at[me], s2.at[k], r2.at[me], (q * 2 + c, y))
+
+    def part_in(k):
+        q = (me + k) % 8
+        return remote(part.at[q], land.at[q], s2.at[k], r2.at[q], (q * 2 + c, y))
+
+    for k in range(1, 8):
+        send_part(k).start()
+    land[me] = part[me]
+    for k in range(1, 8):
+        part_in(k).wait_recv()
+    total = land[0]
+    for q in range(1, 8):
+        total = total + land[q]
+    mine[...] = total
+    swap = remote(mine, other, s3.at[0], s3.at[1], sib)
+    swap.start()
+    for k in range(1, 16):
+        piece(k).wait_send()
+    for k in range(1, 8):
+        send_part(k).wait_send()
+    swap.wait()
+    mod_ref[...] = mine[...] + other[...] + bias_ref[...]
+
+
+def mod_forward(pieces, w_mod, bias, collective_id):
+    vmem = pl.BlockSpec(memory_space=pltpu.VMEM)
+    n = w_mod.shape[1]
+    return pl.pallas_call(
+        mod_forward_kernel,
+        out_shape=[jax.ShapeDtypeStruct((1, n), F32), jax.ShapeDtypeStruct((16, 8, 128), BF16)],
+        in_specs=[vmem] * 3,
+        out_specs=[vmem] * 2,
+        scratch_shapes=[
+            pltpu.VMEM((8, 1, n), F32),
+            pltpu.VMEM((8, 1, n), F32),
+            pltpu.VMEM((1, n), F32),
+            pltpu.VMEM((1, n), F32),
+            pltpu.SemaphoreType.DMA((16,)),
+            pltpu.SemaphoreType.DMA((16,)),
+            pltpu.SemaphoreType.DMA((8,)),
+            pltpu.SemaphoreType.DMA((8,)),
+            pltpu.SemaphoreType.DMA((2,)),
+        ],
+        compiler_params=pltpu.CompilerParams(
+            collective_id=collective_id, has_side_effects=True, vmem_limit_bytes=40 * 2**20
+        ),
+    )(pieces, w_mod, bias)
+
+
+def mod_backward_kernel(
+    v1_ref, v2_ref, v3_ref, silu_ref, w_ref,
+    mwg_ref, mbg_ref, sg_ref, v2_out, v3_out,
+    v1_in, v2_in, mods, b2, b3, sgp, s0, s1, r1, s2, r2, s3, r3, s4, r4,
+):
+    pos = place()
+    d, z, x, c, y = pos
+    sib = neighbours(pos)[0]
+    lin = d * 2 + y
+    greet([(((lin + k) % 32) // 2, (lin + k) % 2) for k in range(1, 32)])
+    me = (z * 2 + x) * 2 + y
+    a = remote(v1_ref, v1_in, s0.at[0], s0.at[1], sib)
+    b = remote(v2_ref, v2_in, s0.at[2], s0.at[3], sib)
+    a.start()
+    b.start()
+
+    @pl.when(y == c)
+    def _():
+        b3[me] = v3_ref[...]
+
+    sgp[...] = jnp.zeros_like(sgp)
+
+    def send3(q, core):
+        s = q * 2 + core
+        return remote(v3_ref, b3.at[me], s3.at[s], r3.at[me], (s, c))
+
+    for q in range(8):
+        for core in range(2):
+
+            @pl.when(jnp.logical_or(d != q * 2 + core, y != c))
+            def _():
+                send3(q, core).start()
+
+    a.wait()
+    b.wait()
+    mods[me] = (v1_ref[...] + v1_in[...]).astype(BF16)
+    b2[me] = v2_ref[...] + v2_in[...]
+
+    def chip(k):
+        m = (me + k) % 16
+        return m, ((m // 2) * 2 + c, m % 2)
+
+    for k in range(1, 16):
+        m, peer = chip(k)
+        remote(mods.at[me], mods.at[me], s1.at[k], r1.at[me], peer).start()
+        remote(b2.at[me], b2.at[me], s2.at[k], r2.at[me], peer).start()
+    for k in range(1, 16):
+        m, peer = chip(k)
+        remote(mods.at[m], mods.at[m], s1.at[k], r1.at[m], peer).wait_recv()
+    every = jnp.concatenate([mods[i].astype(F32) for i in range(16)], axis=0)
+    mbg_ref[...] = jnp.sum(every, axis=0, keepdims=True)
+    every = every.astype(BF16)
+    grad = lax.dot_general(
+        every, w_ref[...], (((1,), (1,)), ((), ())), preferred_element_type=F32
+    )
+    for i in range(16):
+        sgp[i, 0:1, :72] = grad[i : i + 1, :]
+
+    def send4(k):
+        m = (d + k) % 16
+        return remote(sgp.at[m], sg_ref.at[d], s4.at[k], r4.at[d], (m, y))
+
+    for k in range(1, 16):
+        send4(k).start()
+    sg_ref[d] = sgp[d]
+    owned = jnp.concatenate([silu_ref[i].astype(F32)[0:1, :] for i in range(16)], axis=0)
+    owned = owned.astype(BF16)[:, :72]
+    width = w_ref.shape[1] // 6
+    for j in range(6):
+        cols = slice(j * width, (j + 1) * width)
+        mwg_ref[:, cols] = lax.dot_general(
+            owned, every[:, cols], (((0,), (0,)), ((), ())), preferred_element_type=F32
+        )
+    for k in range(1, 16):
+        m, peer = chip(k)
+        remote(b2.at[m], b2.at[m], s2.at[k], r2.at[m], peer).wait_recv()
+    total = b2[0]
+    for i in range(1, 16):
+        total = total + b2[i]
+    v2_out[...] = total
+
+    def arrive3(i, guard):
+        @pl.when(guard)
+        def _():
+            remote(v3_ref, b3.at[i], s3.at[0], r3.at[i], sib).wait_recv()
+
+    for i in range(16):
+        arrive3(i, jnp.logical_or(i != me, y != c))
+    total = b3[0]
+    for i in range(1, 16):
+        total = total + b3[i]
+    v3_out[...] = total
+    for k in range(1, 16):
+        m = (d + k) % 16
+        remote(sgp.at[m], sg_ref.at[m], s4.at[k], r4.at[m], (m, y)).wait_recv()
+    for q in range(8):
+        for core in range(2):
+
+            @pl.when(jnp.logical_or(d != q * 2 + core, y != c))
+            def _():
+                send3(q, core).wait_send()
+
+    for k in range(1, 16):
+        m, peer = chip(k)
+        remote(mods.at[me], mods.at[me], s1.at[k], r1.at[me], peer).wait_send()
+        remote(b2.at[me], b2.at[me], s2.at[k], r2.at[me], peer).wait_send()
+        send4(k).wait_send()
+
+
+def mod_backward(v1, v2, v3, silu, w_mod, collective_id):
+    vmem = pl.BlockSpec(memory_space=pltpu.VMEM)
+    n = w_mod.shape[1]
+    n2, n3 = v2.shape[1], v3.shape[1]
+    dma = pltpu.SemaphoreType.DMA((16,))
+    return pl.pallas_call(
+        mod_backward_kernel,
+        out_shape=[
+            jax.ShapeDtypeStruct((72, n), F32),
+            jax.ShapeDtypeStruct((1, n), F32),
+            jax.ShapeDtypeStruct((16, 8, 128), F32),
+            jax.ShapeDtypeStruct((1, n2), F32),
+            jax.ShapeDtypeStruct((1, n3), F32),
+        ],
+        in_specs=[vmem] * 5,
+        out_specs=[vmem] * 5,
+        scratch_shapes=[
+            pltpu.VMEM((1, n), F32),
+            pltpu.VMEM((1, n2), F32),
+            pltpu.VMEM((16, 1, n), BF16),
+            pltpu.VMEM((16, 1, n2), F32),
+            pltpu.VMEM((16, 1, n3), F32),
+            pltpu.VMEM((16, 8, 128), F32),
+            pltpu.SemaphoreType.DMA((4,)),
+        ]
+        + [dma] * 8,
+        compiler_params=pltpu.CompilerParams(
+            collective_id=collective_id, has_side_effects=True, vmem_limit_bytes=40 * 2**20
+        ),
+    )(v1, v2, v3, silu, w_mod)
+
+
+def index_of(z, x, c, y):
+    return ((z * 2 + x) * 2 + c) * 2 + y
+
+
+def core_pairs():
+    return [
+        (index_of(z, x, c, y), index_of(z, x, 1 - c, y))
+        for z in range(4)
+        for x in range(2)
+        for c in range(2)
+        for y in range(2)
+    ]
+
+
+def latent_pairs():
+    return [
+        (index_of(z, x, c, y), index_of(z, x, y, c))
+        for z in range(4)
+        for x in range(2)
+        for c in range(2)
+        for y in range(2)
+        if c != y
+    ]
+
+
+def trade(value):
+    moved = lax.ppermute(value, AXES, latent_pairs())
+    home = lax.axis_index("dp") % 2 == lax.axis_index("tensor")
+    return jnp.where(home, value, moved)
+
+
+def both_halves(value):
+    return jnp.concatenate([value, lax.ppermute(value, AXES, core_pairs())], axis=0)
+
+
+def own_sum(partial):
+    n = partial.shape[0] // 2
+    moved = lax.ppermute(partial[n:].astype(BF16), AXES, core_pairs())
+    return partial[:n] + moved.astype(F32)
+
+
+def columns(n, step):
+    return [(i, min(step, n - i)) for i in range(0, n, step)]
+
+
+def on_device_chip(
+    tokens,
+    cond,
+    mod_weight,
+    mod_bias,
+    query_key_value_weight,
+    qkv_bias,
+    attention_out_weight,
+    attention_out_bias,
+    first_hidden_weight,
+    first_hidden_bias,
+    second_hidden_weight,
+    second_hidden_bias,
+    out_grad,
+):
+    half, _, width = tokens.shape
+    owned, _, cols = query_key_value_weight.shape
+    head_size = width // HEADS
+    heads_here = cols // head_size
+    hidden = first_hidden_weight.shape[1]
+
+    silu_cond, silu_back = jax.vjp(jax.nn.silu, cond.astype(F32))
+    pieces = jnp.pad(
+        silu_cond.astype(BF16).reshape(16, 1, owned), ((0, 0), (0, 7), (0, 128 - owned))
+    )
+    modulation, silu_owned = mod_forward(pieces, mod_weight, mod_bias.astype(F32)[None], 1)
+    shift_a, scale_a, gate_a, shift_m, scale_m, gate_m = [
+        modulation[:, i * width : (i + 1) * width] for i in range(6)
+    ]
+
+    bias_rows = jnp.concatenate([qkv_bias.reshape(-1), first_hidden_bias]).reshape(-1, width)
+    carried = trade(jnp.concatenate([tokens.reshape(half, width), bias_rows], axis=0))
+    tokens_here = carried[:half].astype(F32)
+    biases = carried[half:].reshape(-1)
+    q_bias, v_bias, fc1_bias = biases[:cols], biases[cols : 2 * cols], biases[2 * cols :]
+    grad_out = trade(out_grad.reshape(half, width)).astype(F32)
+
+    s_qkv = query_key_value_weight.reshape(1, owned, 3 * cols)
+    s_proj = attention_out_weight.T.reshape(1, owned, cols)
+    s_fc1 = first_hidden_weight.reshape(1, owned, hidden)
+    s_fc2 = second_hidden_weight.T.reshape(1, owned, hidden)
+    (w_qkv,) = gather_weights([s_qkv], [(0, (0, 896)), (0, (896, 832))], 2)
+    w_qkv = w_qkv.reshape(width, 3 * cols)
+    chunks = [(0, None)] + [(g, p) for g in (1, 2) for p in columns(hidden, 1152)]
+    w_proj, w_fc1, w_fc2 = gather_weights([s_proj, s_fc1, s_fc2], chunks, 3)
+    w_proj, w_fc1, w_fc2 = (w.reshape(width, -1) for w in (w_proj, w_fc1, w_fc2))
+
+    normed_a, norm_a_back = jax.vjp(modulate, tokens_here, shift_a, scale_a)
+    rows_a = both_halves(normed_a.astype(BF16))
+    qkv_shift = jnp.concatenate([q_bias, jnp.zeros_like(q_bias), v_bias]).astype(F32)
+    qkv = (jnp.dot(rows_a, w_qkv, preferred_element_type=F32) + qkv_shift).astype(BF16)
+    packed = qkv.reshape(2 * half, 3, heads_here, head_size)
+    attended, log_totals = attend_forward(packed)
+    branch_a = own_sum(
+        jnp.einsum("rc,dc->rd", attended, w_proj, preferred_element_type=F32)
+    ) + attention_out_bias.astype(F32)
+    resid_mid = tokens_here + gate_a * branch_a
+
+    normed_m, norm_m_back = jax.vjp(modulate, resid_mid, shift_m, scale_m)
+    rows_m = both_halves(normed_m.astype(BF16))
+    preact = jnp.dot(rows_m, w_fc1, preferred_element_type=F32) + fc1_bias.astype(F32)
+    activated, gelu_back = jax.vjp(gelu_tanh, preact)
+    act_low = activated.astype(BF16)
+    branch_m = own_sum(
+        jnp.einsum("rf,df->rd", act_low, w_fc2, preferred_element_type=F32)
+    ) + second_hidden_bias.astype(F32)
+    output = (resid_mid + gate_m * branch_m).astype(BF16)
+
+    gate_m_grad = jnp.sum(grad_out * branch_m, axis=0)
+    grad_m_own = (grad_out * gate_m).astype(BF16)
+    fc2_bias_part = jnp.sum(grad_m_own, axis=0, dtype=F32)
+    grad_m = both_halves(grad_m_own)
+    fc2_grad = jnp.einsum("rd,rf->df", grad_m, act_low, preferred_element_type=F32).astype(BF16)
+    act_grad = jnp.dot(grad_m, w_fc2, preferred_element_type=F32)
+    pre_grad = gelu_back(act_grad)[0].astype(BF16)
+    fc1_bias_part = jnp.sum(pre_grad, axis=0, dtype=F32)
+    fc1_grad = jnp.einsum("rd,rf->df", rows_m, pre_grad, preferred_element_type=F32).astype(BF16)
+    normed_m_grad = own_sum(
+        jnp.einsum("rf,df->rd", pre_grad, w_fc1, preferred_element_type=F32)
+    )
+    resid_part, shift_m_grad, scale_m_grad = norm_m_back(normed_m_grad)
+    resid_grad = grad_out + resid_part
+
+    gate_a_grad = jnp.sum(resid_grad * branch_a, axis=0)
+    grad_a_own = (resid_grad * gate_a).astype(BF16)
+    proj_bias_part = jnp.sum(grad_a_own, axis=0, dtype=F32)
+    grad_a = both_halves(grad_a_own)
+    proj_grad = jnp.einsum("rd,rc->dc", grad_a, attended, preferred_element_type=F32).astype(BF16)
+    attended_grad = jnp.dot(grad_a, w_proj, preferred_element_type=F32).astype(BF16)
+    qkv_grad = attend_backward(
+        (packed, attended_grad.reshape(2 * half, heads_here, head_size), log_totals)
+    ).reshape(2 * half, 3 * cols)
+    qkv_bias_part = jnp.sum(qkv_grad, axis=0, dtype=F32)
+    qkv_bias_part = jnp.concatenate([qkv_bias_part[:cols], qkv_bias_part[2 * cols :]])
+    qkv_wgrad = jnp.einsum("rd,rc->dc", rows_a, qkv_grad, preferred_element_type=F32).astype(BF16)
+    normed_a_grad = own_sum(
+        jnp.einsum("rc,dc->rd", qkv_grad, w_qkv, preferred_element_type=F32)
+    )
+    input_part, shift_a_grad, scale_a_grad = norm_a_back(normed_a_grad)
+    tokens_grad = (resid_grad + input_part).astype(BF16)
+
+    chunks = [(g, p) for g in (0, 1) for p in columns(hidden, 768)] + [(2, (0, cols))]
+    fc2_out, fc1_out, proj_out = reduce_grads(
+        [g.reshape(16, owned, -1) for g in (fc2_grad, fc1_grad, proj_grad)], chunks, 4
+    )
+    (qkv_out,) = reduce_grads(
+        [qkv_wgrad.reshape(16, owned, -1)], [(0, (0, 640)), (0, (640, 640)), (0, (1280, 448))], 5
+    )
+
+    mod_part = jnp.concatenate(
+        [
+            shift_a_grad.reshape(1, -1),
+            scale_a_grad.reshape(1, -1),
+            gate_a_grad.reshape(1, -1),
+            shift_m_grad.reshape(1, -1),
+            scale_m_grad.reshape(1, -1),
+            gate_m_grad.reshape(1, -1),
+        ],
+        axis=1,
+    )
+    wide_part = jnp.concatenate([fc2_bias_part, proj_bias_part])[None]
+    half_part = jnp.concatenate([fc1_bias_part, qkv_bias_part])[None]
+    mod_weight_grad, mod_bias_grad, silu_grad, wide, narrow = mod_backward(
+        mod_part, wide_part, half_part, silu_owned, mod_weight, 6
+    )
+    cond_grad = silu_back(silu_grad[:, 0, :owned].reshape(1, width))[0]
+    return (
+        trade(output).reshape(half, 1, width),
+        trade(tokens_grad).reshape(half, 1, width),
+        cond_grad,
+        mod_weight_grad,
+        mod_bias_grad[0],
+        qkv_out.reshape(owned, 3, cols),
+        narrow[0, hidden:].reshape(2, cols),
+        proj_out.T,
+        wide[0, width:],
+        fc1_out,
+        narrow[0, :hidden],
+        fc2_out.T,
+        wide[0, :width],
+    )
+
+
 def solution(mesh):
+    shape = dict(mesh.shape)
+    body = on_device_chip if shape == {"dp": 16, "tensor": 2} else on_device_general
     return jax.shard_map(
-        on_device,
+        body,
         mesh=mesh,
         in_specs=(
             P("tensor", "dp", None),

time: 1030 us -> 719 us (0.70)
  waiting for transfers between devices: 543 us -> 11 us
  Pallas kernels: 0 us -> 406 us
  blocking collectives: 109 us -> 0 us
  local copies, waits for them, and re-layouts: 62.2 us -> 31.5 us
  matrix products: 208 us -> 179 us
  other arithmetic: 87.4 us -> 66.7 us
  starting transfers between devices: 1.19 us -> 17.2 us
  between operations: 15 us -> 2.15 us
    pallas_call x0 -> x6, Pallas kernels: none -> 406 us  [the longest x2 182 us: reduce_grads(): pl.pallas_call(functools.partial(reduce_kernel, chunks, count), out_shape...]
    all_gather x9 -> x0, waiting for transfers between devices: 378 us -> none  [the longest x1 124 us: on_device(): lax.all_gather(mod_weight, 'dp', axis=0, tiled=True)]
    reduce_scatter x6 -> x0, waiting for transfers between devices: 133 us -> none  [the longest x1 35.9 us: on_device(): lax.psum_scatter(jnp.einsum('rc,dc->rd', qkv_grad_rows, qkv_flat, preferr...]
    psum x2 -> x0, blocking collectives: 64.4 us -> none  [the longest x1 58.4 us: on_device(): lax.psum((qkv_bias_grad, proj_bias_grad, fc1_bias_grad, fc2_bias_grad), '...]
    all_gather x2 -> x0, blocking collectives: 44.9 us -> none  [the longest x1 23 us: on_device(): lax.all_gather(mod_grad_low, 'dp', axis=0, tiled=True)]
    unnamed x164 -> x151, local copies, waits for them, and re-layouts: 50.9 us -> 13.3 us
    unnamed x19 -> x0, waiting for transfers between devices: 31.7 us -> none
    dot_general x15 -> x12, matrix products: 125 us -> 96.3 us  [the longest x1 15.1 us: on_device_chip(): act_grad = jnp.dot(grad_m, w_fc2, preferred_element_type=F32)]
  transfers between devices with their start and end apart: 17 -> 12, of which waited for: 13 -> 1; matrix products, arithmetic and copies ran while one was open for 29% -> 26% of each run, Pallas kernels for 0% -> 57%
where the time goes in v1:
time: 719 us; the launch traced here: 714 us
  Pallas kernels  406 us (56%)
  matrix products  179 us (25%)
  other arithmetic  66.7 us (9%)
  local copies, waits for them, and re-layouts  31.5 us (4%)
  starting transfers between devices  17.2 us (2%)
  waiting for transfers between devices  11 us (2%)
    pallas_call x2, Pallas kernels, reduce_grads(): pl.pallas_call(functools.partial(reduce_kernel, chunks, count), out_shape...  182 us
    pallas_call x2, Pallas kernels, gather_weights(): pl.pallas_call(functools.partial(gather_kernel, chunks, count), out_shape...  177 us
    pallas_call x1, Pallas kernels, mod_backward(): pl.pallas_call(mod_backward_kernel, out_shape=[jax.ShapeDtypeStruct((72,...  31.5 us
    convert_element_type x2, other arithmetic, attend_backward(): score_grad = (probs * (prob_grad - inner)).astype(jnp.bfloat16)  26.5 us
    dot_general x2, matrix products, attend_backward(): jnp.einsum('qhe,khe->hqk', grad_block, values_all, preferred_element_type...  26.2 us
    pallas_call x1, Pallas kernels, mod_forward(): pl.pallas_call(mod_forward_kernel, out_shape=[jax.ShapeDtypeStruct((1, n)...  15.7 us
    dot_general x1, matrix products, on_device_chip(): act_grad = jnp.dot(grad_m, w_fc2, preferred_element_type=F32)  15.1 us
    dot_general x2, matrix products, attend_backward(): jnp.einsum('hqk,qhe->khe', prob_low, grad_block, preferred_element_type=j...  14.9 us
  transfers between devices with their start and end apart: 12, of which 1 were waited for; matrix products, arithmetic and copies ran while one was open for 26% of the time, Pallas kernels for 57%

profile of v1, /device:TPU:1, one launch (start us, length us, event | category | flops | bytes accessed | tf_op | source)
XLA Modules:
  0.0 714.4 jit_solution(7678026588017761648)
XLA Ops:
  2.3 2.4 pad_maximum_fusion.14
  4.7 4.5 collective-permute-start
  10.1 15.7 %shard_map.228 = (f32[1,6912]{1,0:T(1,128)S(1)}, bf16[16,8,128]{2,1,0:T(8,128)(2,1)S(1)}) custom-call(bf16[16,8,128]{2,1,0:T(8,128)(2,1)S(1)} %pad.4.piece_ref, bf16[72,6912]{1,0:T(8,128)(2,1)S(1)} %copy-done, f32[1,6912]{1,0:T(1,128)S(1)} %reshape.265.bias_ref), custom_call_target="tpu_custom_call" | custom-call | tf_op jit(solution)/shard_map/pallas_call | solution.py:769
  30.0 48.4 %shard_map.229 = bf16[16,72,1728]{2,1,0:T(8,128)(2,1)} custom-call(bf16[1,72,1728]{2,1,0:T(8,128)(2,1)} %reshape.239.refs_0_), custom_call_target="tpu_custom_call" | custom-call | tf_op jit(solution)/shard_map/pallas_call | solution.py:480
  78.3 128.9 %shard_map.230 = (bf16[16,72,576]{2,1,0:T(8,128)(2,1)}, bf16[16,72,2304]{2,1,0:T(8,128)(2,1)}, bf16[16,72,2304]{2,1,0:T(8,128)(2,1)}) custom-call(bf16[1,72,576]{2,1,0:T(8,128)(2,1)} %bitcast.138, bf16[1,72,2304]{2,1,0:T(8,128)(2,1)} %bitcast.135, bf16[1,72,2304]{2,1,0:T(8,128)(2,1)} %bitcast.136), custom_call_target="tpu_custom_call" | custom-call | tf_op jit(solution)/shard_map/pallas_call | solution.py:480
  207.4 7.4 %add_convert_fusion = bf16[1024,1728]{0,1:T(8,128)(2,1)S(1)} fusion(bf16[1152,1728]{1,0:T(8,128)(2,1)} %bitcast.129, f32[1728]{0:T(1024)S(1)} %convert_element_type.147, bf16[512,1152]{1,0:T(8,128)(2,1)} %collective-permute-done.1, bf16[512,1152]{1,0:T(8,128)(2,1)S(1)} %fusion.28), kind=kOutput, calls=%fused_computation.40 | convolution fusion | flops 4085121024 | bytes 9886464 | tf_op jit(solution)/shard_map/dot_general | solution.py:1027
  214.8 2.5 multiply_reduce_fusion.2
  217.3 8.7 %multiply_reduce_fusion.3 = (f32[8,512]{1,0:T(8,128)S(1)}, f32[8,512,1024]{2,1,0:T(8,128)}) fusion(bf16[1024,3,8,72]{0,3,2,1:T(8,128)(2,1)S(1)} %bitcast.106), kind=kOutput, calls=%fused_computation.13 | convolution fusion | flops 612364288 | bytes 18563072 | tf_op jit(solution)/shard_map/qhe,khe->hqk/dot_general | solution.py:39
  226.0 4.2 fusion.1
  230.2 4.7 fusion.42
  234.9 8.0 %fusion = f32[8,512]{1,0:T(8,128)S(1)} fusion(f32[8,512,1024]{2,1,0:T(8,128)} %get-tuple-element.108, f32[8,512]{1,0:T(8,128)S(1)} %get-tuple-element.107), kind=kLoop, calls=%fused_computation.10 | loop fusion | flops 12578816 | bytes 16809984 | tf_op jit(solution)/shard_map/reduce_sum | solution.py:44
  243.0 2.7 copy-done.3
  245.7 4.7 fusion.43
  250.5 2.2 fusion.44
  254.5 4.3 collective-permute-start.6
  261.8 10.9 %collective-permute-done.6 = bf16[512,1152]{1,0:T(8,128)(2,1)S(1)} collective-permute-done((bf16[512,1152]{1,0:T(8,128)(2,1)S(1)}, bf16[512,1152]{1,0:T(8,128)(2,1)S(1)}, u32[]{:S(2)}, u32[]{:S(2)}) %collective-permute-start.6) | collective-permute-done | bytes 1179680 | tf_op jit(solution)/shard_map/ppermute | solution.py:958
  272.7 1.9 convert_reduce_fusion.4
  274.7 12.1 %fusion.39 = f32[1024,2304]{1,0:T(8,128)} fusion(bf16[1152,2304]{1,0:T(8,128)(2,1)} %bitcast.139, bf16[512,1152]{1,0:T(8,128)(2,1)} %collective-permute-done.3, bf16[512,1152]{1,0:T(8,128)(2,1)} %add_convert_fusion.3), kind=kOutput, calls=%fused_computation.92 | convolution fusion | flops 5440536576 | bytes 17104896 | tf_op jit(solution)/shard_map/dot_general | solution.py:1037
  286.8 12.6 %fusion.69 = f32[1024,1152]{1,0:T(8,128)S(1)} fusion(bf16[1152,2304]{1,0:T(8,128)(2,1)} %bitcast.143, f32[1024,2304]{1,0:T(8,128)} %fusion.39, f32[2304]{0:T(1024)S(1)} %reshape.266), kind=kOutput, calls=%fused_computation.167 | convolution fusion | flops 5459410944 | bytes 19473408 | tf_op jit(solution)/shard_map/rf,df->rd/dot_general | solution.py:1041
  299.5 15.1 %convert_reduce_fusion = (f32[2304]{0:T(1024)S(1)}, bf16[1024,2304]{1,0:T(8,128)(2,1)S(1)}) fusion(f32[1024,2304]{1,0:T(8,128)} %fusion.39, f32[2304]{0:T(1024)S(1)} %reshape.266, bf16[1152,2304]{1,0:T(8,128)(2,1)S(1)} %bitcast.146, bf16[512,1152]{1,0:T(8,128)(2,1)} %collective-permute-done.7, bf16[512,1152]{1,0:T(8,128)(2,1)} %get-tuple-element.84), kind=kOutput, calls=%fused_computation.27 | convolution fusion | flops 5494798336 | bytes 21841920 | tf_op jit(solution)/shard_map/dot_general | solution.py:1050
  314.6 6.3 fusion.77
  321.8 11.8 %convolution_convert_fusion.1 = bf16[1152,2304]{1,0:T(8,128)(2,1)} fusion(bf16[512,1152]{1,0:T(8,128)(2,1)} %collective-permute-done.7, bf16[512,1152]{1,0:T(8,128)(2,1)} %get-tuple-element.84, f32[1024,2304]{1,0:T(8,128)} %fusion.39, f32[2304]{0:T(1024)S(1)} %reshape.266), kind=kOutput, calls=%fused_computation.17 | convolution fusion | flops 5466783744 | bytes 17114112 | tf_op jit(solution)/shard_map/rd,rf->df/dot_general | solution.py:1049
  336.3 2.6 fusion.33
  339.3 9.6 %convolution_convert_fusion = bf16[1152,2304]{1,0:T(8,128)(2,1)} fusion(bf16[1024,2304]{1,0:T(8,128)(2,1)S(1)} %get-tuple-element.114, bf16[512,1152]{1,0:T(8,128)(2,1)} %collective-permute-done.3, bf16[512,1152]{1,0:T(8,128)(2,1)} %add_convert_fusion.3), kind=kOutput, calls=%fused_computation.16 | convolution fusion | flops 5443190784 | bytes 12386304 | tf_op jit(solution)/shard_map/rd,rf->df/dot_general | solution.py:1053
  348.9 3.6 collective-permute-start.5
  352.6 1.8 convolution_convert_fusion.4
  355.3 11.5 %multiply_reduce_fusion.1 = (f32[8,512]{1,0:T(8,128)S(1)}, f32[8,512,1024]{2,1,0:T(8,128)}) fusion(f32[8,512,1024]{2,1,0:T(8,128)} %get-tuple-element.108, f32[8,512]{1,0:T(8,128)S(1)} %log_add_fusion.1, bf16[512,8,72]{0,2,1:T(8,128)(2,1)S(1)} %bitcast.123, bf16[1024,3,8,72]{0,3,2,1:T(8,128)(2,1)S(1)} %bitcast.112), kind=kOutput, calls=%fused_computation.4 | convolution fusion | flops 620752896 | bytes 35356672 | tf_op jit(solution)/shard_map/qhe,khe->hqk/dot_general | solution.py:74
  366.9 16.0 %multiply_convert_fusion.1 = bf16[8,512,1024]{2,1,0:T(8,128)(2,1)} fusion(f32[8,512,1024]{2,1,0:T(8,128)} %get-tuple-element.110, f32[8,512,1024]{2,1,0:T(8,128)} %get-tuple-element.108, f32[8,512]{1,0:T(8,128)S(1)} %get-tuple-element.109, f32[8,512]{1,0:T(8,128)S(1)} %log_add_fusion.1), kind=kLoop, calls=%fused_computation.3 | loop fusion | flops 20971520 | bytes 41975808 | tf_op jit(solution)/shard_map/convert_element_type | solution.py:78
  382.8 7.2 %fusion.40 = bf16[512,8,72]{0,2,1:T(8,128)(2,1)} fusion(bf16[8,512,1024]{2,1,0:T(8,128)(2,1)} %multiply_convert_fusion.1, bf16[1024,3,8,72]{0,3,2,1:T(8,128)(2,1)S(1)} %bitcast.113), kind=kOutput, calls=%fused_computation.95 | convolution fusion | flops 604569600 | bytes 10158080 | tf_op jit(solution)/shard_map/hqk,khe->qhe/dot_general | solution.py:80
  390.1 5.0 fusion.49
  395.1 4.6 fusion.11
  399.7 14.7 %multiply_reduce_fusion = (f32[8,512]{1,0:T(8,128)S(1)}, f32[8,512,1024]{2,1,0:T(8,128)}) fusion(f32[8,512,1024]{2,1,0:T(8,128)} %copy-done.2, f32[8,512]{1,0:T(8,128)S(1)} %log_add_fusion, bf16[512,8,72]{0,2,1:T(8,128)(2,1)} %bitcast.126, bf16[1024,3,8,72]{0,3,2,1:T(8,128)(2,1)} %bitcast.109), kind=kOutput, calls=%fused_computation.1 | convolution fusion | flops 620752896 | bytes 35356672 | tf_op jit(solution)/shard_map/qhe,khe->hqk/dot_general | solution.py:74
  414.4 10.3 %add_bitcast_fusion = bf16[1024,1,8,72]{0,3,2,1:T(8,128)(2,1)} fusion(f32[8,72,1024]{2,1,0:T(8,128)S(1)} %fusion.11, bf16[512,8,72]{0,2,1:T(8,128)(2,1)} %bitcast.124, f32[8,512,1024]{2,1,0:T(8,128)} %get-tuple-element.108, f32[8,512]{1,0:T(8,128)S(1)} %log_add_fusion.1), kind=kOutput, calls=%fused_computation.84 | convolution fusion | flops 617742336 | bytes 20922368 | tf_op jit(solution)/shard_map/hqk,qhe->khe/dot_general | solution.py:90
  424.7 10.5 %multiply_convert_fusion = bf16[8,512,1024]{2,1,0:T(8,128)(2,1)} fusion(f32[8,512,1024]{2,1,0:T(8,128)} %get-tuple-element.112, f32[8,512,1024]{2,1,0:T(8,128)S(1)} %bitcast.104, f32[8,512]{1,0:T(8,128)S(1)} %get-tuple-element.111, f32[8,512]{1,0:T(8,128)S(1)} %log_add_fusion), kind=kLoop, calls=%fused_computation | loop fusion | flops 20971520 | bytes 41975808 | tf_op jit(solution)/shard_map/convert_element_type | solution.py:78
  435.2 6.6 fusion.41
  441.8 2.8 multiply_bitcast_fusion
  446.7 2.5 copy-done.20
  449.2 6.7 fusion.78
  459.2 128.0 %shard_map.233 = (f32[72,2304]{1,0:T(8,128)}, f32[72,2304]{1,0:T(8,128)}, f32[72,576]{1,0:T(8,128)}) custom-call(bf16[16,72,2304]{2,1,0:T(8,128)(2,1)} %bitcast.121, bf16[16,72,2304]{2,1,0:T(8,128)(2,1)} %bitcast.122, bf16[16,72,576]{2,1,0:T(8,128)(2,1)} %bitcast.120), custom_call_target="tpu_custom_call" | custom-call | tf_op jit(solution)/shard_map/pallas_call | solution.py:695
  587.5 2.9 slice.258
  590.5 9.0 %convolution_convert_fusion.2 = bf16[1152,1728]{0,1:T(8,128)(2,1)} fusion(bf16[1024,1728]{0,1:T(8,128)(2,1)} %bitcast.132, bf16[512,1152]{1,0:T(8,128)(2,1)} %collective-permute-done.1, bf16[512,1152]{1,0:T(8,128)(2,1)S(1)} %copy-done.27), kind=kOutput, calls=%fused_computation.37 | convolution fusion | flops 4083572736 | bytes 9879552 | tf_op jit(solution)/shard_map/rd,rc->dc/dot_general | solution.py:1071
  599.5 6.5 copy.32
  606.0 53.9 %shard_map.232 = f32[72,1728]{1,0:T(8,128)} custom-call(bf16[16,72,1728]{2,1,0:T(8,128)(2,1)} %bitcast.115), custom_call_target="tpu_custom_call" | custom-call | tf_op jit(solution)/shard_map/pallas_call | solution.py:695
  662.2 2.6 select_bitcast_fusion.1
  664.9 2.7 fusion.29
  671.1 1.9 collective-permute-start.11
  673.1 31.5 %shard_map.231 = (f32[72,6912]{1,0:T(8,128)S(1)}, f32[1,6912]{1,0:T(1,128)S(1)}, f32[16,8,128]{2,1,0:T(8,128)S(1)}, f32[1,2304]{1,0:T(1,128)S(1)}, f32[1,3456]{1,0:T(1,128)S(1)}) custom-call(f32[1,6912]{1,0:T(1,128)S(1)} %constant_dynamic-update-slice_fusion.v1_ref, f32[1,2304]{1,0:T(1,128)S(1)} %broadcast_in_dim.47.v2_ref, ...), custom_call_target="tpu_custom_call" | custom-call | tf_op jit(solution)/shard_map/pallas_call | solution.py:905
  708.0 2.4 select_bitcast_fusion
  (238 shorter events, 34.8 us)
Async XLA Ops:
  0.6 25.2 %copy-start.18 = (bf16[512,1,1152]{2,0,1:T(8,128)(2,1)S(1)}, bf16[512,1,1152]{2,0,1:T(8,128)(2,1)}, u32[]{:S(2)}) copy-start(bf16[512,1,1152]{2,0,1:T(8,128)(2,1)} %param.13) | copy-start | bytes 3538948
  0.7 8.6 %copy-start.40 = (bf16[1,1152]{1,0:T(2,128)(2,1)S(1)}, bf16[1,1152]{1,0:T(2,128)(2,1)}, u32[]{:S(2)}) copy-start(bf16[1,1152]{1,0:T(2,128)(2,1)} %param.14) | copy-start | bytes 6916
  0.7 9.3 %copy-start.43 = (bf16[6912]{0:T(1024)(128)(2,1)S(1)}, bf16[6912]{0:T(1024)(128)(2,1)}, u32[]{:S(2)}) copy-start(bf16[6912]{0:T(1024)(128)(2,1)} %param.16) | copy-start | bytes 41476
  0.7 9.4 %copy-start = (bf16[72,6912]{1,0:T(8,128)(2,1)S(1)}, bf16[72,6912]{1,0:T(8,128)(2,1)}, u32[]{:S(2)}) copy-start(bf16[72,6912]{1,0:T(8,128)(2,1)} %w_ref.3) | copy-start | bytes 2985988
  4.7 21.2 %collective-permute-start = (bf16[515,1152]{1,0:T(8,128)(2,1)}, bf16[515,1152]{1,0:T(8,128)(2,1)}, u32[]{:S(2)}, u32[]{:S(2)}) collective-permute-start(bf16[515,1152]{1,0:T(8,128)(2,1)} %pad_maximum_fusion.14), channel_id=1, source_target_pairs={{1,2},{2,1},{5,6},{6,5},{9,10},{10,9},{13,14},{14,13},{17,18},{18,... | collective-permute-start | bytes 3559688 | tf_op jit(solution)/shard_map/ppermute | solution.py:958
  27.5 179.8 %copy-start.5 = (bf16[515,1152]{1,0:T(8,128)(2,1)}, bf16[515,1152]{1,0:T(8,128)(2,1)S(1)}, u32[]{:S(2)}) copy-start(bf16[515,1152]{1,0:T(8,128)(2,1)S(1)} %broadcast_select_fusion) | copy-start | bytes 3559684
  28.8 178.7 %copy-start.26 = (bf16[512,1152]{1,0:T(8,128)(2,1)}, bf16[512,1152]{1,0:T(8,128)(2,1)S(1)}, u32[]{:S(2)}) copy-start(bf16[512,1152]{1,0:T(8,128)(2,1)S(1)} %fusion.28) | copy-start | bytes 3538948
  28.8 178.7 %collective-permute-start.1 = (bf16[512,1152]{1,0:T(8,128)(2,1)S(1)}, bf16[512,1152]{1,0:T(8,128)(2,1)}, u32[]{:S(2)}, u32[]{:S(2)}) collective-permute-start(bf16[512,1152]{1,0:T(8,128)(2,1)S(1)} %fusion.28), channel_id=1, source_target_pairs={{0,2},{1,3},{2,0},{3,1},{4,6},{5,7},{6,4},{7,5},{8,10},{9,11},{10,... | collective-permute-start | bytes 3538952 | tf_op jit(solution)/shard_map/ppermute | solution.py:964
  214.8 28.2 %copy-start.8 = (bf16[1024,1728]{0,1:T(8,128)(2,1)}, bf16[1024,1728]{0,1:T(8,128)(2,1)S(1)}, u32[]{:S(2)}) copy-start(bf16[1024,1728]{0,1:T(8,128)(2,1)S(1)} %add_convert_fusion) | copy-start | bytes 10616836
  217.3 12.9 %copy-start.2 = (f32[8,512,1024]{2,1,0:T(8,128)}, f32[8,512,1024]{2,1,0:T(8,128)S(1)}, u32[]{:S(2)}) copy-start(f32[8,512,1024]{2,1,0:T(8,128)S(1)} %get-tuple-element.106) | copy-start | bytes 50331652
  234.9 15.5 %copy-start.50 = (bf16[8,72,512]{2,1,0:T(8,128)(2,1)}, bf16[8,72,512]{2,1,0:T(8,128)(2,1)S(1)}, u32[]{:S(2)}) copy-start(bf16[8,72,512]{2,1,0:T(8,128)(2,1)S(1)} %fusion.42) | copy-start | bytes 1769476
  234.9 10.8 %copy-start.3 = (f32[8,512,1024]{2,1,0:T(8,128)S(1)}, f32[8,512,1024]{2,1,0:T(8,128)}, u32[]{:S(2)}) copy-start(f32[8,512,1024]{2,1,0:T(8,128)} %get-tuple-element.108) | copy-start | bytes 50331652
  252.7 6.8 copy-start.14
  252.9 6.0 collective-permute-start.2
  254.5 18.2 %collective-permute-start.6 = (bf16[512,1152]{1,0:T(8,128)(2,1)S(1)}, bf16[512,1152]{1,0:T(8,128)(2,1)S(1)}, u32[]{:S(2)}, u32[]{:S(2)}) collective-permute-start(bf16[512,1152]{1,0:T(8,128)(2,1)S(1)} %bitcast.133), channel_id=1, source_target_pairs={{1,2},{2,1},{5,6},{6,5},{9,10},{10,9},{13,14},{14,13},{17,18},{18,... | collective-permute-start | bytes 3538952 | tf_op jit(solution)/shard_map/ppermute | solution.py:958
  261.7 12.9 %collective-permute-start.3 = (bf16[512,1152]{1,0:T(8,128)(2,1)}, bf16[512,1152]{1,0:T(8,128)(2,1)}, u32[]{:S(2)}, u32[]{:S(2)}) collective-permute-start(bf16[512,1152]{1,0:T(8,128)(2,1)} %add_convert_fusion.3), channel_id=1, source_target_pairs={{0,2},{1,3},{2,0},{3,1},{4,6},{5,7},{6,4},{7,5},{8,10},{9,11},{10,... | collective-permute-start | bytes 3538952 | tf_op jit(solution)/shard_map/ppermute | solution.py:964
  274.6 24.8 %collective-permute-start.7 = (bf16[512,1152]{1,0:T(8,128)(2,1)}, bf16[512,1152]{1,0:T(8,128)(2,1)}, u32[]{:S(2)}, u32[]{:S(2)}) collective-permute-start(bf16[512,1152]{1,0:T(8,128)(2,1)} %get-tuple-element.84), channel_id=1, source_target_pairs={{0,2},{1,3},{2,0},{3,1},{4,6},{5,7},{6,4},{7,5},{8,10},{9,11},{10,... | collective-permute-start | bytes 3538952 | tf_op jit(solution)/shard_map/ppermute | solution.py:964
  274.7 24.8 %slice-start.14 = ((s8[5308416]{0:T(1024)(128)(4,1)}), s8[4194304]{0:T(1024)(128)(4,1)S(1)}, s32[]{:S(2)}) async-start(s8[5308416]{0:T(1024)(128)(4,1)} %bitcast.144), calls=%async_computation.14 | async-start | bytes 8388608
  286.8 12.6 %slice-start.15 = ((s8[5308416]{0:T(1024)(128)(4,1)}), s8[1114112]{0:T(1024)(128)(4,1)S(1)}, s32[]{:S(2)}) async-start(s8[5308416]{0:T(1024)(128)(4,1)} %bitcast.144), calls=%async_computation.15 | async-start | bytes 2228224
  286.8 27.8 %slice-start.12 = ((s8[5308416]{0:T(1024)(128)(4,1)}), s8[1114112]{0:T(1024)(128)(4,1)S(1)}, s32[]{:S(2)}) async-start(s8[5308416]{0:T(1024)(128)(4,1)} %bitcast.140), calls=%async_computation.12 | async-start | bytes 2228224
  299.4 15.2 %slice-start.13 = ((s8[5308416]{0:T(1024)(128)(4,1)}), s8[4194304]{0:T(1024)(128)(4,1)S(1)}, s32[]{:S(2)}) async-start(s8[5308416]{0:T(1024)(128)(4,1)} %bitcast.140), calls=%async_computation.13 | async-start | bytes 8388608
  320.9 14.7 %slice-start.10 = ((s8[4718592]{0:T(1024)(128)(4,1)}), s8[4194304]{0:T(1024)(128)(4,1)S(1)}, s32[]{:S(2)}) async-start(s8[4718592]{0:T(1024)(128)(4,1)} %bitcast.118), calls=%async_computation.10 | async-start | bytes 8388608
  321.1 14.5 %slice-start.11 = ((s8[4718592]{0:T(1024)(128)(4,1)}), s8[524288]{0:T(1024)(128)(4,1)S(1)}, s32[]{:S(2)}) async-start(s8[4718592]{0:T(1024)(128)(4,1)} %bitcast.118), calls=%async_computation.11 | async-start | bytes 1048576
  321.2 14.4 %collective-permute-start.4 = (bf16[512,1152]{1,0:T(8,128)(2,1)S(1)}, bf16[512,1152]{1,0:T(8,128)(2,1)S(1)}, u32[]{:S(2)}, u32[]{:S(2)}) collective-permute-start(bf16[512,1152]{1,0:T(8,128)(2,1)S(1)} %slice.260), channel_id=1, source_target_pairs={{0,2},{1,3},{2,0},{3,1},{4,6},{5,7},{6,4},{7,5},{8,10},{9,11},{10,... | collective-permute-start | bytes 3538952 | tf_op jit(solution)/shard_map/ppermute | solution.py:969
  321.7 11.9 %collective-permute-start.8 = (bf16[512,1152]{1,0:T(8,128)(2,1)S(1)}, bf16[512,1152]{1,0:T(8,128)(2,1)S(1)}, u32[]{:S(2)}, u32[]{:S(2)}) collective-permute-start(bf16[512,1152]{1,0:T(8,128)(2,1)S(1)} %slice.259), channel_id=1, source_target_pairs={{0,2},{1,3},{2,0},{3,1},{4,6},{5,7},{6,4},{7,5},{8,10},{9,11},{10,... | collective-permute-start | bytes 3538952 | tf_op jit(solution)/shard_map/ppermute | solution.py:969
  338.9 13.7 %copy-start.23 = (bf16[512,1152]{1,0:T(8,128)(2,1)}, bf16[512,1152]{1,0:T(8,128)(2,1)S(1)}, u32[]{:S(2)}) copy-start(bf16[512,1152]{1,0:T(8,128)(2,1)S(1)} %get-tuple-element.98) | copy-start | bytes 3538948
  338.9 13.7 %copy-start.47 = (bf16[16,72,576]{2,1,0:T(8,128)(2,1)S(1)}, bf16[16,72,576]{2,1,0:T(8,128)(2,1)}, u32[]{:S(2)}) copy-start(bf16[16,72,576]{2,1,0:T(8,128)(2,1)} %get-tuple-element.27) | copy-start | bytes 3981316
  338.9 13.7 %collective-permute-start.9 = (bf16[512,1152]{1,0:T(8,128)(2,1)S(1)}, bf16[512,1152]{1,0:T(8,128)(2,1)S(1)}, u32[]{:S(2)}, u32[]{:S(2)}) collective-permute-start(bf16[512,1152]{1,0:T(8,128)(2,1)S(1)} %get-tuple-element.98), channel_id=1, source_target_pairs={{0,2},{1,3},{2,0},{3,1},{4,6},{5,7},{6,4},{7,5},{8,10},{9,11},{10,... | collective-permute-start | bytes 3538952 | tf_op jit(solution)/shard_map/ppermute | solution.py:964
  348.9 313.3 %collective-permute-start.5 = (bf16[512,1152]{1,0:T(8,128)(2,1)}, bf16[512,1152]{1,0:T(8,128)(2,1)}, u32[]{:S(2)}, u32[]{:S(2)}) collective-permute-start(bf16[512,1152]{1,0:T(8,128)(2,1)} %get-tuple-element.96), channel_id=1, source_target_pairs={{1,2},{2,1},{5,6},{6,5},{9,10},{10,9},{13,14},{14,13},{17,18},{18,... | collective-permute-start | bytes 3538952 | tf_op jit(solution)/shard_map/ppermute | solution.py:958
  355.3 11.5 %copy-start.15 = (bf16[512,576]{0,1:T(8,128)(2,1)}, bf16[512,576]{0,1:T(8,128)(2,1)S(1)}, u32[]{:S(2)}) copy-start(bf16[512,576]{0,1:T(8,128)(2,1)S(1)} %get-tuple-element.99) | copy-start | bytes 1769476
  366.8 28.2 %slice-start = ((s8[16777216]{0:T(1024)(128)(4,1)}), s8[4194304]{0:T(1024)(128)(4,1)S(1)}, s32[]{:S(2)}) async-start(s8[16777216]{0:T(1024)(128)(4,1)} %bitcast.101), calls=%async_computation | async-start | bytes 8388608
  366.8 28.2 %slice-start.1 = ((s8[16777216]{0:T(1024)(128)(4,1)}), s8[4194304]{0:T(1024)(128)(4,1)S(1)}, s32[]{:S(2)}) async-start(s8[16777216]{0:T(1024)(128)(4,1)} %bitcast.101), calls=%async_computation.1 | async-start | bytes 8388608
  366.9 28.2 %slice-start.2 = ((s8[16777216]{0:T(1024)(128)(4,1)}), s8[4194304]{0:T(1024)(128)(4,1)S(1)}, s32[]{:S(2)}) async-start(s8[16777216]{0:T(1024)(128)(4,1)} %bitcast.101), calls=%async_computation.2 | async-start | bytes 8388608
  382.8 12.2 %slice-start.3 = ((s8[16777216]{0:T(1024)(128)(4,1)}), s8[4194304]{0:T(1024)(128)(4,1)S(1)}, s32[]{:S(2)}) async-start(s8[16777216]{0:T(1024)(128)(4,1)} %bitcast.101), calls=%async_computation.3 | async-start | bytes 8388608
  399.7 25.0 %slice-start.4 = ((s8[16777216]{0:T(1024)(128)(4,1)}), s8[4194304]{0:T(1024)(128)(4,1)S(1)}, s32[]{:S(2)}) async-start(s8[16777216]{0:T(1024)(128)(4,1)} %bitcast.103), calls=%async_computation.4 | async-start | bytes 8388608
  399.7 25.0 %slice-start.5 = ((s8[16777216]{0:T(1024)(128)(4,1)}), s8[4194304]{0:T(1024)(128)(4,1)S(1)}, s32[]{:S(2)}) async-start(s8[16777216]{0:T(1024)(128)(4,1)} %bitcast.103), calls=%async_computation.5 | async-start | bytes 8388608
  399.7 25.0 %slice-start.6 = ((s8[16777216]{0:T(1024)(128)(4,1)}), s8[4194304]{0:T(1024)(128)(4,1)S(1)}, s32[]{:S(2)}) async-start(s8[16777216]{0:T(1024)(128)(4,1)} %bitcast.103), calls=%async_computation.6 | async-start | bytes 8388608
  414.4 10.3 %slice-start.7 = ((s8[16777216]{0:T(1024)(128)(4,1)}), s8[4194304]{0:T(1024)(128)(4,1)S(1)}, s32[]{:S(2)}) async-start(s8[16777216]{0:T(1024)(128)(4,1)} %bitcast.103), calls=%async_computation.7 | async-start | bytes 8388608
  446.7 9.1 %copy-start.21 = (bf16[1024,3,8,72]{0,3,2,1:T(8,128)(2,1)}, bf16[1024,3,8,72]{0,3,2,1:T(8,128)(2,1)S(1)}, u32[]{:S(2)}) copy-start(bf16[1024,3,8,72]{0,3,2,1:T(8,128)(2,1)S(1)} %get-tuple-element.82) | copy-start | bytes 10616836
  449.1 6.7 copy-start.24
  449.1 6.7 copy-start.49
  449.2 6.7 copy-start.51
  449.2 6.7 copy-start.53
  590.4 74.5 %collective-permute-start.10 = (bf16[512,1152]{1,0:T(8,128)(2,1)}, bf16[512,1152]{1,0:T(8,128)(2,1)S(1)}, u32[]{:S(2)}, u32[]{:S(2)}) collective-permute-start(bf16[512,1152]{1,0:T(8,128)(2,1)} %slice.258), channel_id=1, source_target_pairs={{0,2},{1,3},{2,0},{3,1},{4,6},{5,7},{6,4},{7,5},{8,10},{9,11},{10,... | collective-permute-start | bytes 3538952 | tf_op jit(solution)/shard_map/ppermute | solution.py:969
  660.0 7.7 %slice-start.8 = ((s8[4718592]{0:T(1024)(128)(4,1)}), s8[524288]{0:T(1024)(128)(4,1)S(1)}, s32[]{:S(2)}) async-start(s8[4718592]{0:T(1024)(128)(4,1)} %bitcast.116), calls=%async_computation.8 | async-start | bytes 1048576
  669.6 37.8 %copy-start.41 = (bf16[1,1152]{1,0:T(2,128)(2,1)S(1)}, bf16[1,1152]{1,0:T(2,128)(2,1)}, u32[]{:S(2)}) copy-start(bf16[1,1152]{1,0:T(2,128)(2,1)} %param.14) | copy-start | bytes 6916
  669.6 37.8 %copy-start.42 = (f32[1,1152]{1,0:T(1,128)S(1)}, f32[1,1152]{1,0:T(1,128)}, u32[]{:S(2)}) copy-start(f32[1,1152]{1,0:T(1,128)} %get-tuple-element.95) | copy-start | bytes 13828
  671.1 36.9 %collective-permute-start.11 = (bf16[512,1152]{1,0:T(8,128)(2,1)}, bf16[512,1152]{1,0:T(8,128)(2,1)}, u32[]{:S(2)}, u32[]{:S(2)}) collective-permute-start(bf16[512,1152]{1,0:T(8,128)(2,1)} %add_convert_fusion.1), channel_id=1, source_target_pairs={{1,2},{2,1},{5,6},{6,5},{9,10},{10,9},{13,14},{14,13},{17,18},{18,... | collective-permute-start | bytes 3538952 | tf_op jit(solution)/shard_map/ppermute | solution.py:958
  (34 other events, 99.4 us)

commit v2 on v1

--- a/solution.py
+++ b/solution.py
@@ -1,4 +1,5 @@
 import functools
+import math
 
 import jax
 import jax.numpy as jnp
@@ -329,7 +330,9 @@
 
 
 def chip_peers(pos):
-    return list(neighbours(pos)) + [z_peer(pos, k) for k in (1, 2, 3)]
+    d, z, x, c, y = pos
+    across = [(z * 4 + x * 2 + 1 - c, 1 - y)]
+    return list(neighbours(pos)) + across + [z_peer(pos, k) for k in (1, 2, 3)]
 
 
 def remote(src, dst, send, recv, peer):
@@ -338,131 +341,149 @@
     )
 
 
-GATHER_RECV = 17
-GATHER_SEND = 17
+GATHER_RECV = 24
+GATHER_SEND = 28
 
 
 class Gather:
-    def __init__(self, shard, full, cols, recv, send, pos):
-        self.shard, self.full, self.cols = shard, full, cols
+    def __init__(self, shard, full, relay, cols, recv, send, pos):
+        self.shard, self.full, self.relay, self.cols = shard, full, relay, cols
         self.recv, self.send, self.pos = recv, send, pos
-        self.sib, self.xn, self.yn = neighbours(pos)
-        self.home = pos[3] == pos[4]
-        self.away = pos[3] != pos[4]
-
-    def rows(self, b, n):
+        d, z, x, c, y = pos
+        self.sib, self.xn, _ = neighbours(pos)
+        self.far = (z * 4 + x * 2 + y, 1 - y)
+        self.home, self.away = c == y, c != y
+
+    def part(self, ref, b):
         if self.cols is None:
-            return self.full.at[pl.ds(b, n)]
-        return self.full.at[pl.ds(b, n), :, pl.ds(*self.cols)]
-
-    def own(self):
-        if self.cols is None:
-            return self.shard
-        return self.shard.at[:, :, pl.ds(*self.cols)]
-
-    def copy(self, b, n, peer, s, r):
-        ref = self.rows(b, n)
-        return remote(ref, ref, self.send.at[s], self.recv.at[r], peer)
+            return ref.at[pl.ds(b, 1)]
+        return ref.at[pl.ds(b, 1), :, pl.ds(*self.cols)]
+
+    def move(self, src, dst, s, r, peer):
+        return remote(src, dst, self.send.at[s], self.recv.at[r], peer)
+
+    def came(self, r):
+        block = self.part(self.full, 0)
+        self.move(block, block, 0, r, self.sib).wait_recv()
 
     def stay(self):
-        return pltpu.make_async_copy(self.own(), self.rows(self.pos[0], 1), self.send.at[16])
-
-    def join(self):
-        d = self.pos[0]
-
-        @pl.when(self.away)
-        def _():
-            remote(
-                self.own(), self.rows(d, 1), self.send.at[15], self.recv.at[16], self.sib
-            ).start()
-
-        @pl.when(self.home)
-        def _():
-            self.stay().start()
-
-    def spread(self):
+        return pltpu.make_async_copy(
+            self.part(self.shard, 0), self.part(self.full, self.pos[0]), self.send.at[27]
+        )
+
+    def start(self):
         d, z, x, c, y = self.pos
         q = z * 2 + x
+        own = self.part(self.shard, 0)
 
         @pl.when(self.home)
         def _():
-            self.stay().wait()
-            self.copy(2 * q + 1 - c, 1, self.sib, 15, 16).wait_recv()
             for k in (2, 1, 3):
-                self.copy(2 * q, 2, z_peer(self.pos, k), k - 1, q).start()
-            self.copy(2 * q, 2, self.xn, 3, q).start()
-            self.copy(2 * q, 2, self.yn, 4, q).start()
+                self.move(own, self.part(self.full, d), k, q, z_peer(self.pos, k)).start()
+            self.move(own, self.part(self.full, d), 4, q, self.xn).start()
+            self.move(own, self.part(self.full, d), 8, 8 + q, self.far).start()
+            self.stay().start()
+
+        @pl.when(self.away)
+        def _():
+            for k in (2, 1, 3):
+                self.move(own, self.part(self.relay, q), k, q, z_peer(self.pos, k)).start()
+            self.move(own, self.part(self.full, d), 8, 16 + q, self.far).start()
+            self.move(own, self.part(self.relay, q), 4, q, self.xn).start()
+            self.move(own, self.part(self.full, d), 16, 8 + q, self.sib).start()
 
     def from_z(self, k):
         d, z, x, c, y = self.pos
         q = ((z + k) % 4) * 2 + x
+        dst = self.part(self.full, 2 * q + c)
 
         @pl.when(self.home)
         def _():
-            self.copy(2 * q, 2, self.xn, 0, q).wait_recv()
-            self.copy(2 * q, 2, self.xn, 3 + 2 * k, q).start()
-            self.copy(2 * q, 2, self.yn, 4 + 2 * k, q).start()
-
-    def cross(self, k):
+            self.came(q)
+            self.move(dst, dst, 4 + k, q, self.xn).start()
+            self.move(dst, dst, 8 + k, 8 + q, self.far).start()
+
+        @pl.when(self.away)
+        def _():
+            self.came(q)
+            src = self.part(self.relay, q)
+            self.move(src, dst, 8 + k, 16 + q, self.far).start()
+            self.move(src, src, 4 + k, q, self.xn).start()
+            self.move(src, dst, 16 + k, 8 + q, self.sib).start()
+
+    def from_x(self, k):
         d, z, x, c, y = self.pos
-        zz = (z + k) % 4
+        q = ((z + k) % 4) * 2 + 1 - x
+        dst = self.part(self.full, 2 * q + c)
 
         @pl.when(self.home)
         def _():
-            q = zz * 2 + 1 - x
-            self.copy(2 * q, 2, self.xn, 0, q).wait_recv()
-            self.copy(2 * q, 1, self.yn, 11 + k, 8 + zz).start()
+            self.came(q)
+            self.move(dst, dst, 12 + k, 8 + q, self.far).start()
 
         @pl.when(self.away)
         def _():
-            q = zz * 2 + x
-            self.copy(2 * q, 2, self.xn, 0, q).wait_recv()
-            self.copy(2 * q + 1, 1, self.xn, 11 + k, 12 + zz).start()
+            self.came(q)
+            self.move(self.part(self.relay, q), dst, 20 + k, 8 + q, self.sib).start()
+
+    def from_y(self, k):
+        d, z, x, c, y = self.pos
+        q = ((z + k) % 4) * 2 + x
+
+        @pl.when(self.away)
+        def _():
+            block = self.part(self.full, 2 * q + 1 - c)
+            self.came(16 + q)
+            self.move(block, block, 12 + k, 16 + q, self.xn).start()
 
     def finish(self):
         d, z, x, c, y = self.pos
+        block = self.part(self.full, 0)
 
         @pl.when(self.home)
         def _():
-            for i in range(11):
-                self.copy(0, 2, self.xn, i, 0).wait_send()
+            self.stay().wait()
+            for q in range(8):
+                self.came(8 + q)
+            for s in list(range(1, 16)):
+                self.move(block, block, s, 0, self.sib).wait_send()
+
+        @pl.when(self.away)
+        def _():
+            for q in range(8):
+                self.came(8 + q)
             for k in range(4):
-                self.copy(0, 1, self.yn, 11 + k, 8).wait_send()
-
-        @pl.when(self.away)
-        def _():
-            for k in range(4):
-                zz = (z + k) % 4
-                q = zz * 2 + 1 - x
-                self.copy(2 * q, 1, self.yn, 0, 8 + zz).wait_recv()
-                self.copy(2 * q + 1, 1, self.xn, 0, 12 + zz).wait_recv()
-            self.copy(0, 1, self.sib, 15, 16).wait_send()
-            for k in range(4):
-                self.copy(0, 1, self.xn, 11 + k, 12).wait_send()
+                self.came(16 + ((z + k) % 4) * 2 + 1 - x)
+            for s in list(range(1, 24)):
+                self.move(block, block, s, 0, self.sib).wait_send()
 
 
 def gather_events(parts):
-    events = [p.join for p in parts] + [p.spread for p in parts]
+    events = [p.start for p in parts]
     for p in parts:
-        events += [functools.partial(p.from_z, k) for k in (1, 2, 3)]
+        for k in (1, 2, 3):
+            events.append(functools.partial(p.from_z, k))
+    late = []
     for p in parts:
-        events += [functools.partial(p.cross, k) for k in range(4)]
-    return events + [p.finish for p in parts]
-
-
-def gather_parts(shards, fulls, chunks, recv, send, pos):
+        for k in range(4):
+            late.append(functools.partial(p.from_x, k))
+            late.append(functools.partial(p.from_y, k))
+    return events + late + [p.finish for p in parts]
+
+
+def gather_parts(shards, fulls, relays, chunks, recv, send, pos):
     return [
-        Gather(shards[g], fulls[g], cols, recv.at[i], send.at[i], pos)
+        Gather(shards[g], fulls[g], relays[g], cols, recv.at[i], send.at[i], pos)
         for i, (g, cols) in enumerate(chunks)
     ]
 
 
 def gather_kernel(chunks, count, *refs):
-    shards, fulls = refs[:count], refs[count : 2 * count]
-    recv, send = refs[2 * count :]
+    shards, fulls, relays = (refs[i * count : (i + 1) * count] for i in range(3))
+    recv, send = refs[3 * count :]
     pos = place()
     greet(chip_peers(pos))
-    for event in gather_events(gather_parts(shards, fulls, chunks, recv, send, pos)):
+    for event in gather_events(gather_parts(shards, fulls, relays, chunks, recv, send, pos)):
         event()
 
 
@@ -474,206 +495,211 @@
     ]
 
 
+def gather_shapes(shards):
+    return [jax.ShapeDtypeStruct((16,) + s.shape[1:], s.dtype) for s in shards] + [
+        jax.ShapeDtypeStruct((8,) + s.shape[1:], s.dtype) for s in shards
+    ]
+
+
 def gather_weights(shards, chunks, collective_id):
     count = len(shards)
     anywhere = pl.BlockSpec(memory_space=pl.ANY)
     return pl.pallas_call(
         functools.partial(gather_kernel, chunks, count),
-        out_shape=[jax.ShapeDtypeStruct((16,) + s.shape[1:], s.dtype) for s in shards],
+        out_shape=gather_shapes(shards),
         in_specs=[anywhere] * count,
-        out_specs=[anywhere] * count,
+        out_specs=[anywhere] * (2 * count),
         scratch_shapes=gather_sems(chunks),
         compiler_params=pltpu.CompilerParams(
             collective_id=collective_id, has_side_effects=True
         ),
-    )(*shards)
-
-
-REDUCE_RECV = 24
-REDUCE_SEND = 17
+    )(*shards)[:count]
+
+
+REDUCE_RECV = 27
+REDUCE_SEND = 23
 
 
 class Reduce:
-    def __init__(self, grad, land, spare, out, recv, send, pos, cols):
-        self.grad, self.land, self.spare, self.out = grad, land, spare, out
+    def __init__(self, grad, land, out, recv, send, pos, cols):
+        self.grad, self.land, self.out = grad, land, out
         self.recv, self.send, self.pos, self.cols = recv, send, pos, pl.ds(*cols)
+        d, z, x, c, y = pos
         self.sib, self.xn, self.yn = neighbours(pos)
-        self.home = pos[3] == pos[4]
-        self.away = pos[3] != pos[4]
-
-    def rows(self, b, n=1):
-        return self.grad.at[pl.ds(b, n), :, self.cols]
-
-    def copy(self, src, slot, n, r, s, peer):
-        return remote(src, self.land.at[pl.ds(slot, n)], self.send.at[s], self.recv.at[r], peer)
-
-    def arrive(self, slot, n, r):
-        self.copy(self.land.at[pl.ds(slot, n)], slot, n, r, 0, self.xn).wait_recv()
-
-    def add(self, b, *slots):
-        total = self.grad[b, :, self.cols].astype(F32)
-        for slot in slots:
-            total = total + self.land[slot].astype(F32)
-        self.grad[b, :, self.cols] = total.astype(BF16)
+        self.home, self.away = c == y, c != y
+
+    def rows(self, b):
+        return self.grad.at[pl.ds(b, 1), :, self.cols]
+
+    def slot(self, i):
+        return self.land.at[pl.ds(i, 1)]
+
+    def push(self, src, slot, s, peer):
+        return remote(src, self.slot(slot), self.send.at[s], self.recv.at[slot], peer)
+
+    def came(self, slot):
+        self.push(self.slot(slot), slot, 0, self.sib).wait_recv()
+
+    def value(self, i):
+        return self.land[i].astype(F32)
 
     def first(self):
         d, z, x, c, y = self.pos
 
-        def over_y(column, sem):
-            def step(k, _):
-                zz = lax.rem(z + 1 + k, 4)
-                q = zz * 2 + column
-                self.copy(self.rows(2 * q), q, 1, q, sem + k, self.yn).start()
-                return 0
-
-            lax.fori_loop(0, 4, step, 0)
-
-        def over_x(k, _):
-            zz = lax.rem(z + 1 + k, 4)
-            b = zz * 4 + (1 - x) * 2 + 1
-            self.copy(self.rows(b), 8 + zz, 1, 8 + zz, 8 + k, self.xn).start()
-            return 0
-
         @pl.when(self.away)
         def _():
-            over_y(1 - x, 0)
-
-        lax.fori_loop(0, 4, over_x, 0)
-
-        @pl.when(self.away)
-        def _():
-            over_y(x, 4)
+            for column, base in ((1 - x, 0), (x, 4)):
+
+                def step(k, _):
+                    q = lax.rem(z + 1 + k, 4) * 2 + column
+                    self.push(self.rows(2 * q + c), q, base + k, self.yn).start()
+                    self.push(self.rows(2 * q + 1 - c), 15 + q, 8 + base + k, self.sib).start()
+                    return 0
+
+                lax.fori_loop(0, 4, step, 0)
+
+        @pl.when(self.home)
+        def _():
+            for column, base in ((1 - x, 0), (x, 4)):
+
+                def step(k, _):
+                    q = lax.rem(z + 1 + k, 4) * 2 + column
+                    self.push(self.rows(2 * q + 1 - c), q, base + k, self.sib).start()
+                    return 0
+
+                lax.fori_loop(0, 4, step, 0)
 
     def second(self):
         d, z, x, c, y = self.pos
 
-        @pl.when(self.home)
+        @pl.when(self.away)
         def _():
             def step(k, _):
                 zz = lax.rem(z + 1 + k, 4)
                 q = zz * 2 + 1 - x
-                self.arrive(q, 1, q)
-                self.add(2 * q, q)
-                self.copy(self.rows(2 * q), 12 + zz, 1, 12 + zz, k, self.xn).start()
+                self.came(q)
+                self.push(self.slot(q), 8 + zz, 16 + k, self.xn).start()
                 return 0
 
             lax.fori_loop(0, 4, step, 0)
 
-        def step(k, _):
-            zz = lax.rem(z + 1 + k, 4)
-            q = zz * 2 + x
-            self.arrive(8 + zz, 1, 8 + zz)
-            self.add(2 * q + 1, 8 + zz)
-
-            @pl.when(self.away)
-            def _():
-                self.copy(self.rows(2 * q + 1), 16 + zz, 1, 16 + zz, 12 + k, self.yn).start()
-
-            return 0
-
-        lax.fori_loop(0, 4, step, 0)
+        @pl.when(self.home)
+        def _():
+            def over_x(k, _):
+                zz = lax.rem(z + 1 + k, 4)
+                q = zz * 2 + 1 - x
+                self.came(15 + q)
+                self.push(self.slot(15 + q), 23 + zz, 15 + k, self.xn).start()
+                return 0
+
+            lax.fori_loop(0, 4, over_x, 0)
+
+            def step(k, _):
+                zz = lax.rem(z + 1 + k, 4)
+                q = zz * 2 + 1 - x
+                b = 2 * q + c
+                self.came(q)
+                total = self.grad[b, :, self.cols].astype(F32) + self.value(q)
+                self.grad[b, :, self.cols] = total.astype(BF16)
+                self.push(self.rows(b), 8 + zz, 8 + k, self.xn).start()
+                return 0
+
+            lax.fori_loop(0, 4, step, 0)
 
     def third(self):
         d, z, x, c, y = self.pos
 
         @pl.when(self.home)
         def _():
+            def far(k, _):
+                zz = lax.rem(z + 1 + k, 4)
+                q = zz * 2 + x
+                self.came(15 + q)
+                self.came(23 + zz)
+                self.land[15 + q] = (self.value(15 + q) + self.value(23 + zz)).astype(BF16)
+                self.push(self.slot(15 + q), 15 + zz, 19 + k, self.yn).start()
+                return 0
+
+            lax.fori_loop(0, 4, far, 0)
+
             def step(k, _):
                 zz = lax.rem(z + 1 + k, 4)
                 q = zz * 2 + x
-                self.arrive(q, 1, q)
-                self.arrive(12 + zz, 1, 12 + zz)
-                self.add(2 * q, q, 12 + zz)
-                self.arrive(16 + zz, 1, 16 + zz)
-                self.add(2 * q + 1, 16 + zz)
-                peer = (zz * 4 + x * 2 + c, y)
-                self.copy(self.rows(2 * q, 2), 20 + 2 * k, 2, 20 + k, 4 + k, peer).start()
+                b = 2 * q + c
+                self.came(q)
+                self.came(8 + zz)
+                total = self.grad[b, :, self.cols].astype(F32)
+                total = total + self.value(q) + self.value(8 + zz)
+                self.grad[b, :, self.cols] = total.astype(BF16)
+                self.push(self.rows(b), 12 + k, 12 + k, (zz * 4 + x * 2 + c, y)).start()
                 return 0
 
             lax.fori_loop(0, 3, step, 0)
-
-    def hand_over(self):
-        return remote(
-            self.spare, self.out.at[:, self.cols], self.send.at[16], self.recv.at[23], self.sib
-        )
 
     def fourth(self):
         d, z, x, c, y = self.pos
 
+        @pl.when(self.away)
+        def _():
+            def step(k, _):
+                zz = lax.rem(z + 1 + k, 4)
+                q = zz * 2 + x
+                self.came(q)
+                self.came(8 + zz)
+                self.came(15 + zz)
+                total = self.value(q) + self.value(8 + zz) + self.value(15 + zz)
+                self.land[q] = total.astype(BF16)
+                self.push(self.slot(q), 12 + k, 20 + k, (zz * 4 + x * 2 + c, y)).start()
+                return 0
+
+            lax.fori_loop(0, 3, step, 0)
+
+    def fifth(self):
+        d, z, x, c, y = self.pos
+        q = z * 2 + x
+        self.came(q)
+        self.came(8 + z)
+        for k in range(3):
+            self.came(12 + k)
+        total = self.value(q) + self.value(8 + z)
+        total = total + self.value(12) + self.value(13) + self.value(14)
+
         @pl.when(self.home)
         def _():
-            q = z * 2 + x
-            self.arrive(q, 1, q)
-            self.arrive(12 + z, 1, 12 + z)
-            self.arrive(16 + z, 1, 16 + z)
-            for k in range(3):
-                self.arrive(20 + 2 * k, 2, 20 + k)
-            low = self.grad[2 * q, :, self.cols].astype(F32)
-            for slot in (q, 12 + z, 20, 22, 24):
-                low = low + self.land[slot].astype(F32)
-            high = self.grad[2 * q + 1, :, self.cols].astype(F32)
-            for slot in (16 + z, 21, 23, 25):
-                high = high + self.land[slot].astype(F32)
-
-            @pl.when(c == 0)
-            def _():
-                self.out[:, self.cols] = low
-                self.spare[...] = high
-
-            @pl.when(c == 1)
-            def _():
-                self.out[:, self.cols] = high
-                self.spare[...] = low
-
-            self.hand_over().start()
+            self.out[:, self.cols] = total + self.grad[d, :, self.cols].astype(F32)
+
+        @pl.when(self.away)
+        def _():
+            self.came(15 + z)
+            self.out[:, self.cols] = total + self.value(15 + z)
 
     def finish(self):
-        one, two = self.rows(0), self.rows(0, 2)
-
-        @pl.when(self.home)
-        def _():
-            for k in range(4):
-                self.copy(one, 0, 1, 0, k, self.xn).wait_send()
-            for k in range(3):
-                self.copy(two, 0, 2, 0, 4 + k, self.xn).wait_send()
-            self.hand_over().wait_send()
-
-        @pl.when(self.away)
-        def _():
-            for k in range(8):
-                self.copy(one, 0, 1, 0, k, self.yn).wait_send()
-            for k in range(4):
-                self.copy(one, 0, 1, 0, 12 + k, self.yn).wait_send()
-            self.hand_over().wait_recv()
-
-        for k in range(4):
-            self.copy(one, 0, 1, 0, 8 + k, self.xn).wait_send()
+        block = self.slot(0)
+        for s in range(REDUCE_SEND):
+            self.push(block, 0, s, self.sib).wait_send()
 
 
 def reduce_events(parts):
     n = len(parts)
+    stages = (Reduce.first, Reduce.second, Reduce.third, Reduce.fourth, Reduce.fifth)
     events = [parts[0].first]
-    for i in range(n + 2):
+    for i in range(n + 3):
         if i + 1 < n:
             events.append(parts[i + 1].first)
-        if i < n:
-            events.append(parts[i].second)
-        if 0 <= i - 1 < n:
-            events.append(parts[i - 1].third)
-        if 0 <= i - 2 < n:
-            events.append(parts[i - 2].fourth)
+        for lag, stage in enumerate(stages[1:]):
+            if 0 <= i - lag < n:
+                events.append(functools.partial(stage, parts[i - lag]))
     return events + [p.finish for p in parts]
 
 
 def reduce_kernel(chunks, count, *refs):
     n = len(chunks)
     grads, outs = refs[:count], refs[count : 2 * count]
-    lands, spares = refs[2 * count : 2 * count + n], refs[2 * count + n : 2 * count + 2 * n]
-    recv, send = refs[2 * count + 2 * n :]
+    lands, (recv, send) = refs[2 * count : 2 * count + n], refs[2 * count + n :]
     pos = place()
     greet(chip_peers(pos))
     parts = [
-        Reduce(grads[g], lands[i], spares[i], outs[g], recv.at[i], send.at[i], pos, cols)
+        Reduce(grads[g], lands[i], outs[g], recv.at[i], send.at[i], pos, cols)
         for i, (g, cols) in enumerate(chunks)
     ]
     for event in reduce_events(parts):
@@ -682,11 +708,10 @@
 
 def reduce_scratch(chunks):
     n = len(chunks)
-    return (
-        [pltpu.VMEM((26, 72, cols[1]), BF16) for _, cols in chunks]
-        + [pltpu.VMEM((72, cols[1]), F32) for _, cols in chunks]
-        + [pltpu.SemaphoreType.DMA((n, REDUCE_RECV)), pltpu.SemaphoreType.DMA((n, REDUCE_SEND))]
-    )
+    return [pltpu.VMEM((27, 72, cols[1]), BF16) for _, cols in chunks] + [
+        pltpu.SemaphoreType.DMA((n, REDUCE_RECV)),
+        pltpu.SemaphoreType.DMA((n, REDUCE_SEND)),
+    ]
 
 
 def reduce_grads(grads, chunks, collective_id):

time: 719 us -> 698 us (0.971)
  Pallas kernels: 406 us -> 385 us
    pallas_call x2, Pallas kernels: 177 us -> 164 us  [gather_weights(): pl.pallas_call(functools.partial(gather_kernel, chunks, count), out_shape...]
  transfers between devices with their start and end apart: 12 -> 12, of which waited for: 1 -> 1; matrix products, arithmetic and copies ran while one was open for 26% -> 27% of each run, Pallas kernels for 57% -> 56%
where the time goes in v2:
time: 698 us; the launch traced here: 693 us
  Pallas kernels  385 us (55%)
  matrix products  180 us (26%)
  other arithmetic  66.2 us (9%)
  local copies, waits for them, and re-layouts  31.4 us (4%)
  starting transfers between devices  17.2 us (2%)
  waiting for transfers between devices  11 us (2%)
    pallas_call x2, Pallas kernels, reduce_grads(): pl.pallas_call(functools.partial(reduce_kernel, chunks, count), out_shape...  175 us
    pallas_call x2, Pallas kernels, gather_weights(): pl.pallas_call(functools.partial(gather_kernel, chunks, count), out_shape...  164 us
    pallas_call x1, Pallas kernels, mod_backward(): pl.pallas_call(mod_backward_kernel, out_shape=[jax.ShapeDtypeStruct((72,...  30.5 us
    convert_element_type x2, other arithmetic, attend_backward(): score_grad = (probs * (prob_grad - inner)).astype(jnp.bfloat16)  26.5 us
    dot_general x2, matrix products, attend_backward(): jnp.einsum('qhe,khe->hqk', grad_block, values_all, preferred_element_type...  26.2 us
    pallas_call x1, Pallas kernels, mod_forward(): pl.pallas_call(mod_forward_kernel, out_shape=[jax.ShapeDtypeStruct((1, n)...  15.7 us
    ppermute x4, starting transfers between devices, trade(): moved = lax.ppermute(value, AXES, latent_pairs())  15.6 us
    dot_general x1, matrix products, on_device_chip(): act_grad = jnp.dot(grad_m, w_fc2, preferred_element_type=F32)  15.3 us
  transfers between devices with their start and end apart: 12, of which 1 were waited for; matrix products, arithmetic and copies ran while one was open for 27% of the time, Pallas kernels for 56%

profile of v2, /device:TPU:1, one launch (start us, length us, event | category | flops | bytes accessed | tf_op | source)
XLA Modules:
  0.0 692.6 jit_solution(5394394754231343214)
XLA Ops:
  2.3 2.4 pad_maximum_fusion.14
  4.7 4.5 collective-permute-start
  10.1 15.7 %shard_map.228 = (f32[1,6912]{1,0:T(1,128)S(1)}, bf16[16,8,128]{2,1,0:T(8,128)(2,1)S(1)}) custom-call(bf16[16,8,128]{2,1,0:T(8,128)(2,1)S(1)} %pad.4.piece_ref, bf16[72,6912]{1,0:T(8,128)(2,1)S(1)} %copy-done, f32[1,6912]{1,0:T(1,128)S(1)} %reshape.265.bias_ref), custom_call_target="tpu_custom_call" | custom-call | tf_op jit(solution)/shard_map/pallas_call | solution.py:794
  30.0 42.8 %shard_map.229 = (bf16[16,72,1728]{2,1,0:T(8,128)(2,1)}, bf16[8,72,1728]{2,1,0:T(8,128)(2,1)}) custom-call(bf16[1,72,1728]{2,1,0:T(8,128)(2,1)} %reshape.239.refs_0_), custom_call_target="tpu_custom_call" | custom-call | tf_op jit(solution)/shard_map/pallas_call | solution.py:507
  72.7 121.2 %shard_map.230 = (bf16[16,72,576]{2,1,0:T(8,128)(2,1)}, bf16[16,72,2304]{2,1,0:T(8,128)(2,1)}, bf16[16,72,2304]{2,1,0:T(8,128)(2,1)}, bf16[8,72,576]{2,1,0:T(8,1...) custom-call(bf16[1,72,576]{2,1,0:T(8,128)(2,1)} %bitcast.136, bf16[1,72,2304]{2,1,0:T(8,128)(2,1)} %bitcast.133, ...), custom_call_target="tpu_custom_call" | custom-call | tf_op jit(solution)/shard_map/pallas_call | solution.py:507
  194.2 7.4 %add_convert_fusion = bf16[1024,1728]{0,1:T(8,128)(2,1)S(1)} fusion(bf16[1152,1728]{1,0:T(8,128)(2,1)} %bitcast.145, f32[1728]{0:T(1024)S(1)} %convert_element_type.147, bf16[512,1152]{1,0:T(8,128)(2,1)} %collective-permute-done.1, bf16[512,1152]{1,0:T(8,128)(2,1)S(1)} %fusion.28), kind=kOutput, calls=%fused_computation.40 | convolution fusion | flops 4085121024 | bytes 9886464 | tf_op jit(solution)/shard_map/dot_general | solution.py:1052
  201.6 2.5 multiply_reduce_fusion.2
  204.1 8.8 %multiply_reduce_fusion.3 = (f32[8,512]{1,0:T(8,128)S(1)}, f32[8,512,1024]{2,1,0:T(8,128)}) fusion(bf16[1024,3,8,72]{0,3,2,1:T(8,128)(2,1)S(1)} %bitcast.106), kind=kOutput, calls=%fused_computation.13 | convolution fusion | flops 612364288 | bytes 18563072 | tf_op jit(solution)/shard_map/qhe,khe->hqk/dot_general | solution.py:40
  212.9 3.7 fusion.1
  216.6 4.7 fusion.42
  221.4 8.0 %fusion = f32[8,512]{1,0:T(8,128)S(1)} fusion(f32[8,512,1024]{2,1,0:T(8,128)} %get-tuple-element.110, f32[8,512]{1,0:T(8,128)S(1)} %get-tuple-element.109), kind=kLoop, calls=%fused_computation.10 | loop fusion | flops 12578816 | bytes 16809984 | tf_op jit(solution)/shard_map/reduce_sum | solution.py:45
  229.4 2.7 copy-done.3
  232.2 4.7 fusion.43
  236.9 2.2 fusion.44
  239.8 4.3 collective-permute-start.6
  247.1 10.9 %collective-permute-done.6 = bf16[512,1152]{1,0:T(8,128)(2,1)S(1)} collective-permute-done((bf16[512,1152]{1,0:T(8,128)(2,1)S(1)}, bf16[512,1152]{1,0:T(8,128)(2,1)S(1)}, u32[]{:S(2)}, u32[]{:S(2)}) %collective-permute-start.6) | collective-permute-done | bytes 1179680 | tf_op jit(solution)/shard_map/ppermute | solution.py:983
  258.0 1.9 convert_reduce_fusion.4
  260.0 12.2 %fusion.39 = f32[1024,2304]{1,0:T(8,128)} fusion(bf16[1152,2304]{1,0:T(8,128)(2,1)} %bitcast.137, bf16[512,1152]{1,0:T(8,128)(2,1)} %collective-permute-done.3, bf16[512,1152]{1,0:T(8,128)(2,1)} %add_convert_fusion.3), kind=kOutput, calls=%fused_computation.92 | convolution fusion | flops 5440536576 | bytes 17104896 | tf_op jit(solution)/shard_map/dot_general | solution.py:1062
  272.2 12.6 %fusion.69 = f32[1024,1152]{1,0:T(8,128)S(1)} fusion(bf16[1152,2304]{1,0:T(8,128)(2,1)} %bitcast.141, f32[1024,2304]{1,0:T(8,128)} %fusion.39, f32[2304]{0:T(1024)S(1)} %reshape.266), kind=kOutput, calls=%fused_computation.167 | convolution fusion | flops 5459410944 | bytes 19473408 | tf_op jit(solution)/shard_map/rf,df->rd/dot_general | solution.py:1066
  284.8 15.3 %convert_reduce_fusion = (f32[2304]{0:T(1024)S(1)}, bf16[1024,2304]{1,0:T(8,128)(2,1)S(1)}) fusion(f32[1024,2304]{1,0:T(8,128)} %fusion.39, f32[2304]{0:T(1024)S(1)} %reshape.266, bf16[1152,2304]{1,0:T(8,128)(2,1)S(1)} %bitcast.144, bf16[512,1152]{1,0:T(8,128)(2,1)} %collective-permute-done.7, bf16[512,1152]{1,0:T(8,128)(2,1)} %get-tuple-element.86), kind=kOutput, calls=%fused_computation.27 | convolution fusion | flops 5494798336 | bytes 21841920 | tf_op jit(solution)/shard_map/dot_general | solution.py:1075
  300.2 6.3 fusion.77
  307.4 11.8 %convolution_convert_fusion.1 = bf16[1152,2304]{1,0:T(8,128)(2,1)} fusion(bf16[512,1152]{1,0:T(8,128)(2,1)} %collective-permute-done.7, bf16[512,1152]{1,0:T(8,128)(2,1)} %get-tuple-element.86, f32[1024,2304]{1,0:T(8,128)} %fusion.39, f32[2304]{0:T(1024)S(1)} %reshape.266), kind=kOutput, calls=%fused_computation.17 | convolution fusion | flops 5466783744 | bytes 17114112 | tf_op jit(solution)/shard_map/rd,rf->df/dot_general | solution.py:1074
  321.9 2.6 fusion.33
  324.9 9.6 %convolution_convert_fusion = bf16[1152,2304]{1,0:T(8,128)(2,1)} fusion(bf16[1024,2304]{1,0:T(8,128)(2,1)S(1)} %get-tuple-element.116, bf16[512,1152]{1,0:T(8,128)(2,1)} %collective-permute-done.3, bf16[512,1152]{1,0:T(8,128)(2,1)} %add_convert_fusion.3), kind=kOutput, calls=%fused_computation.16 | convolution fusion | flops 5443190784 | bytes 12386304 | tf_op jit(solution)/shard_map/rd,rf->df/dot_general | solution.py:1078
  334.5 3.7 collective-permute-start.5
  338.2 1.8 convolution_convert_fusion.4
  340.9 11.5 %multiply_reduce_fusion.1 = (f32[8,512]{1,0:T(8,128)S(1)}, f32[8,512,1024]{2,1,0:T(8,128)}) fusion(f32[8,512,1024]{2,1,0:T(8,128)} %get-tuple-element.110, f32[8,512]{1,0:T(8,128)S(1)} %log_add_fusion.1, bf16[512,8,72]{0,2,1:T(8,128)(2,1)S(1)} %bitcast.123, bf16[1024,3,8,72]{0,3,2,1:T(8,128)(2,1)S(1)} %bitcast.112), kind=kOutput, calls=%fused_computation.4 | convolution fusion | flops 620752896 | bytes 35356672 | tf_op jit(solution)/shard_map/qhe,khe->hqk/dot_general | solution.py:75
  352.4 16.0 %multiply_convert_fusion.1 = bf16[8,512,1024]{2,1,0:T(8,128)(2,1)} fusion(f32[8,512,1024]{2,1,0:T(8,128)} %get-tuple-element.112, f32[8,512,1024]{2,1,0:T(8,128)} %get-tuple-element.110, f32[8,512]{1,0:T(8,128)S(1)} %get-tuple-element.111, f32[8,512]{1,0:T(8,128)S(1)} %log_add_fusion.1), kind=kLoop, calls=%fused_computation.3 | loop fusion | flops 20971520 | bytes 41975808 | tf_op jit(solution)/shard_map/convert_element_type | solution.py:79
  368.4 7.2 %fusion.40 = bf16[512,8,72]{0,2,1:T(8,128)(2,1)} fusion(bf16[8,512,1024]{2,1,0:T(8,128)(2,1)} %multiply_convert_fusion.1, bf16[1024,3,8,72]{0,3,2,1:T(8,128)(2,1)S(1)} %bitcast.113), kind=kOutput, calls=%fused_computation.95 | convolution fusion | flops 604569600 | bytes 10158080 | tf_op jit(solution)/shard_map/hqk,khe->qhe/dot_general | solution.py:81
  375.6 5.0 fusion.49
  380.6 4.6 fusion.11
  385.3 14.7 %multiply_reduce_fusion = (f32[8,512]{1,0:T(8,128)S(1)}, f32[8,512,1024]{2,1,0:T(8,128)}) fusion(f32[8,512,1024]{2,1,0:T(8,128)} %copy-done.2, f32[8,512]{1,0:T(8,128)S(1)} %log_add_fusion, bf16[512,8,72]{0,2,1:T(8,128)(2,1)} %bitcast.126, bf16[1024,3,8,72]{0,3,2,1:T(8,128)(2,1)} %bitcast.109), kind=kOutput, calls=%fused_computation.1 | convolution fusion | flops 620752896 | bytes 35356672 | tf_op jit(solution)/shard_map/qhe,khe->hqk/dot_general | solution.py:75
  400.0 10.3 %add_bitcast_fusion = bf16[1024,1,8,72]{0,3,2,1:T(8,128)(2,1)} fusion(f32[8,72,1024]{2,1,0:T(8,128)S(1)} %fusion.11, bf16[512,8,72]{0,2,1:T(8,128)(2,1)} %bitcast.124, f32[8,512,1024]{2,1,0:T(8,128)} %get-tuple-element.110, f32[8,512]{1,0:T(8,128)S(1)} %log_add_fusion.1), kind=kOutput, calls=%fused_computation.84 | convolution fusion | flops 617742336 | bytes 20922368 | tf_op jit(solution)/shard_map/hqk,qhe->khe/dot_general | solution.py:91
  410.3 10.5 %multiply_convert_fusion = bf16[8,512,1024]{2,1,0:T(8,128)(2,1)} fusion(f32[8,512,1024]{2,1,0:T(8,128)} %get-tuple-element.114, f32[8,512,1024]{2,1,0:T(8,128)S(1)} %bitcast.104, f32[8,512]{1,0:T(8,128)S(1)} %get-tuple-element.113, f32[8,512]{1,0:T(8,128)S(1)} %log_add_fusion), kind=kLoop, calls=%fused_computation | loop fusion | flops 20971520 | bytes 41975808 | tf_op jit(solution)/shard_map/convert_element_type | solution.py:79
  420.8 6.6 fusion.41
  427.4 2.8 multiply_bitcast_fusion
  432.3 2.5 copy-done.45
  434.7 6.6 fusion.78
  444.8 124.7 %shard_map.233 = (f32[72,2304]{1,0:T(8,128)}, f32[72,2304]{1,0:T(8,128)}, f32[72,576]{1,0:T(8,128)}) custom-call(bf16[16,72,2304]{2,1,0:T(8,128)(2,1)} %bitcast.121, bf16[16,72,2304]{2,1,0:T(8,128)(2,1)} %bitcast.122, bf16[16,72,576]{2,1,0:T(8,128)(2,1)} %bitcast.120), custom_call_target="tpu_custom_call" | custom-call | tf_op jit(solution)/shard_map/pallas_call | solution.py:720
  569.7 2.9 slice.258
  572.6 9.0 %convolution_convert_fusion.2 = bf16[1152,1728]{0,1:T(8,128)(2,1)} fusion(bf16[1024,1728]{0,1:T(8,128)(2,1)} %bitcast.130, bf16[512,1152]{1,0:T(8,128)(2,1)} %collective-permute-done.1, bf16[512,1152]{1,0:T(8,128)(2,1)S(1)} %copy-done.26), kind=kOutput, calls=%fused_computation.37 | convolution fusion | flops 4083572736 | bytes 9879552 | tf_op jit(solution)/shard_map/rd,rc->dc/dot_general | solution.py:1096
  581.6 6.4 copy.32
  588.1 50.1 %shard_map.232 = f32[72,1728]{1,0:T(8,128)} custom-call(bf16[16,72,1728]{2,1,0:T(8,128)(2,1)} %bitcast.115), custom_call_target="tpu_custom_call" | custom-call | tf_op jit(solution)/shard_map/pallas_call | solution.py:720
  640.5 2.6 select_bitcast_fusion.1
  643.1 2.7 fusion.29
  649.4 3.1 collective-permute-start.11
  652.6 30.5 %shard_map.231 = (f32[72,6912]{1,0:T(8,128)S(1)}, f32[1,6912]{1,0:T(1,128)S(1)}, f32[16,8,128]{2,1,0:T(8,128)S(1)}, f32[1,2304]{1,0:T(1,128)S(1)}, f32[1,3456]{1,0:T(1,128)S(1)}) custom-call(f32[1,6912]{1,0:T(1,128)S(1)} %constant_dynamic-update-slice_fusion.v1_ref, f32[1,2304]{1,0:T(1,128)S(1)} %broadcast_in_dim.47.v2_ref, ...), custom_call_target="tpu_custom_call" | custom-call | tf_op jit(solution)/shard_map/pallas_call | solution.py:930
  686.4 2.4 select_bitcast_fusion
  (238 shorter events, 33.6 us)
Async XLA Ops:
  0.6 25.2 %copy-start.18 = (bf16[512,1,1152]{2,0,1:T(8,128)(2,1)S(1)}, bf16[512,1,1152]{2,0,1:T(8,128)(2,1)}, u32[]{:S(2)}) copy-start(bf16[512,1,1152]{2,0,1:T(8,128)(2,1)} %param.13) | copy-start | bytes 3538948
  0.7 8.6 %copy-start.39 = (bf16[1,1152]{1,0:T(2,128)(2,1)S(1)}, bf16[1,1152]{1,0:T(2,128)(2,1)}, u32[]{:S(2)}) copy-start(bf16[1,1152]{1,0:T(2,128)(2,1)} %param.14) | copy-start | bytes 6916
  0.7 9.3 %copy-start.42 = (bf16[6912]{0:T(1024)(128)(2,1)S(1)}, bf16[6912]{0:T(1024)(128)(2,1)}, u32[]{:S(2)}) copy-start(bf16[6912]{0:T(1024)(128)(2,1)} %param.16) | copy-start | bytes 41476
  0.7 9.4 %copy-start = (bf16[72,6912]{1,0:T(8,128)(2,1)S(1)}, bf16[72,6912]{1,0:T(8,128)(2,1)}, u32[]{:S(2)}) copy-start(bf16[72,6912]{1,0:T(8,128)(2,1)} %w_ref.3) | copy-start | bytes 2985988
  4.7 21.2 %collective-permute-start = (bf16[515,1152]{1,0:T(8,128)(2,1)}, bf16[515,1152]{1,0:T(8,128)(2,1)}, u32[]{:S(2)}, u32[]{:S(2)}) collective-permute-start(bf16[515,1152]{1,0:T(8,128)(2,1)} %pad_maximum_fusion.14), channel_id=1, source_target_pairs={{1,2},{2,1},{5,6},{6,5},{9,10},{10,9},{13,14},{14,13},{17,18},{18,... | collective-permute-start | bytes 3559688 | tf_op jit(solution)/shard_map/ppermute | solution.py:983
  27.5 166.5 %copy-start.5 = (bf16[515,1152]{1,0:T(8,128)(2,1)}, bf16[515,1152]{1,0:T(8,128)(2,1)S(1)}, u32[]{:S(2)}) copy-start(bf16[515,1152]{1,0:T(8,128)(2,1)S(1)} %broadcast_select_fusion) | copy-start | bytes 3559684
  28.8 172.8 %copy-start.25 = (bf16[512,1152]{1,0:T(8,128)(2,1)}, bf16[512,1152]{1,0:T(8,128)(2,1)S(1)}, u32[]{:S(2)}) copy-start(bf16[512,1152]{1,0:T(8,128)(2,1)S(1)} %fusion.28) | copy-start | bytes 3538948
  28.8 165.4 %collective-permute-start.1 = (bf16[512,1152]{1,0:T(8,128)(2,1)S(1)}, bf16[512,1152]{1,0:T(8,128)(2,1)}, u32[]{:S(2)}, u32[]{:S(2)}) collective-permute-start(bf16[512,1152]{1,0:T(8,128)(2,1)S(1)} %fusion.28), channel_id=1, source_target_pairs={{0,2},{1,3},{2,0},{3,1},{4,6},{5,7},{6,4},{7,5},{8,10},{9,11},{10,... | collective-permute-start | bytes 3538952 | tf_op jit(solution)/shard_map/ppermute | solution.py:989
  201.6 27.8 %copy-start.8 = (bf16[1024,1728]{0,1:T(8,128)(2,1)}, bf16[1024,1728]{0,1:T(8,128)(2,1)S(1)}, u32[]{:S(2)}) copy-start(bf16[1024,1728]{0,1:T(8,128)(2,1)S(1)} %add_convert_fusion) | copy-start | bytes 10616836
  204.1 12.5 %copy-start.2 = (f32[8,512,1024]{2,1,0:T(8,128)}, f32[8,512,1024]{2,1,0:T(8,128)S(1)}, u32[]{:S(2)}) copy-start(f32[8,512,1024]{2,1,0:T(8,128)S(1)} %get-tuple-element.108) | copy-start | bytes 50331652
  221.3 15.5 %copy-start.50 = (bf16[8,72,512]{2,1,0:T(8,128)(2,1)}, bf16[8,72,512]{2,1,0:T(8,128)(2,1)S(1)}, u32[]{:S(2)}) copy-start(bf16[8,72,512]{2,1,0:T(8,128)(2,1)S(1)} %fusion.42) | copy-start | bytes 1769476
  221.3 10.8 %copy-start.3 = (f32[8,512,1024]{2,1,0:T(8,128)S(1)}, f32[8,512,1024]{2,1,0:T(8,128)}, u32[]{:S(2)}) copy-start(f32[8,512,1024]{2,1,0:T(8,128)} %get-tuple-element.110) | copy-start | bytes 50331652
  239.3 4.9 collective-permute-start.2
  239.8 18.2 %collective-permute-start.6 = (bf16[512,1152]{1,0:T(8,128)(2,1)S(1)}, bf16[512,1152]{1,0:T(8,128)(2,1)S(1)}, u32[]{:S(2)}, u32[]{:S(2)}) collective-permute-start(bf16[512,1152]{1,0:T(8,128)(2,1)S(1)} %bitcast.131), channel_id=1, source_target_pairs={{1,2},{2,1},{5,6},{6,5},{9,10},{10,9},{13,14},{14,13},{17,18},{18,... | collective-permute-start | bytes 3538952 | tf_op jit(solution)/shard_map/ppermute | solution.py:983
  247.1 12.9 %collective-permute-start.3 = (bf16[512,1152]{1,0:T(8,128)(2,1)}, bf16[512,1152]{1,0:T(8,128)(2,1)}, u32[]{:S(2)}, u32[]{:S(2)}) collective-permute-start(bf16[512,1152]{1,0:T(8,128)(2,1)} %add_convert_fusion.3), channel_id=1, source_target_pairs={{0,2},{1,3},{2,0},{3,1},{4,6},{5,7},{6,4},{7,5},{8,10},{9,11},{10,... | collective-permute-start | bytes 3538952 | tf_op jit(solution)/shard_map/ppermute | solution.py:989
  259.9 24.9 %collective-permute-start.7 = (bf16[512,1152]{1,0:T(8,128)(2,1)}, bf16[512,1152]{1,0:T(8,128)(2,1)}, u32[]{:S(2)}, u32[]{:S(2)}) collective-permute-start(bf16[512,1152]{1,0:T(8,128)(2,1)} %get-tuple-element.86), channel_id=1, source_target_pairs={{0,2},{1,3},{2,0},{3,1},{4,6},{5,7},{6,4},{7,5},{8,10},{9,11},{10,... | collective-permute-start | bytes 3538952 | tf_op jit(solution)/shard_map/ppermute | solution.py:989
  260.0 24.8 %slice-start.14 = ((s8[5308416]{0:T(1024)(128)(4,1)}), s8[4194304]{0:T(1024)(128)(4,1)S(1)}, s32[]{:S(2)}) async-start(s8[5308416]{0:T(1024)(128)(4,1)} %bitcast.142), calls=%async_computation.14 | async-start | bytes 8388608
  272.2 12.6 %slice-start.15 = ((s8[5308416]{0:T(1024)(128)(4,1)}), s8[1114112]{0:T(1024)(128)(4,1)S(1)}, s32[]{:S(2)}) async-start(s8[5308416]{0:T(1024)(128)(4,1)} %bitcast.142), calls=%async_computation.15 | async-start | bytes 2228224
  272.2 28.0 %slice-start.12 = ((s8[5308416]{0:T(1024)(128)(4,1)}), s8[1114112]{0:T(1024)(128)(4,1)S(1)}, s32[]{:S(2)}) async-start(s8[5308416]{0:T(1024)(128)(4,1)} %bitcast.138), calls=%async_computation.12 | async-start | bytes 2228224
  284.8 15.4 %slice-start.13 = ((s8[5308416]{0:T(1024)(128)(4,1)}), s8[4194304]{0:T(1024)(128)(4,1)S(1)}, s32[]{:S(2)}) async-start(s8[5308416]{0:T(1024)(128)(4,1)} %bitcast.138), calls=%async_computation.13 | async-start | bytes 8388608
  306.4 14.8 %slice-start.10 = ((s8[4718592]{0:T(1024)(128)(4,1)}), s8[4194304]{0:T(1024)(128)(4,1)S(1)}, s32[]{:S(2)}) async-start(s8[4718592]{0:T(1024)(128)(4,1)} %bitcast.118), calls=%async_computation.10 | async-start | bytes 8388608
  306.7 14.5 %slice-start.11 = ((s8[4718592]{0:T(1024)(128)(4,1)}), s8[524288]{0:T(1024)(128)(4,1)S(1)}, s32[]{:S(2)}) async-start(s8[4718592]{0:T(1024)(128)(4,1)} %bitcast.118), calls=%async_computation.11 | async-start | bytes 1048576
  306.7 14.5 %collective-permute-start.4 = (bf16[512,1152]{1,0:T(8,128)(2,1)S(1)}, bf16[512,1152]{1,0:T(8,128)(2,1)S(1)}, u32[]{:S(2)}, u32[]{:S(2)}) collective-permute-start(bf16[512,1152]{1,0:T(8,128)(2,1)S(1)} %slice.260), channel_id=1, source_target_pairs={{0,2},{1,3},{2,0},{3,1},{4,6},{5,7},{6,4},{7,5},{8,10},{9,11},{10,... | collective-permute-start | bytes 3538952 | tf_op jit(solution)/shard_map/ppermute | solution.py:994
  307.3 11.9 %collective-permute-start.8 = (bf16[512,1152]{1,0:T(8,128)(2,1)S(1)}, bf16[512,1152]{1,0:T(8,128)(2,1)S(1)}, u32[]{:S(2)}, u32[]{:S(2)}) collective-permute-start(bf16[512,1152]{1,0:T(8,128)(2,1)S(1)} %slice.259), channel_id=1, source_target_pairs={{0,2},{1,3},{2,0},{3,1},{4,6},{5,7},{6,4},{7,5},{8,10},{9,11},{10,... | collective-permute-start | bytes 3538952 | tf_op jit(solution)/shard_map/ppermute | solution.py:994
  324.5 13.7 %copy-start.22 = (bf16[512,1152]{1,0:T(8,128)(2,1)}, bf16[512,1152]{1,0:T(8,128)(2,1)S(1)}, u32[]{:S(2)}) copy-start(bf16[512,1152]{1,0:T(8,128)(2,1)S(1)} %get-tuple-element.100) | copy-start | bytes 3538948
  324.5 13.7 %copy-start.47 = (bf16[16,72,576]{2,1,0:T(8,128)(2,1)S(1)}, bf16[16,72,576]{2,1,0:T(8,128)(2,1)}, u32[]{:S(2)}) copy-start(bf16[16,72,576]{2,1,0:T(8,128)(2,1)} %get-tuple-element.29) | copy-start | bytes 3981316
  324.5 13.7 %collective-permute-start.9 = (bf16[512,1152]{1,0:T(8,128)(2,1)S(1)}, bf16[512,1152]{1,0:T(8,128)(2,1)S(1)}, u32[]{:S(2)}, u32[]{:S(2)}) collective-permute-start(bf16[512,1152]{1,0:T(8,128)(2,1)S(1)} %get-tuple-element.100), channel_id=1, source_target_pairs={{0,2},{1,3},{2,0},{3,1},{4,6},{5,7},{6,4},{7,5},{8,10},{9,11},{10,... | collective-permute-start | bytes 3538952 | tf_op jit(solution)/shard_map/ppermute | solution.py:989
  334.5 306.0 %collective-permute-start.5 = (bf16[512,1152]{1,0:T(8,128)(2,1)}, bf16[512,1152]{1,0:T(8,128)(2,1)}, u32[]{:S(2)}, u32[]{:S(2)}) collective-permute-start(bf16[512,1152]{1,0:T(8,128)(2,1)} %get-tuple-element.98), channel_id=1, source_target_pairs={{1,2},{2,1},{5,6},{6,5},{9,10},{10,9},{13,14},{14,13},{17,18},{18,... | collective-permute-start | bytes 3538952 | tf_op jit(solution)/shard_map/ppermute | solution.py:983
  340.9 11.5 %copy-start.15 = (bf16[512,576]{0,1:T(8,128)(2,1)}, bf16[512,576]{0,1:T(8,128)(2,1)S(1)}, u32[]{:S(2)}) copy-start(bf16[512,576]{0,1:T(8,128)(2,1)S(1)} %get-tuple-element.101) | copy-start | bytes 1769476
  352.4 28.2 %slice-start = ((s8[16777216]{0:T(1024)(128)(4,1)}), s8[4194304]{0:T(1024)(128)(4,1)S(1)}, s32[]{:S(2)}) async-start(s8[16777216]{0:T(1024)(128)(4,1)} %bitcast.101), calls=%async_computation | async-start | bytes 8388608
  352.4 28.2 %slice-start.1 = ((s8[16777216]{0:T(1024)(128)(4,1)}), s8[4194304]{0:T(1024)(128)(4,1)S(1)}, s32[]{:S(2)}) async-start(s8[16777216]{0:T(1024)(128)(4,1)} %bitcast.101), calls=%async_computation.1 | async-start | bytes 8388608
  352.4 28.2 %slice-start.2 = ((s8[16777216]{0:T(1024)(128)(4,1)}), s8[4194304]{0:T(1024)(128)(4,1)S(1)}, s32[]{:S(2)}) async-start(s8[16777216]{0:T(1024)(128)(4,1)} %bitcast.101), calls=%async_computation.2 | async-start | bytes 8388608
  368.4 12.2 %slice-start.3 = ((s8[16777216]{0:T(1024)(128)(4,1)}), s8[4194304]{0:T(1024)(128)(4,1)S(1)}, s32[]{:S(2)}) async-start(s8[16777216]{0:T(1024)(128)(4,1)} %bitcast.101), calls=%async_computation.3 | async-start | bytes 8388608
  385.3 25.0 %slice-start.4 = ((s8[16777216]{0:T(1024)(128)(4,1)}), s8[4194304]{0:T(1024)(128)(4,1)S(1)}, s32[]{:S(2)}) async-start(s8[16777216]{0:T(1024)(128)(4,1)} %bitcast.103), calls=%async_computation.4 | async-start | bytes 8388608
  385.3 25.0 %slice-start.5 = ((s8[16777216]{0:T(1024)(128)(4,1)}), s8[4194304]{0:T(1024)(128)(4,1)S(1)}, s32[]{:S(2)}) async-start(s8[16777216]{0:T(1024)(128)(4,1)} %bitcast.103), calls=%async_computation.5 | async-start | bytes 8388608
  385.3 25.0 %slice-start.6 = ((s8[16777216]{0:T(1024)(128)(4,1)}), s8[4194304]{0:T(1024)(128)(4,1)S(1)}, s32[]{:S(2)}) async-start(s8[16777216]{0:T(1024)(128)(4,1)} %bitcast.103), calls=%async_computation.6 | async-start | bytes 8388608
  400.0 10.3 %slice-start.7 = ((s8[16777216]{0:T(1024)(128)(4,1)}), s8[4194304]{0:T(1024)(128)(4,1)S(1)}, s32[]{:S(2)}) async-start(s8[16777216]{0:T(1024)(128)(4,1)} %bitcast.103), calls=%async_computation.7 | async-start | bytes 8388608
  420.8 6.6 copy-start.4
  432.3 9.1 %copy-start.20 = (bf16[1024,3,8,72]{0,3,2,1:T(8,128)(2,1)}, bf16[1024,3,8,72]{0,3,2,1:T(8,128)(2,1)S(1)}, u32[]{:S(2)}) copy-start(bf16[1024,3,8,72]{0,3,2,1:T(8,128)(2,1)S(1)} %get-tuple-element.84) | copy-start | bytes 10616836
  434.7 6.7 copy-start.23
  434.7 6.7 copy-start.49
  434.7 6.7 copy-start.51
  434.7 6.7 copy-start.53
  572.6 70.5 %collective-permute-start.10 = (bf16[512,1152]{1,0:T(8,128)(2,1)}, bf16[512,1152]{1,0:T(8,128)(2,1)S(1)}, u32[]{:S(2)}, u32[]{:S(2)}) collective-permute-start(bf16[512,1152]{1,0:T(8,128)(2,1)} %slice.258), channel_id=1, source_target_pairs={{0,2},{1,3},{2,0},{3,1},{4,6},{5,7},{6,4},{7,5},{8,10},{9,11},{10,... | collective-permute-start | bytes 3538952 | tf_op jit(solution)/shard_map/ppermute | solution.py:994
  638.2 7.7 %slice-start.8 = ((s8[4718592]{0:T(1024)(128)(4,1)}), s8[524288]{0:T(1024)(128)(4,1)S(1)}, s32[]{:S(2)}) async-start(s8[4718592]{0:T(1024)(128)(4,1)} %bitcast.116), calls=%async_computation.8 | async-start | bytes 1048576
  647.9 37.9 %copy-start.40 = (bf16[1,1152]{1,0:T(2,128)(2,1)S(1)}, bf16[1,1152]{1,0:T(2,128)(2,1)}, u32[]{:S(2)}) copy-start(bf16[1,1152]{1,0:T(2,128)(2,1)} %param.14) | copy-start | bytes 6916
  647.9 37.9 %copy-start.41 = (f32[1,1152]{1,0:T(1,128)S(1)}, f32[1,1152]{1,0:T(1,128)}, u32[]{:S(2)}) copy-start(f32[1,1152]{1,0:T(1,128)} %get-tuple-element.97) | copy-start | bytes 13828
  649.4 37.0 %collective-permute-start.11 = (bf16[512,1152]{1,0:T(8,128)(2,1)}, bf16[512,1152]{1,0:T(8,128)(2,1)}, u32[]{:S(2)}, u32[]{:S(2)}) collective-permute-start(bf16[512,1152]{1,0:T(8,128)(2,1)} %add_convert_fusion.1), channel_id=1, source_target_pairs={{1,2},{2,1},{5,6},{6,5},{9,10},{10,9},{13,14},{14,13},{17,18},{18,... | collective-permute-start | bytes 3538952 | tf_op jit(solution)/shard_map/ppermute | solution.py:983
  (34 other events, 95.2 us)

commit v3 on v2

--- a/solution.py
+++ b/solution.py
@@ -436,39 +436,51 @@
             self.came(16 + q)
             self.move(block, block, 12 + k, 16 + q, self.xn).start()
 
-    def finish(self):
+    def ready(self):
         d, z, x, c, y = self.pos
-        block = self.part(self.full, 0)
+        for q in range(8):
+            self.came(8 + q)
 
         @pl.when(self.home)
         def _():
             self.stay().wait()
-            for q in range(8):
-                self.came(8 + q)
-            for s in list(range(1, 16)):
-                self.move(block, block, s, 0, self.sib).wait_send()
 
         @pl.when(self.away)
         def _():
-            for q in range(8):
-                self.came(8 + q)
             for k in range(4):
                 self.came(16 + ((z + k) % 4) * 2 + 1 - x)
-            for s in list(range(1, 24)):
+
+    def finish(self):
+        block = self.part(self.full, 0)
+        for s in range(1, 16):
+            self.move(block, block, s, 0, self.sib).wait_send()
+
+        @pl.when(self.away)
+        def _():
+            for s in range(16, 24):
                 self.move(block, block, s, 0, self.sib).wait_send()
 
-
-def gather_events(parts):
-    events = [p.start for p in parts]
-    for p in parts:
-        for k in (1, 2, 3):
-            events.append(functools.partial(p.from_z, k))
-    late = []
-    for p in parts:
+    def early(self):
+        return [functools.partial(self.from_z, k) for k in (1, 2, 3)]
+
+    def late(self):
+        steps = []
         for k in range(4):
-            late.append(functools.partial(p.from_x, k))
-            late.append(functools.partial(p.from_y, k))
-    return events + late + [p.finish for p in parts]
+            steps += [functools.partial(self.from_x, k), functools.partial(self.from_y, k)]
+        return steps + [self.ready]
+
+
+def gather_events(parts, lead=2):
+    n = len(parts)
+    events = [p.start for p in parts[:lead]]
+    for i in range(n + 1):
+        if i < n:
+            events += parts[i].early()
+        if i + lead < n:
+            events.append(parts[i + lead].start)
+        if i > 0:
+            events += parts[i - 1].late()
+    return events
 
 
 def gather_parts(shards, fulls, relays, chunks, recv, send, pos):
@@ -483,7 +495,8 @@
     recv, send = refs[3 * count :]
     pos = place()
     greet(chip_peers(pos))
-    for event in gather_events(gather_parts(shards, fulls, relays, chunks, recv, send, pos)):
+    parts = gather_parts(shards, fulls, relays, chunks, recv, send, pos)
+    for event in gather_events(parts) + [p.finish for p in parts]:
         event()
 
 
@@ -729,13 +742,39 @@
     )(*grads)
 
 
-def mod_forward_kernel(
-    piece_ref, w_ref, bias_ref, mod_ref, silu_ref, part, land, mine, other, s1, r1, s2, r2, s3
+class Pump:
+    def __init__(self, events):
+        self.events, self.next = list(events), 0
+
+    def run(self, count=None):
+        stop = len(self.events) if count is None else min(len(self.events), self.next + count)
+        for event in self.events[self.next : stop]:
+            event()
+        self.next = stop
+
+    def loop(self, steps, body, first=0, every=1, count=None):
+        todo = self.events[self.next :][: len(range(first, steps, every))]
+        todo = todo if count is None else todo[:count]
+        self.next += len(todo)
+
+        def step(i, _):
+            for j, event in enumerate(todo):
+                pl.when(i == first + j * every)(event)
+            body(i)
+            return 0
+
+        lax.fori_loop(0, steps, step, 0)
+
+
+def first_kernel(
+    chunks, piece_ref, w_ref, bias_ref, shard, mod_ref, silu_ref, full, relay,
+    part, land, mine, other, s1, r1, s2, r2, s3, recv, send,
 ):
     pos = place()
     d, z, x, c, y = pos
-    sib = neighbours(pos)[0]
-    greet([((d + k) % 16, y) for k in range(1, 16)])
+    sib, _, yn = neighbours(pos)
+    far = (z * 4 + x * 2 + 1 - c, 1 - y)
+    greet([((d + k) % 16, y) for k in range(1, 16)] + [yn, far])
 
     def piece(k):
         to = (d + k) % 16
@@ -747,6 +786,9 @@
 
     for k in range(1, 16):
         piece(k).start()
+    parts = gather_parts([shard], [full], [relay], chunks, recv, send, pos)
+    pump = Pump(gather_events(parts))
+    pump.run(2)
     silu_ref[d] = piece_ref[d]
     for k in range(1, 16):
         piece_in(k).wait_recv()
@@ -772,6 +814,7 @@
     for k in range(1, 8):
         send_part(k).start()
     land[me] = part[me]
+    pump.run(6)
     for k in range(1, 8):
         part_in(k).wait_recv()
     total = land[0]
@@ -780,22 +823,27 @@
     mine[...] = total
     swap = remote(mine, other, s3.at[0], s3.at[1], sib)
     swap.start()
+    pump.run(3)
     for k in range(1, 16):
         piece(k).wait_send()
     for k in range(1, 8):
         send_part(k).wait_send()
     swap.wait()
     mod_ref[...] = mine[...] + other[...] + bias_ref[...]
-
-
-def mod_forward(pieces, w_mod, bias, collective_id):
-    vmem = pl.BlockSpec(memory_space=pltpu.VMEM)
+    pump.run()
+    for p in parts:
+        p.finish()
+
+
+def first_stage(pieces, w_mod, bias, shard, chunks, collective_id):
+    vmem, anywhere = pl.BlockSpec(memory_space=pltpu.VMEM), pl.BlockSpec(memory_space=pl.ANY)
     n = w_mod.shape[1]
     return pl.pallas_call(
-        mod_forward_kernel,
-        out_shape=[jax.ShapeDtypeStruct((1, n), F32), jax.ShapeDtypeStruct((16, 8, 128), BF16)],
-        in_specs=[vmem] * 3,
-        out_specs=[vmem] * 2,
+        functools.partial(first_kernel, chunks),
+        out_shape=[jax.ShapeDtypeStruct((1, n), F32), jax.ShapeDtypeStruct((16, 8, 128), BF16)]
+        + gather_shapes([shard]),
+        in_specs=[vmem] * 3 + [anywhere],
+        out_specs=[vmem] * 2 + [anywhere] * 2,
         scratch_shapes=[
             pltpu.VMEM((8, 1, n), F32),
             pltpu.VMEM((8, 1, n), F32),
@@ -806,70 +854,153 @@
             pltpu.SemaphoreType.DMA((8,)),
             pltpu.SemaphoreType.DMA((8,)),
             pltpu.SemaphoreType.DMA((2,)),
-        ],
+        ]
+        + gather_sems(chunks),
         compiler_params=pltpu.CompilerParams(
             collective_id=collective_id, has_side_effects=True, vmem_limit_bytes=40 * 2**20
         ),
-    )(pieces, w_mod, bias)
-
-
-def mod_backward_kernel(
-    v1_ref, v2_ref, v3_ref, silu_ref, w_ref,
-    mwg_ref, mbg_ref, sg_ref, v2_out, v3_out,
-    v1_in, v2_in, mods, b2, b3, sgp, s0, s1, r1, s2, r2, s3, r3, s4, r4,
+    )(pieces, w_mod, bias, shard)[:3]
+
+
+def flat(value):
+    return value.reshape(-1, value.shape[-1])
+
+
+def product(a, b, ca, cb):
+    return lax.dot_general(a, b, (((ca,), (cb,)), ((), ())), preferred_element_type=F32)
+
+
+def last_kernel(
+    rows_ref, dqkv_ref, wqkv_ref, tokens_ref, resid_ref, scale_ref, parts_ref, wide_ref, half_ref,
+    silu_ref, w_ref,
+    tgrad_ref, qkv_out, mwg_ref, mbg_ref, sg_ref, wide_out, half_out,
+    grad, ngrad, sent, got, v1, v1_in, v2_in, mods, b2, b3, sgp, land0, land1, land2,
+    s0, s1, r1, s2, r2, s3, r3, s4, r4, recv, send,
 ):
     pos = place()
     d, z, x, c, y = pos
     sib = neighbours(pos)[0]
     lin = d * 2 + y
+    half, width = tokens_ref.shape
+    heads = dqkv_ref.shape[0] // 3
     greet([(((lin + k) % 32) // 2, (lin + k) % 2) for k in range(1, 32)])
     me = (z * 2 + x) * 2 + y
-    a = remote(v1_ref, v1_in, s0.at[0], s0.at[1], sib)
-    b = remote(v2_ref, v2_in, s0.at[2], s0.at[3], sib)
+
+    @pl.when(y == c)
+    def _():
+        b3[me] = half_ref[...]
+
+    sgp[...] = jnp.zeros_like(sgp)
+
+    def send3(q, core):
+        s = q * 2 + core
+        return remote(half_ref, b3.at[me], s3.at[s], r3.at[me], (s, c))
+
+    def each3(action):
+        for q in range(8):
+            for core in range(2):
+                pl.when(jnp.logical_or(d != q * 2 + core, y != c))(
+                    functools.partial(action, q, core)
+                )
+
+    n = dqkv_ref.shape[1] * heads
+    reducers = [
+        Reduce(grad.at[j], land, qkv_out.at[j], recv.at[j], send.at[j], pos, (0, n))
+        for j, land in enumerate((land0, land1, land2))
+    ]
+
+    def weight_grad(j, _):
+        value = product(rows_ref[...], flat(dqkv_ref[pl.ds(j * heads, heads)]), 0, 1)
+        grad[j] = value.reshape(grad.shape[1:]).astype(BF16)
+        for i, reducer in enumerate(reducers):
+            pl.when(j == i)(reducer.first)
+        pl.when(j == 2)(reducers[0].second)
+        return 0
+
+    lax.fori_loop(0, 3, weight_grad, 0)
+    each3(lambda q, core: send3(q, core).start())
+    pump = Pump(reduce_events(reducers)[:-3])
+    pump.events = [e for e in pump.events if e not in [r.first for r in reducers]][1:]
+
+    tile = half // 2
+    swap = remote(sent, got, s0.at[4], s0.at[5], sib)
+
+    def into_norm(i):
+        cols = pl.ds(pl.multiple_of(i * tile, tile), tile)
+        return product(flat(dqkv_ref[:, :, cols]), wqkv_ref[...], 0, 1)
+
+    def other_rows(i, _):
+        sent[pl.ds(pl.multiple_of(i * tile, tile), tile), :] = into_norm(i + 2).astype(BF16)
+        return 0
+
+    def own_rows(i, _):
+        ngrad[pl.ds(pl.multiple_of(i * tile, tile), tile), :] = into_norm(i)
+        return 0
+
+    lax.fori_loop(0, 2, other_rows, 0)
+    swap.start()
+    pump.run(1)
+    lax.fori_loop(0, 2, own_rows, 0)
+    swap.wait()
+    piece = half // 4
+    scale = 1.0 + scale_ref[...]
+
+    def norm_back(i, sums):
+        part = pl.ds(pl.multiple_of(i * piece, piece), piece)
+        value = tokens_ref[part, :].astype(F32)
+        center = value - jnp.mean(value, axis=-1, keepdims=True)
+        rate = lax.rsqrt(jnp.mean(center * center, axis=-1, keepdims=True) + 1e-06)
+        normed = center * rate
+        g = ngrad[part, :] + got[part, :].astype(F32)
+        e = g * scale
+        inner = jnp.mean(e * normed, axis=-1, keepdims=True)
+        back = rate * (e - jnp.mean(e, axis=-1, keepdims=True) - normed * inner)
+        tgrad_ref[part, :] = (resid_ref[part, :] + back).astype(BF16)
+        return (
+            sums[0] + jnp.sum(g, axis=0, keepdims=True),
+            sums[1] + jnp.sum(g * normed, axis=0, keepdims=True),
+        )
+
+    zero = jnp.zeros((1, width), F32)
+    shift_sum, scale_sum = lax.fori_loop(0, 4, norm_back, (zero, zero))
+    v1[:, :width] = shift_sum
+    v1[:, width : 2 * width] = scale_sum
+    v1[:, 2 * width :] = parts_ref[...]
+
+    a = remote(v1, v1_in, s0.at[0], s0.at[1], sib)
+    b = remote(wide_ref, v2_in, s0.at[2], s0.at[3], sib)
     a.start()
     b.start()
-
-    @pl.when(y == c)
-    def _():
-        b3[me] = v3_ref[...]
-
-    sgp[...] = jnp.zeros_like(sgp)
-
-    def send3(q, core):
-        s = q * 2 + core
-        return remote(v3_ref, b3.at[me], s3.at[s], r3.at[me], (s, c))
-
-    for q in range(8):
-        for core in range(2):
-
-            @pl.when(jnp.logical_or(d != q * 2 + core, y != c))
-            def _():
-                send3(q, core).start()
-
+    pump.run(1)
     a.wait()
     b.wait()
-    mods[me] = (v1_ref[...] + v1_in[...]).astype(BF16)
-    b2[me] = v2_ref[...] + v2_in[...]
+    mods[me] = (v1[...] + v1_in[...]).astype(BF16)
+    b2[me] = wide_ref[...] + v2_in[...]
 
     def chip(k):
         m = (me + k) % 16
         return m, ((m // 2) * 2 + c, m % 2)
 
+    def to_chip(buf, send, recv, k):
+        return remote(buf.at[me], buf.at[me], send.at[k], recv.at[me], chip(k)[1])
+
+    def from_chip(buf, send, recv, k):
+        m, peer = chip(k)
+        return remote(buf.at[m], buf.at[m], send.at[k], recv.at[m], peer)
+
+    both = ((mods, s1, r1), (b2, s2, r2))
     for k in range(1, 16):
-        m, peer = chip(k)
-        remote(mods.at[me], mods.at[me], s1.at[k], r1.at[me], peer).start()
-        remote(b2.at[me], b2.at[me], s2.at[k], r2.at[me], peer).start()
+        for buf in both:
+            to_chip(*buf, k).start()
+    pump.run(3)
     for k in range(1, 16):
-        m, peer = chip(k)
-        remote(mods.at[m], mods.at[m], s1.at[k], r1.at[m], peer).wait_recv()
+        from_chip(*both[0], k).wait_recv()
     every = jnp.concatenate([mods[i].astype(F32) for i in range(16)], axis=0)
     mbg_ref[...] = jnp.sum(every, axis=0, keepdims=True)
     every = every.astype(BF16)
-    grad = lax.dot_general(
-        every, w_ref[...], (((1,), (1,)), ((), ())), preferred_element_type=F32
-    )
+    back = product(every, w_ref[...], 1, 1)
     for i in range(16):
-        sgp[i, 0:1, :72] = grad[i : i + 1, :]
+        sgp[i, 0:1, :72] = back[i : i + 1, :]
 
     def send4(k):
         m = (d + k) % 16
@@ -878,80 +1009,321 @@
     for k in range(1, 16):
         send4(k).start()
     sg_ref[d] = sgp[d]
+    pump.run(2)
     owned = jnp.concatenate([silu_ref[i].astype(F32)[0:1, :] for i in range(16)], axis=0)
     owned = owned.astype(BF16)[:, :72]
-    width = w_ref.shape[1] // 6
     for j in range(6):
         cols = slice(j * width, (j + 1) * width)
-        mwg_ref[:, cols] = lax.dot_general(
-            owned, every[:, cols], (((0,), (0,)), ((), ())), preferred_element_type=F32
-        )
+        mwg_ref[:, cols] = product(owned, every[:, cols], 0, 0)
     for k in range(1, 16):
-        m, peer = chip(k)
-        remote(b2.at[m], b2.at[m], s2.at[k], r2.at[m], peer).wait_recv()
+        from_chip(*both[1], k).wait_recv()
     total = b2[0]
     for i in range(1, 16):
         total = total + b2[i]
-    v2_out[...] = total
-
-    def arrive3(i, guard):
-        @pl.when(guard)
-        def _():
-            remote(v3_ref, b3.at[i], s3.at[0], r3.at[i], sib).wait_recv()
+    wide_out[...] = total
+
+    def arrive3(i):
+        remote(half_ref, b3.at[i], s3.at[0], r3.at[i], sib).wait_recv()
 
     for i in range(16):
-        arrive3(i, jnp.logical_or(i != me, y != c))
+        pl.when(jnp.logical_or(i != me, y != c))(functools.partial(arrive3, i))
     total = b3[0]
     for i in range(1, 16):
         total = total + b3[i]
-    v3_out[...] = total
+    half_out[...] = total
     for k in range(1, 16):
         m = (d + k) % 16
         remote(sgp.at[m], sg_ref.at[m], s4.at[k], r4.at[m], (m, y)).wait_recv()
-    for q in range(8):
-        for core in range(2):
-
-            @pl.when(jnp.logical_or(d != q * 2 + core, y != c))
-            def _():
-                send3(q, core).wait_send()
-
+    pump.run()
+    for reducer in reducers:
+        reducer.finish()
+    each3(lambda q, core: send3(q, core).wait_send())
     for k in range(1, 16):
-        m, peer = chip(k)
-        remote(mods.at[me], mods.at[me], s1.at[k], r1.at[me], peer).wait_send()
-        remote(b2.at[me], b2.at[me], s2.at[k], r2.at[me], peer).wait_send()
+        for buf in both:
+            to_chip(*buf, k).wait_send()
         send4(k).wait_send()
 
 
-def mod_backward(v1, v2, v3, silu, w_mod, collective_id):
+def last_stage(rows, dqkv, w_qkv, tokens, resid, scale, parts, wide, halves, silu, w_mod, collective_id):
     vmem = pl.BlockSpec(memory_space=pltpu.VMEM)
     n = w_mod.shape[1]
-    n2, n3 = v2.shape[1], v3.shape[1]
+    n2, n3 = wide.shape[1], halves.shape[1]
+    half, width = tokens.shape
+    cols = dqkv.shape[0] * dqkv.shape[1] // 3
     dma = pltpu.SemaphoreType.DMA((16,))
+    shape = jax.ShapeDtypeStruct
     return pl.pallas_call(
-        mod_backward_kernel,
+        last_kernel,
         out_shape=[
-            jax.ShapeDtypeStruct((72, n), F32),
-            jax.ShapeDtypeStruct((1, n), F32),
-            jax.ShapeDtypeStruct((16, 8, 128), F32),
-            jax.ShapeDtypeStruct((1, n2), F32),
-            jax.ShapeDtypeStruct((1, n3), F32),
+            shape((half, width), BF16),
+            shape((3, 72, cols), F32),
+            shape((72, n), F32),
+            shape((1, n), F32),
+            shape((16, 8, 128), F32),
+            shape((1, n2), F32),
+            shape((1, n3), F32),
         ],
-        in_specs=[vmem] * 5,
-        out_specs=[vmem] * 5,
+        in_specs=[vmem] * 11,
+        out_specs=[vmem] * 7,
         scratch_shapes=[
+            pltpu.VMEM((3, 16, 72, cols), BF16),
+            pltpu.VMEM((half, width), F32),
+            pltpu.VMEM((half, width), BF16),
+            pltpu.VMEM((half, width), BF16),
+            pltpu.VMEM((1, n), F32),
             pltpu.VMEM((1, n), F32),
             pltpu.VMEM((1, n2), F32),
             pltpu.VMEM((16, 1, n), BF16),
             pltpu.VMEM((16, 1, n2), F32),
             pltpu.VMEM((16, 1, n3), F32),
             pltpu.VMEM((16, 8, 128), F32),
-            pltpu.SemaphoreType.DMA((4,)),
         ]
-        + [dma] * 8,
+        + [pltpu.VMEM((27, 72, cols), BF16)] * 3
+        + [pltpu.SemaphoreType.DMA((6,))]
+        + [dma] * 8
+        + [
+            pltpu.SemaphoreType.DMA((3, REDUCE_RECV)),
+            pltpu.SemaphoreType.DMA((3, REDUCE_SEND)),
+        ],
         compiler_params=pltpu.CompilerParams(
-            collective_id=collective_id, has_side_effects=True, vmem_limit_bytes=40 * 2**20
+            collective_id=collective_id, has_side_effects=True, vmem_limit_bytes=63000 * 1024
         ),
-    )(v1, v2, v3, silu, w_mod)
+    )(rows, dqkv, w_qkv, tokens, resid, scale, parts, wide, halves, silu, w_mod)
+
+
+LOG2E = math.log2(math.e)
+
+
+def attention_step(qkv, out, lse, block, scale):
+    heads, blocks = qkv.shape[0] // 3, qkv.shape[2] // block
+    factor = scale * LOG2E
+
+    def body(i):
+        h = i // blocks
+        cols = pl.ds(pl.multiple_of((i % blocks) * block, block), block)
+        scores = product(qkv[heads + h], qkv[h, :, cols], 0, 0)
+        top = jnp.max(scores, axis=0, keepdims=True)
+        probs = jnp.exp2((scores - top) * factor)
+        total = jnp.sum(probs, axis=0, keepdims=True)
+        mixed = product(qkv[2 * heads + h], probs.astype(BF16), 1, 0)
+        out[h, :, cols] = (mixed / total).astype(BF16)
+        lse[h, :, cols] = top * factor + jnp.log2(total)
+
+    return heads * blocks, body
+
+
+GELU = math.sqrt(2 / math.pi)
+
+
+def gelu_and_slope(v):
+    square = v * v
+    t = jnp.tanh(v * (GELU + GELU * 0.044715 * square))
+    half = 0.5 * (1.0 + t)
+    return v * half, half + 0.5 * v * (1.0 - t * t) * (GELU + GELU * 3 * 0.044715 * square)
+
+
+def forward_kernel(
+    chunks, block, scale, qkv, tokens, vecs, fc1_bias, grad_m, s_proj, s_fc1, s_fc2,
+    out, lse, branch, resid, rows, act, slope, fc2_grad,
+    w_proj, w_fc1, w_fc2, relay_proj, relay_1, relay_2,
+    proj_here, fc1_here, sent, got, sems, recv, send,
+):
+    pos = place()
+    sib = neighbours(pos)[0]
+    half, width = tokens.shape
+    greet(chip_peers(pos))
+    parts = gather_parts(
+        [s_proj, s_fc1, s_fc2],
+        [w_proj, w_fc1, w_fc2],
+        [relay_proj, relay_1, relay_2],
+        chunks,
+        recv,
+        send,
+        pos,
+    )
+    first = [i for i, (g, _) in enumerate(chunks) if g < 2]
+    events = gather_events(parts, 3)
+    pump = Pump(events)
+    pump.run(3)
+    steps, body = attention_step(qkv, out, lse, block, scale)
+    pump.loop(steps, body, first=2)
+    pump.run(events.index(parts[0].ready) + 1 - pump.next)
+
+    load = pltpu.make_async_copy(w_proj, proj_here, sems.at[0])
+    load.start()
+    load.wait()
+    tile = half // 2
+    swap = remote(sent, got, sems.at[1], sems.at[2], sib)
+
+    def project(i):
+        cols = pl.ds(pl.multiple_of(i * tile, tile), tile)
+        heads = flat(out[:, :, cols])
+        return product(heads, flat(proj_here[...]), 0, 1)
+
+    def other_rows(i, _):
+        sent[pl.ds(pl.multiple_of(i * tile, tile), tile), :] = project(i + 2).astype(BF16)
+        return 0
+
+    def own_rows(i, _):
+        branch[pl.ds(pl.multiple_of(i * tile, tile), tile), :] = project(i) + vecs[3:4, :]
+        return 0
+
+    lax.fori_loop(0, 2, other_rows, 0)
+    swap.start()
+    lax.fori_loop(0, 2, own_rows, 0)
+    pump.run(4)
+    swap.wait()
+    share = remote(rows.at[:half], rows.at[half:], sems.at[3], sems.at[4], sib)
+    piece = half // 4
+
+    def norm(i, _):
+        part = pl.ds(pl.multiple_of(i * piece, piece), piece)
+        total = branch[part, :] + got[part, :].astype(F32)
+        branch[part, :] = total
+        mid = tokens[part, :].astype(F32) + vecs[0:1, :] * total
+        resid[part, :] = mid
+        center = mid - jnp.mean(mid, axis=-1, keepdims=True)
+        spread = jnp.mean(center * center, axis=-1, keepdims=True)
+        normed = center * lax.rsqrt(spread + 1e-06) * (1.0 + vecs[2:3, :]) + vecs[1:2, :]
+        rows[part, :] = normed.astype(BF16)
+        return 0
+
+    lax.fori_loop(0, 4, norm, 0)
+    share.start()
+    pump.run(events.index(parts[first[-1]].ready) + 1 - pump.next)
+
+    load = pltpu.make_async_copy(w_fc1, fc1_here, sems.at[0])
+    load.start()
+    load.wait()
+    share.wait()
+    n = 256
+
+    def hidden(i):
+        cols = pl.ds(pl.multiple_of(i * n, n), n)
+        weight = flat(fc1_here[:, :, cols])
+        value, rate = gelu_and_slope(product(rows[...], weight, 1, 0) + fc1_bias[:, cols])
+        act[:, cols] = value.astype(BF16)
+        slope[:, cols] = rate.astype(BF16)
+
+    pump.loop(act.shape[1] // n, hidden)
+
+    def weight_grad(i):
+        cols = pl.ds(pl.multiple_of(i * n, n), n)
+        value = product(grad_m[...], act[:, cols], 0, 0)
+        fc2_grad[:, :, cols] = value.reshape(fc2_grad.shape[:2] + (n,)).astype(BF16)
+
+    pump.loop(act.shape[1] // n, weight_grad)
+    pump.run()
+    for p in parts:
+        p.finish()
+
+
+def forward_stage(qkv, tokens, vecs, fc1_bias, grad_m, shards, chunks, collective_id, block=512):
+    heads, size, count = qkv.shape[0] // 3, qkv.shape[1], qkv.shape[2]
+    half, width = tokens.shape
+    owned, cols = shards[0].shape[1:]
+    hidden = shards[1].shape[2]
+    vmem, anywhere = pl.BlockSpec(memory_space=pltpu.VMEM), pl.BlockSpec(memory_space=pl.ANY)
+    shape = jax.ShapeDtypeStruct
+    return pl.pallas_call(
+        functools.partial(forward_kernel, chunks, block, size**-0.5),
+        out_shape=[
+            shape((heads, size, count), BF16),
+            shape((heads, 1, count), F32),
+            shape((half, width), F32),
+            shape((half, width), F32),
+            shape((count, width), BF16),
+            shape((count, hidden), BF16),
+            shape((count, hidden), BF16),
+            shape((16, owned, hidden), BF16),
+        ]
+        + gather_shapes(shards),
+        in_specs=[vmem] * 5 + [anywhere] * 3,
+        out_specs=[vmem] * 8 + [anywhere] * 6,
+        scratch_shapes=[
+            pltpu.VMEM((16, owned, cols), BF16),
+            pltpu.VMEM((16, owned, hidden), BF16),
+            pltpu.VMEM((half, width), BF16),
+            pltpu.VMEM((half, width), BF16),
+            pltpu.SemaphoreType.DMA((5,)),
+        ]
+        + gather_sems(chunks),
+        compiler_params=pltpu.CompilerParams(
+            collective_id=collective_id, has_side_effects=True, vmem_limit_bytes=63000 * 1024
+        ),
+    )(qkv, tokens, vecs, fc1_bias, grad_m, *shards)[:11]
+
+
+def attention_back_step(qkv, grad, out, lse, result, key_sum, value_sum, block, scale):
+    heads, blocks = qkv.shape[0] // 3, qkv.shape[2] // block
+    factor = scale * LOG2E
+
+    def body(i):
+        h, j = i // blocks, i % blocks
+        cols = pl.ds(pl.multiple_of(j * block, block), block)
+        queries, keys, values = qkv[h, :, cols], qkv[heads + h], qkv[2 * heads + h]
+        grads = grad[h, :, cols]
+        inner = jnp.sum(out[h, :, cols].astype(F32) * grads.astype(F32), axis=0, keepdims=True)
+        probs = jnp.exp2(product(keys, queries, 0, 0) * factor - lse[h, :, cols])
+        score_grad = (probs * (product(values, grads, 0, 0) - inner)).astype(BF16)
+        value_part = product(grads, probs.astype(BF16), 1, 1)
+        key_part = product(queries, score_grad, 1, 1)
+        result[h, :, cols] = (product(keys, score_grad, 1, 0) * scale).astype(BF16)
+
+        @pl.when(j == 0)
+        def _():
+            key_sum[...] = key_part
+            value_sum[...] = value_part
+
+        @pl.when(j > 0)
+        def _():
+            key_sum[...] += key_part
+            value_sum[...] += value_part
+
+        @pl.when(j == blocks - 1)
+        def _():
+            result[heads + h] = (key_sum[...] * scale).astype(BF16)
+            result[2 * heads + h] = value_sum[...].astype(BF16)
+
+    return heads * blocks, body
+
+
+def attention_backward_kernel(chunks, count, block, scale, qkv, grad, out, lse, *refs):
+    n = len(chunks)
+    grads, result, outs = refs[:count], refs[count], refs[count + 1 : 2 * count + 1]
+    key_sum, value_sum = refs[2 * count + 1 : 2 * count + 3]
+    rest = refs[2 * count + 3 :]
+    lands, (recv, send) = rest[:n], rest[n:]
+    pos = place()
+    greet(chip_peers(pos))
+    parts = [
+        Reduce(grads[g], lands[i], outs[g], recv.at[i], send.at[i], pos, cols)
+        for i, (g, cols) in enumerate(chunks)
+    ]
+    steps, body = attention_back_step(
+        qkv, grad, out, lse, result, key_sum, value_sum, block, scale
+    )
+    pump = Pump(reduce_events(parts))
+    pump.run(2)
+    pump.loop(steps, body, first=4, every=4)
+    pump.run()
+
+
+def attention_backward(qkv, grad, out, lse, grads, chunks, collective_id, block=512):
+    count = len(grads)
+    heads, size, tokens = qkv.shape[0] // 3, qkv.shape[1], qkv.shape[2]
+    vmem = pl.BlockSpec(memory_space=pltpu.VMEM)
+    return pl.pallas_call(
+        functools.partial(attention_backward_kernel, chunks, count, block, size**-0.5),
+        out_shape=[jax.ShapeDtypeStruct(qkv.shape, BF16)]
+        + [jax.ShapeDtypeStruct(g.shape[1:], F32) for g in grads],
+        in_specs=[vmem] * (4 + count),
+        out_specs=[vmem] * (1 + count),
+        scratch_shapes=[pltpu.VMEM((size, tokens), F32)] * 2 + reduce_scratch(chunks),
+        compiler_params=pltpu.CompilerParams(
+            collective_id=collective_id, has_side_effects=True, vmem_limit_bytes=63000 * 1024
+        ),
+    )(qkv, grad, out, lse, *grads)
 
 
 def index_of(z, x, c, y):
@@ -1024,7 +1396,11 @@
     pieces = jnp.pad(
         silu_cond.astype(BF16).reshape(16, 1, owned), ((0, 0), (0, 7), (0, 128 - owned))
     )
-    modulation, silu_owned = mod_forward(pieces, mod_weight, mod_bias.astype(F32)[None], 1)
+    s_qkv = query_key_value_weight.reshape(1, owned, 3 * cols)
+    modulation, silu_owned, w_qkv = first_stage(
+        pieces, mod_weight, mod_bias.astype(F32)[None], s_qkv, [(0, p) for p in columns(3 * cols, 896)], 2
+    )
+    w_qkv = w_qkv.reshape(width, 3 * cols)
     shift_a, scale_a, gate_a, shift_m, scale_m, gate_m = [
         modulation[:, i * width : (i + 1) * width] for i in range(6)
     ]
@@ -1036,44 +1412,53 @@
     q_bias, v_bias, fc1_bias = biases[:cols], biases[cols : 2 * cols], biases[2 * cols :]
     grad_out = trade(out_grad.reshape(half, width)).astype(F32)
 
-    s_qkv = query_key_value_weight.reshape(1, owned, 3 * cols)
     s_proj = attention_out_weight.T.reshape(1, owned, cols)
     s_fc1 = first_hidden_weight.reshape(1, owned, hidden)
     s_fc2 = second_hidden_weight.T.reshape(1, owned, hidden)
-    (w_qkv,) = gather_weights([s_qkv], [(0, (0, 896)), (0, (896, 832))], 2)
-    w_qkv = w_qkv.reshape(width, 3 * cols)
     chunks = [(0, None)] + [(g, p) for g in (1, 2) for p in columns(hidden, 1152)]
-    w_proj, w_fc1, w_fc2 = gather_weights([s_proj, s_fc1, s_fc2], chunks, 3)
-    w_proj, w_fc1, w_fc2 = (w.reshape(width, -1) for w in (w_proj, w_fc1, w_fc2))
-
-    normed_a, norm_a_back = jax.vjp(modulate, tokens_here, shift_a, scale_a)
+
+    normed_a = modulate(tokens_here, shift_a, scale_a)
     rows_a = both_halves(normed_a.astype(BF16))
     qkv_shift = jnp.concatenate([q_bias, jnp.zeros_like(q_bias), v_bias]).astype(F32)
-    qkv = (jnp.dot(rows_a, w_qkv, preferred_element_type=F32) + qkv_shift).astype(BF16)
-    packed = qkv.reshape(2 * half, 3, heads_here, head_size)
-    attended, log_totals = attend_forward(packed)
-    branch_a = own_sum(
-        jnp.einsum("rc,dc->rd", attended, w_proj, preferred_element_type=F32)
-    ) + attention_out_bias.astype(F32)
-    resid_mid = tokens_here + gate_a * branch_a
-
-    normed_m, norm_m_back = jax.vjp(modulate, resid_mid, shift_m, scale_m)
-    rows_m = both_halves(normed_m.astype(BF16))
-    preact = jnp.dot(rows_m, w_fc1, preferred_element_type=F32) + fc1_bias.astype(F32)
-    activated, gelu_back = jax.vjp(gelu_tanh, preact)
-    act_low = activated.astype(BF16)
+    qkv = product(w_qkv, rows_a, 0, 1) + qkv_shift[:, None]
+    qkv = qkv.astype(BF16).reshape(3 * heads_here, head_size, 2 * half)
+    grad_m_own = (grad_out * gate_m).astype(BF16)
+    fc2_bias_part = jnp.sum(grad_m_own, axis=0, dtype=F32)
+    grad_m = both_halves(grad_m_own)
+    vecs = jnp.concatenate([gate_a, shift_m, scale_m, attention_out_bias.astype(F32)[None]])
+    (
+        attended,
+        log_totals,
+        branch_a,
+        resid_mid,
+        rows_m,
+        act_low,
+        slope,
+        fc2_grad,
+        w_proj,
+        w_fc1,
+        w_fc2,
+    ) = forward_stage(
+        qkv,
+        carried[:half],
+        vecs,
+        fc1_bias.astype(F32)[None],
+        grad_m,
+        [s_proj, s_fc1, s_fc2],
+        chunks,
+        3,
+    )
+    w_proj, w_fc1, w_fc2 = (w.reshape(width, -1) for w in (w_proj, w_fc1, w_fc2))
+    attended_rows = attended.reshape(cols, 2 * half)
+    _, norm_m_back = jax.vjp(modulate, resid_mid, shift_m, scale_m)
     branch_m = own_sum(
         jnp.einsum("rf,df->rd", act_low, w_fc2, preferred_element_type=F32)
     ) + second_hidden_bias.astype(F32)
     output = (resid_mid + gate_m * branch_m).astype(BF16)
 
     gate_m_grad = jnp.sum(grad_out * branch_m, axis=0)
-    grad_m_own = (grad_out * gate_m).astype(BF16)
-    fc2_bias_part = jnp.sum(grad_m_own, axis=0, dtype=F32)
-    grad_m = both_halves(grad_m_own)
-    fc2_grad = jnp.einsum("rd,rf->df", grad_m, act_low, preferred_element_type=F32).astype(BF16)
     act_grad = jnp.dot(grad_m, w_fc2, preferred_element_type=F32)
-    pre_grad = gelu_back(act_grad)[0].astype(BF16)
+    pre_grad = (act_grad * slope.astype(F32)).astype(BF16)
     fc1_bias_part = jnp.sum(pre_grad, axis=0, dtype=F32)
     fc1_grad = jnp.einsum("rd,rf->df", rows_m, pre_grad, preferred_element_type=F32).astype(BF16)
     normed_m_grad = own_sum(
@@ -1086,32 +1471,28 @@
     grad_a_own = (resid_grad * gate_a).astype(BF16)
     proj_bias_part = jnp.sum(grad_a_own, axis=0, dtype=F32)
     grad_a = both_halves(grad_a_own)
-    proj_grad = jnp.einsum("rd,rc->dc", grad_a, attended, preferred_element_type=F32).astype(BF16)
-    attended_grad = jnp.dot(grad_a, w_proj, preferred_element_type=F32).astype(BF16)
-    qkv_grad = attend_backward(
-        (packed, attended_grad.reshape(2 * half, heads_here, head_size), log_totals)
-    ).reshape(2 * half, 3 * cols)
-    qkv_bias_part = jnp.sum(qkv_grad, axis=0, dtype=F32)
-    qkv_bias_part = jnp.concatenate([qkv_bias_part[:cols], qkv_bias_part[2 * cols :]])
-    qkv_wgrad = jnp.einsum("rd,rc->dc", rows_a, qkv_grad, preferred_element_type=F32).astype(BF16)
-    normed_a_grad = own_sum(
-        jnp.einsum("rc,dc->rd", qkv_grad, w_qkv, preferred_element_type=F32)
-    )
-    input_part, shift_a_grad, scale_a_grad = norm_a_back(normed_a_grad)
-    tokens_grad = (resid_grad + input_part).astype(BF16)
-
+    proj_grad = product(grad_a, attended_rows, 0, 1).astype(BF16)
+    attended_grad = product(w_proj, grad_a, 0, 1).astype(BF16)
     chunks = [(g, p) for g in (0, 1) for p in columns(hidden, 768)] + [(2, (0, cols))]
-    fc2_out, fc1_out, proj_out = reduce_grads(
-        [g.reshape(16, owned, -1) for g in (fc2_grad, fc1_grad, proj_grad)], chunks, 4
-    )
-    (qkv_out,) = reduce_grads(
-        [qkv_wgrad.reshape(16, owned, -1)], [(0, (0, 640)), (0, (640, 640)), (0, (1280, 448))], 5
-    )
-
+    qkv_grad, fc2_out, fc1_out, proj_out = attention_backward(
+        qkv,
+        attended_grad.reshape(attended.shape),
+        attended,
+        log_totals,
+        [fc2_grad, fc1_grad.reshape(16, owned, -1), proj_grad.reshape(16, owned, -1)],
+        chunks,
+        4,
+    )
+    qkv_bias_part = jnp.sum(qkv_grad, axis=2, dtype=F32)
+    half_part = jnp.concatenate(
+        [
+            fc1_bias_part,
+            qkv_bias_part[:heads_here].reshape(-1),
+            qkv_bias_part[2 * heads_here :].reshape(-1),
+        ]
+    )[None]
     mod_part = jnp.concatenate(
         [
-            shift_a_grad.reshape(1, -1),
-            scale_a_grad.reshape(1, -1),
             gate_a_grad.reshape(1, -1),
             shift_m_grad.reshape(1, -1),
             scale_m_grad.reshape(1, -1),
@@ -1120,9 +1501,19 @@
         axis=1,
     )
     wide_part = jnp.concatenate([fc2_bias_part, proj_bias_part])[None]
-    half_part = jnp.concatenate([fc1_bias_part, qkv_bias_part])[None]
-    mod_weight_grad, mod_bias_grad, silu_grad, wide, narrow = mod_backward(
-        mod_part, wide_part, half_part, silu_owned, mod_weight, 6
+    tokens_grad, qkv_out, mod_weight_grad, mod_bias_grad, silu_grad, wide, narrow = last_stage(
+        rows_a,
+        qkv_grad,
+        w_qkv,
+        carried[:half],
+        resid_grad,
+        scale_a,
+        mod_part,
+        wide_part,
+        half_part,
+        silu_owned,
+        mod_weight,
+        6,
     )
     cond_grad = silu_back(silu_grad[:, 0, :owned].reshape(1, width))[0]
     return (
@@ -1131,7 +1522,7 @@
         cond_grad,
         mod_weight_grad,
         mod_bias_grad[0],
-        qkv_out.reshape(owned, 3, cols),
+        jnp.moveaxis(qkv_out, 0, 1),
         narrow[0, hidden:].reshape(2, cols),
         proj_out.T,
         wide[0, width:],

time: 698 us -> 548 us (0.79)
  matrix products: 180 us -> 46 us
  other arithmetic: 66.2 us -> 40 us
  Pallas kernels: 385 us -> 408 us
  local copies, waits for them, and re-layouts: 31.4 us -> 22.2 us
    dot_general x20 -> x3, matrix products: 136 us -> 14.5 us  [product(): lax.dot_general(a, b, (((ca,), (cb,)), ((), ())), preferred_element_type=...]
    convert_element_type x6 -> x0, other arithmetic: 29.5 us -> none  [the longest x2 26.5 us: attend_backward(): score_grad = (probs * (prob_grad - inner)).astype(jnp.bfloat16)]
    pallas_call x6 -> x4, Pallas kernels: 385 us -> 408 us  [the longest x1 140 us: forward_stage(): pl.pallas_call(functools.partial(forward_kernel, chunks, block, size ** (...]
    concatenate x0 -> x4, other arithmetic: none -> 9.34 us  [the longest x2 8.09 us: both_halves(): jnp.concatenate([value, lax.ppermute(value, AXES, core_pairs())], axis=0)]
    reduce_sum x3, other arithmetic: 12.5 us -> 3.44 us  [the longest x1 2.59 us: on_device_chip(): qkv_bias_part = jnp.sum(qkv_grad, axis=2, dtype=F32)]
  transfers between devices with their start and end apart: 12 -> 9, of which waited for: 1 -> 1; matrix products, arithmetic and copies ran while one was open for 27% -> 12% of each run, Pallas kernels for 56% -> 50%
where the time goes in v3:
time: 548 us; the launch traced here: 541 us
  Pallas kernels  408 us (74%)
  matrix products  46 us (8%)
  other arithmetic  40 us (7%)
  local copies, waits for them, and re-layouts  22.2 us (4%)
  starting transfers between devices  16.8 us (3%)
  waiting for transfers between devices  6.01 us (1%)
    pallas_call x1, Pallas kernels, forward_stage(): pl.pallas_call(functools.partial(forward_kernel, chunks, block, size ** (...  140 us
    pallas_call x1, Pallas kernels, attention_backward(): pl.pallas_call(functools.partial(attention_backward_kernel, chunks, count...  135 us
    pallas_call x1, Pallas kernels, last_stage(): pl.pallas_call(last_kernel, out_shape=[shape((half, width), BF16), shape(...  76.8 us
    pallas_call x1, Pallas kernels, first_stage(): pl.pallas_call(functools.partial(first_kernel, chunks), out_shape=[jax.Sh...  56 us
    ppermute x4, starting transfers between devices, trade(): moved = lax.ppermute(value, AXES, latent_pairs())  15.7 us
    dot_general x3, matrix products, product(): lax.dot_general(a, b, (((ca,), (cb,)), ((), ())), preferred_element_type=...  14.5 us
    dot_general x1, matrix products, on_device_chip(): act_grad = jnp.dot(grad_m, w_fc2, preferred_element_type=F32)  11.4 us
  transfers between devices with their start and end apart: 9, of which 1 were waited for; matrix products, arithmetic and copies ran while one was open for 12% of the time, Pallas kernels for 50%

profile of v3, /device:TPU:1, one launch (start us, length us, event | category | flops | bytes accessed | tf_op | source)
XLA Modules:
  0.0 540.6 jit_solution(15337698814876625825)
XLA Ops:
  0.7 4.7 collective-permute-start.2
  5.4 0.8 reshape.180
  6.2 0.7 pad_maximum_fusion.9
  6.9 2.4 pad_maximum_fusion.5
  9.3 1.9 collective-permute-start
  13.0 56.0 %shard_map.228 = (f32[1,6912]{1,0:T(1,128)S(1)}, bf16[16,8,128]{2,1,0:T(8,128)(2,1)S(1)}, bf16[16,72,1728]{2,1,0:T(8,128)(2,1)S(1)}, bf16[8,72,1728]{2,1,0:T(8,128)(2,1)}) custom-call(bf16[16,8,128]{2,1,0:T(8,128)(2,1)S(1)} %pad.4.piece_ref, bf16[72,6912]{1,0:T(8,128)(2,1)S(1)} %copy-done.2, f32[1,6912]{1,0:T(1,128)S(1)} %reshape.203.bias_ref, ...), custom_call_target="tpu_custom_call" | custom-call | tf_op jit(solution)/shard_map/pallas_call | solution.py:841
  69.0 1.8 fusion.17
  70.8 1.0 copy-done.13
  71.8 3.8 convert_reduce_fusion.4
  75.7 1.6 broadcast_select_fusion
  77.9 1.5 fusion.5
  79.5 0.6 pad_maximum_fusion.6.vecs
  80.1 1.1 slice.94.tokens.tokens_ref
  82.0 3.4 pad_maximum_fusion.1.grad_m
  85.5 8.2 %add_convert_fusion = bf16[1728,1024]{1,0:T(8,128)(2,1)} fusion(bf16[1152,1728]{1,0:T(8,128)(2,1)S(1)} %bitcast.42, f32[1728]{0:T(1024)S(1)} %convert_element_type.93, bf16[512,1152]{1,0:T(8,128)(2,1)} %collective-permute-done.1, bf16[512,1152]{1,0:T(8,128)(2,1)} %fusion.5), kind=kOutput, calls=%fused_computation.4 | convolution fusion | flops 4085121024 | bytes 9886464 | tf_op jit(solution)/shard_map/dot_general | solution.py:870
  93.7 140.1 %shard_map.229 = (bf16[8,72,1024]{2,1,0:T(8,128)(2,1)}, f32[8,1,1024]{2,1,0:T(1,128)}, f32[512,1152]{1,0:T(8,128)}, f32[512,1152]{1,0:T(8,128)}, bf16[1024,1152]...) custom-call(bf16[24,72,1024]{2,1,0:T(8,128)(2,1)} %bitcast.43, ...), custom_call_target="tpu_custom_call" | custom-call | tf_op jit(solution)/shard_map/pallas_call | solution.py:1228
  233.8 11.4 %convert_reduce_fusion = (f32[2304]{0:T(1024)}, bf16[1024,2304]{1,0:T(8,128)(2,1)S(1)}) fusion(bf16[1024,2304]{1,0:T(8,128)(2,1)} %get-tuple-element.44, bf16[1152,2304]{1,0:T(8,128)(2,1)} %bitcast.59, bf16[512,1152]{1,0:T(8,128)(2,1)} %collective-permute-done.3, bf16[512,1152]{1,0:T(8,128)(2,1)} %get-tuple-element.74), kind=kOutput, calls=%fused_computation.1 | convolution fusion | flops 5452331008 | bytes 17114112 | tf_op jit(solution)/shard_map/dot_general | solution.py:1460
  245.2 6.3 %fusion.21 = f32[1024,1152]{1,0:T(8,128)S(1)} fusion(bf16[1024,2304]{1,0:T(8,128)(2,1)S(1)} %get-tuple-element.101, bf16[1152,2304]{1,0:T(8,128)(2,1)S(1)} %bitcast.63), kind=kOutput, calls=%fused_computation.77 | convolution fusion | flops 5435817984 | bytes 14745600 | tf_op jit(solution)/shard_map/rf,df->rd/dot_general | solution.py:1465
  251.5 1.3 slice.137
  252.8 6.3 %fusion.20 = f32[1024,1152]{1,0:T(8,128)S(1)} fusion(bf16[1024,2304]{1,0:T(8,128)(2,1)S(1)} %bitcast.65, bf16[1152,2304]{1,0:T(8,128)(2,1)S(1)} %bitcast.62), kind=kOutput, calls=%fused_computation.76 | convolution fusion | flops 5435817984 | bytes 14745600 | tf_op jit(solution)/shard_map/rf,df->rd/dot_general | solution.py:1455
  259.1 1.1 slice.138
  260.8 1.7 copy-done.36
  262.5 7.6 %convolution_convert_fusion = bf16[1152,2304]{1,0:T(8,128)(2,1)} fusion(bf16[1024,1152]{1,0:T(8,128)(2,1)S(1)} %copy-done.36, bf16[1024,2304]{1,0:T(8,128)(2,1)S(1)} %copy-done.39), kind=kOutput, calls=%fused_computation | convolution fusion | flops 5438472192 | bytes 12386304 | tf_op jit(solution)/shard_map/rd,rf->df/dot_general | solution.py:1463
  270.8 3.1 multiply_reduce_fusion
  274.2 4.3 fusion.7
  279.7 4.7 pad_maximum_fusion.rows_ref
  285.6 6.0 %collective-permute-start.5 = (bf16[512,1152]{1,0:T(8,128)(2,1)}, bf16[512,1152]{1,0:T(8,128)(2,1)}, u32[]{:S(2)}, u32[]{:S(2)}) collective-permute-start(bf16[512,1152]{1,0:T(8,128)(2,1)} %get-tuple-element.84), channel_id=1, source_target_pairs={{1,2},{2,1},{5,6},{6,5},{9,10},{10,9},{13,14},{14,13},{17,18},{18,... | collective-permute-start | bytes 3538952 | tf_op jit(solution)/shard_map/ppermute | solution.py:1355
  292.3 1.0 copy-done.37
  293.3 1.7 convolution_convert_fusion.1
  295.0 1.6 copy.31
  296.7 4.6 convolution_convert_fusion.2
  301.3 135.0 %shard_map.230 = (bf16[24,72,1024]{2,1,0:T(8,128)(2,1)}, f32[72,2304]{1,0:T(8,128)}, f32[72,2304]{1,0:T(8,128)}, f32[72,576]{1,0:T(8,128)}) custom-call(bf16[24,72,1024]{2,1,0:T(8,128)(2,1)} %bitcast.44, bf16[8,72,1024]{2,1,0:T(8,128)(2,1)} %bitcast.50, bf16[8,72,1024]{2,1,0:T(8,128)(2,1)} %get-tuple-element.46.out, f32[8,1,1024]{2,1,0:T(1,128)} %get-tuple-element.47.lse, ...), custom_call_target="tpu_custom_call" | custom-call | tf_op jit(solution)/shard_map/pallas_call | solution.py:1316
  436.3 2.6 convert_reduce_fusion.1
  439.8 76.8 %shard_map.231 = (bf16[512,1152]{1,0:T(8,128)(2,1)}, f32[3,72,576]{2,1,0:T(8,128)}, f32[72,6912]{1,0:T(8,128)}, f32[1,6912]{1,0:T(1,128)}, f32[16,8,128]{2,1,0:T...) custom-call(bf16[1024,1152]{1,0:T(8,128)(2,1)} %pad_maximum_fusion.rows_ref, ...), custom_call_target="tpu_custom_call" | custom-call | tf_op jit(solution)/shard_map/pallas_call | solution.py:1055
  516.6 3.1 collective-permute-start.8
  519.7 0.9 slice_reduce_fusion.1
  520.6 1.4 slice_reduce_fusion.2
  521.9 0.7 reshape_squeeze.7
  522.7 1.4 reduce.7
  524.1 1.3 slice_reduce_fusion
  526.1 2.4 select_bitcast_fusion.1
  528.5 6.0 %collective-permute-done.8 = bf16[512,1152]{1,0:T(8,128)(2,1)S(1)} collective-permute-done((bf16[512,1152]{1,0:T(8,128)(2,1)}, bf16[512,1152]{1,0:T(8,128)(2,1)S(1)}, u32[]{:S(2)}, u32[]{:S(2)}) %collective-permute-start.8) | collective-permute-done | bytes 1179680 | tf_op jit(solution)/shard_map/ppermute | solution.py:1355
  534.5 1.1 select_bitcast_fusion
  535.6 1.3 copy.38
  537.0 0.8 copy.39
  537.8 0.7 copy.40
  538.5 0.8 copy.41
  539.3 0.8 copy.42
  (143 shorter events, 9.5 us)
Async XLA Ops:
  0.6 10.5 %copy-start.28 = (bf16[1,1152]{1,0:T(2,128)(2,1)S(1)}, bf16[1,1152]{1,0:T(2,128)(2,1)}, u32[]{:S(2)}) copy-start(bf16[1,1152]{1,0:T(2,128)(2,1)} %param.14) | copy-start | bytes 6916
  0.7 11.3 %copy-start.20 = (bf16[72,3,576]{2,0,1:T(8,128)(2,1)S(1)}, bf16[72,3,576]{2,0,1:T(8,128)(2,1)}, u32[]{:S(2)}) copy-start(bf16[72,3,576]{2,0,1:T(8,128)(2,1)} %param.17) | copy-start | bytes 746500
  0.7 11.7 %copy-start.31 = (bf16[6912]{0:T(1024)(128)(2,1)S(1)}, bf16[6912]{0:T(1024)(128)(2,1)}, u32[]{:S(2)}) copy-start(bf16[6912]{0:T(1024)(128)(2,1)} %param.16) | copy-start | bytes 41476
  0.7 11.7 %copy-start.34 = (bf16[1152]{0:T(1024)(128)(2,1)S(1)}, bf16[1152]{0:T(1024)(128)(2,1)}, u32[]{:S(2)}) copy-start(bf16[1152]{0:T(1024)(128)(2,1)} %param.20) | copy-start | bytes 6916
  0.7 11.7 %copy-start.33 = (bf16[1152]{0:T(1024)(128)(2,1)S(1)}, bf16[1152]{0:T(1024)(128)(2,1)}, u32[]{:S(2)}) copy-start(bf16[1152]{0:T(1024)(128)(2,1)} %param.24) | copy-start | bytes 6916
  0.7 12.3 %copy-start.2 = (bf16[72,6912]{1,0:T(8,128)(2,1)S(1)}, bf16[72,6912]{1,0:T(8,128)(2,1)}, u32[]{:S(2)}) copy-start(bf16[72,6912]{1,0:T(8,128)(2,1)} %w_ref.3) | copy-start | bytes 2985988
  0.7 70.1 %collective-permute-start.2 = (bf16[512,1152]{1,0:T(8,128)(2,1)}, bf16[512,1152]{1,0:T(8,128)(2,1)S(1)}, u32[]{:S(2)}, u32[]{:S(2)}) collective-permute-start(bf16[512,1152]{1,0:T(8,128)(2,1)} %bitcast.51), channel_id=1, source_target_pairs={{1,2},{2,1},{5,6},{6,5},{9,10},{10,9},{13,14},{14,13},{17,18},{18,... | collective-permute-start | bytes 3538952 | tf_op jit(solution)/shard_map/ppermute | solution.py:1355
  9.3 66.4 %collective-permute-start = (bf16[515,1152]{1,0:T(8,128)(2,1)}, bf16[515,1152]{1,0:T(8,128)(2,1)}, u32[]{:S(2)}, u32[]{:S(2)}) collective-permute-start(bf16[515,1152]{1,0:T(8,128)(2,1)} %pad_maximum_fusion.5), channel_id=1, source_target_pairs={{1,2},{2,1},{5,6},{6,5},{9,10},{10,9},{13,14},{14,13},{17,18},{18,... | collective-permute-start | bytes 3559688 | tf_op jit(solution)/shard_map/ppermute | solution.py:1355
  69.0 6.6 %copy-start = (bf16[16,72,1728]{2,1,0:T(8,128)(2,1)}, bf16[16,72,1728]{2,1,0:T(8,128)(2,1)S(1)}, u32[]{:S(2)}) copy-start(bf16[16,72,1728]{2,1,0:T(8,128)(2,1)S(1)} %get-tuple-element.38) | copy-start | bytes 11943940
  69.0 6.6 %copy-start.3 = (bf16[16,8,128]{2,1,0:T(8,128)(2,1)}, bf16[16,8,128]{2,1,0:T(8,128)(2,1)S(1)}, u32[]{:S(2)}) copy-start(bf16[16,8,128]{2,1,0:T(8,128)(2,1)S(1)} %get-tuple-element.52.silu_ref) | copy-start | bytes 98308
  70.8 6.4 %copy-start.22 = (f32[1152]{0:T(1024)}, f32[1152]{0:T(1024)S(1)}, u32[]{:S(2)}) copy-start(f32[1152]{0:T(1024)S(1)} %get-tuple-element.92) | copy-start | bytes 13828
  71.8 3.8 copy-start.8
  75.6 6.4 %collective-permute-start.3 = (bf16[512,1152]{1,0:T(8,128)(2,1)}, bf16[512,1152]{1,0:T(8,128)(2,1)}, u32[]{:S(2)}, u32[]{:S(2)}) collective-permute-start(bf16[512,1152]{1,0:T(8,128)(2,1)} %get-tuple-element.74), channel_id=1, source_target_pairs={{0,2},{1,3},{2,0},{3,1},{4,6},{5,7},{6,4},{7,5},{8,10},{9,11},{10,... | collective-permute-start | bytes 3538952 | tf_op jit(solution)/shard_map/ppermute | solution.py:1361
  79.5 6.0 %collective-permute-start.1 = (bf16[512,1152]{1,0:T(8,128)(2,1)}, bf16[512,1152]{1,0:T(8,128)(2,1)}, u32[]{:S(2)}, u32[]{:S(2)}) collective-permute-start(bf16[512,1152]{1,0:T(8,128)(2,1)} %fusion.5), channel_id=1, source_target_pairs={{0,2},{1,3},{2,0},{3,1},{4,6},{5,7},{6,4},{7,5},{8,10},{9,11},{10,... | collective-permute-start | bytes 3538952 | tf_op jit(solution)/shard_map/ppermute | solution.py:1361
  82.0 3.4 copy-start.1
  233.8 11.4 %copy-start.35 = (bf16[16,72,2304]{2,1,0:T(8,128)(2,1)S(1)}, bf16[16,72,2304]{2,1,0:T(8,128)(2,1)}, u32[]{:S(2)}) copy-start(bf16[16,72,2304]{2,1,0:T(8,128)(2,1)} %get-tuple-element.45) | copy-start | bytes 15925252
  233.8 19.0 %slice-start = ((s8[5308416]{0:T(1024)(128)(4,1)}), s8[4194304]{0:T(1024)(128)(4,1)S(1)}, s32[]{:S(2)}) async-start(s8[5308416]{0:T(1024)(128)(4,1)} %bitcast.60), calls=%async_computation | async-start | bytes 8388608
  233.8 19.0 %slice-start.2 = ((s8[4718592]{0:T(1024)(128)(4,1)}), s8[4194304]{0:T(1024)(128)(4,1)S(1)}, s32[]{:S(2)}) async-start(s8[4718592]{0:T(1024)(128)(4,1)} %bitcast.64), calls=%async_computation.2 | async-start | bytes 8388608
  245.2 6.3 %copy-start.38 = (bf16[1024,2304]{1,0:T(8,128)(2,1)}, bf16[1024,2304]{1,0:T(8,128)(2,1)S(1)}, u32[]{:S(2)}) copy-start(bf16[1024,2304]{1,0:T(8,128)(2,1)S(1)} %get-tuple-element.101) | copy-start | bytes 14155780
  245.2 7.6 %slice-start.1 = ((s8[5308416]{0:T(1024)(128)(4,1)}), s8[1114112]{0:T(1024)(128)(4,1)S(1)}, s32[]{:S(2)}) async-start(s8[5308416]{0:T(1024)(128)(4,1)} %bitcast.60), calls=%async_computation.1 | async-start | bytes 2228224
  245.2 7.6 %slice-start.3 = ((s8[4718592]{0:T(1024)(128)(4,1)}), s8[524288]{0:T(1024)(128)(4,1)S(1)}, s32[]{:S(2)}) async-start(s8[4718592]{0:T(1024)(128)(4,1)} %bitcast.64), calls=%async_computation.3 | async-start | bytes 1048576
  251.5 7.6 %copy-start.6 = (f32[1024,1152]{1,0:T(8,128)}, f32[1024,1152]{1,0:T(8,128)S(1)}, u32[]{:S(2)}) copy-start(f32[1024,1152]{1,0:T(8,128)S(1)} %fusion.21) | copy-start | bytes 14155780
  252.8 17.9 %collective-permute-start.6 = (bf16[512,1152]{1,0:T(8,128)(2,1)}, bf16[512,1152]{1,0:T(8,128)(2,1)}, u32[]{:S(2)}, u32[]{:S(2)}) collective-permute-start(bf16[512,1152]{1,0:T(8,128)(2,1)} %slice.137), channel_id=1, source_target_pairs={{0,2},{1,3},{2,0},{3,1},{4,6},{5,7},{6,4},{7,5},{8,10},{9,11},{10,... | collective-permute-start | bytes 3538952 | tf_op jit(solution)/shard_map/ppermute | solution.py:1366
  252.8 7.9 %copy-start.39 = (bf16[1024,2304]{1,0:T(8,128)(2,1)S(1)}, bf16[1024,2304]{1,0:T(8,128)(2,1)}, u32[]{:S(2)}) copy-start(bf16[1024,2304]{1,0:T(8,128)(2,1)} %copy-done.38) | copy-start | bytes 14155780
  259.1 11.0 %copy-start.9 = (f32[1024,1152]{1,0:T(8,128)}, f32[1024,1152]{1,0:T(8,128)S(1)}, u32[]{:S(2)}) copy-start(f32[1024,1152]{1,0:T(8,128)S(1)} %fusion.20) | copy-start | bytes 14155780
  259.1 3.4 copy-start.36
  260.3 13.6 %collective-permute-start.4 = (bf16[512,1152]{1,0:T(8,128)(2,1)}, bf16[512,1152]{1,0:T(8,128)(2,1)}, u32[]{:S(2)}, u32[]{:S(2)}) collective-permute-start(bf16[512,1152]{1,0:T(8,128)(2,1)} %slice.138), channel_id=1, source_target_pairs={{0,2},{1,3},{2,0},{3,1},{4,6},{5,7},{6,4},{7,5},{8,10},{9,11},{10,... | collective-permute-start | bytes 3538952 | tf_op jit(solution)/shard_map/ppermute | solution.py:1366
  262.5 7.6 %copy-start.4 = (f32[512,1152]{1,0:T(8,128)S(1)}, f32[512,1152]{1,0:T(8,128)}, u32[]{:S(2)}) copy-start(f32[512,1152]{1,0:T(8,128)} %get-tuple-element.40) | copy-start | bytes 7077892
  270.8 3.4 copy-start.7
  270.8 3.4 copy-start.23
  270.8 3.4 copy-start.26
  274.2 4.3 copy-start.27
  279.1 5.3 copy-start.5
  279.1 13.2 %copy-start.15 = (bf16[512,1152]{1,0:T(8,128)(2,1)}, bf16[512,1152]{1,0:T(8,128)(2,1)S(1)}, u32[]{:S(2)}) copy-start(bf16[512,1152]{1,0:T(8,128)(2,1)S(1)} %get-tuple-element.77) | copy-start | bytes 3538948
  279.1 5.2 copy-start.10
  279.1 13.2 %collective-permute-start.7 = (bf16[512,1152]{1,0:T(8,128)(2,1)S(1)}, bf16[512,1152]{1,0:T(8,128)(2,1)S(1)}, u32[]{:S(2)}, u32[]{:S(2)}) collective-permute-start(bf16[512,1152]{1,0:T(8,128)(2,1)S(1)} %get-tuple-element.77), channel_id=1, source_target_pairs={{0,2},{1,3},{2,0},{3,1},{4,6},{5,7},{6,4},{7,5},{8,10},{9,11},{10,... | collective-permute-start | bytes 3538952 | tf_op jit(solution)/shard_map/ppermute | solution.py:1361
  284.3 9.0 %copy-start.12 = (bf16[8,72,1024]{2,1,0:T(8,128)(2,1)S(1)}, bf16[8,72,1024]{2,1,0:T(8,128)(2,1)}, u32[]{:S(2)}) copy-start(bf16[8,72,1024]{2,1,0:T(8,128)(2,1)} %get-tuple-element.46.out) | copy-start | bytes 3538948
  285.6 240.4 %collective-permute-start.5 = (bf16[512,1152]{1,0:T(8,128)(2,1)}, bf16[512,1152]{1,0:T(8,128)(2,1)}, u32[]{:S(2)}, u32[]{:S(2)}) collective-permute-start(bf16[512,1152]{1,0:T(8,128)(2,1)} %get-tuple-element.84), channel_id=1, source_target_pairs={{1,2},{2,1},{5,6},{6,5},{9,10},{10,9},{13,14},{14,13},{17,18},{18,... | collective-permute-start | bytes 3538952 | tf_op jit(solution)/shard_map/ppermute | solution.py:1355
  295.0 1.7 copy-start.16
  436.3 2.8 copy-start.32
  439.8 85.6 %copy-start.29 = (bf16[1,1152]{1,0:T(2,128)(2,1)S(1)}, bf16[1,1152]{1,0:T(2,128)(2,1)}, u32[]{:S(2)}) copy-start(bf16[1,1152]{1,0:T(2,128)(2,1)} %param.14) | copy-start | bytes 6916
  439.8 85.6 %copy-start.30 = (f32[1,1152]{1,0:T(1,128)S(1)}, f32[1,1152]{1,0:T(1,128)}, u32[]{:S(2)}) copy-start(f32[1,1152]{1,0:T(1,128)} %get-tuple-element.82) | copy-start | bytes 13828
  516.6 17.9 %copy-start.14 = (bf16[512,1152]{1,0:T(8,128)(2,1)S(1)}, bf16[512,1152]{1,0:T(8,128)(2,1)}, u32[]{:S(2)}) copy-start(bf16[512,1152]{1,0:T(8,128)(2,1)} %get-tuple-element.53) | copy-start | bytes 3538948
  516.6 17.9 %collective-permute-start.8 = (bf16[512,1152]{1,0:T(8,128)(2,1)}, bf16[512,1152]{1,0:T(8,128)(2,1)S(1)}, u32[]{:S(2)}, u32[]{:S(2)}) collective-permute-start(bf16[512,1152]{1,0:T(8,128)(2,1)} %get-tuple-element.53), channel_id=1, source_target_pairs={{1,2},{2,1},{5,6},{6,5},{9,10},{10,9},{13,14},{14,13},{17,18},{18,... | collective-permute-start | bytes 3538952 | tf_op jit(solution)/shard_map/ppermute | solution.py:1355
  528.5 7.1 %copy-start.11 = (f32[72,6912]{1,0:T(8,128)S(1)}, f32[72,6912]{1,0:T(8,128)}, u32[]{:S(2)}) copy-start(f32[72,6912]{1,0:T(8,128)} %get-tuple-element.119) | copy-start | bytes 5971972
  535.6 2.2 copy-start.21
  535.6 2.9 copy-start.18
  537.0 2.3 copy-start.17
  (5 other events, 4.8 us)

commit v4 on v3

--- a/solution.py
+++ b/solution.py
@@ -342,11 +342,12 @@
 
 
 GATHER_RECV = 24
-GATHER_SEND = 28
+GATHER_SEND = 32
 
 
 class Gather:
-    def __init__(self, shard, full, relay, cols, recv, send, pos):
+    def __init__(self, shard, full, relay, cols, wide, recv, send, pos):
+        self.wide = wide
         self.shard, self.full, self.relay, self.cols = shard, full, relay, cols
         self.recv, self.send, self.pos = recv, send, pos
         d, z, x, c, y = pos
@@ -368,7 +369,7 @@
 
     def stay(self):
         return pltpu.make_async_copy(
-            self.part(self.shard, 0), self.part(self.full, self.pos[0]), self.send.at[27]
+            self.part(self.shard, 0), self.part(self.full, self.pos[0]), self.send.at[31]
         )
 
     def start(self):
@@ -419,7 +420,8 @@
         @pl.when(self.home)
         def _():
             self.came(q)
-            self.move(dst, dst, 12 + k, 8 + q, self.far).start()
+            if not self.wide:
+                self.move(dst, dst, 12 + k, 8 + q, self.far).start()
 
         @pl.when(self.away)
         def _():
@@ -435,29 +437,43 @@
             block = self.part(self.full, 2 * q + 1 - c)
             self.came(16 + q)
             self.move(block, block, 12 + k, 16 + q, self.xn).start()
+            if self.wide:
+                block = self.part(self.full, 2 * q + c)
+                self.came(8 + q)
+                self.move(block, block, 24 + k, 8 + q, self.xn).start()
 
     def ready(self):
         d, z, x, c, y = self.pos
-        for q in range(8):
-            self.came(8 + q)
 
         @pl.when(self.home)
         def _():
+            for q in range(8):
+                self.came(8 + q)
             self.stay().wait()
 
         @pl.when(self.away)
         def _():
             for k in range(4):
-                self.came(16 + ((z + k) % 4) * 2 + 1 - x)
+                q = ((z + k) % 4) * 2
+                self.came(16 + q + 1 - x)
+                self.came(8 + q + 1 - x)
+                if not self.wide:
+                    self.came(8 + q + x)
 
     def finish(self):
         block = self.part(self.full, 0)
-        for s in range(1, 16):
+        for s in range(1, 12):
             self.move(block, block, s, 0, self.sib).wait_send()
 
+        @pl.when(self.home)
+        def _():
+            if not self.wide:
+                for s in range(12, 16):
+                    self.move(block, block, s, 0, self.sib).wait_send()
+
         @pl.when(self.away)
         def _():
-            for s in range(16, 24):
+            for s in range(12, 28 if self.wide else 24):
                 self.move(block, block, s, 0, self.sib).wait_send()
 
     def early(self):
@@ -485,19 +501,9 @@
 
 def gather_parts(shards, fulls, relays, chunks, recv, send, pos):
     return [
-        Gather(shards[g], fulls[g], relays[g], cols, recv.at[i], send.at[i], pos)
-        for i, (g, cols) in enumerate(chunks)
+        Gather(shards[g], fulls[g], relays[g], cols, wide, recv.at[i], send.at[i], pos)
+        for i, (g, cols, wide) in enumerate(chunks)
     ]
-
-
-def gather_kernel(chunks, count, *refs):
-    shards, fulls, relays = (refs[i * count : (i + 1) * count] for i in range(3))
-    recv, send = refs[3 * count :]
-    pos = place()
-    greet(chip_peers(pos))
-    parts = gather_parts(shards, fulls, relays, chunks, recv, send, pos)
-    for event in gather_events(parts) + [p.finish for p in parts]:
-        event()
 
 
 def gather_sems(chunks):
@@ -512,21 +518,6 @@
     return [jax.ShapeDtypeStruct((16,) + s.shape[1:], s.dtype) for s in shards] + [
         jax.ShapeDtypeStruct((8,) + s.shape[1:], s.dtype) for s in shards
     ]
-
-
-def gather_weights(shards, chunks, collective_id):
-    count = len(shards)
-    anywhere = pl.BlockSpec(memory_space=pl.ANY)
-    return pl.pallas_call(
-        functools.partial(gather_kernel, chunks, count),
-        out_shape=gather_shapes(shards),
-        in_specs=[anywhere] * count,
-        out_specs=[anywhere] * (2 * count),
-        scratch_shapes=gather_sems(chunks),
-        compiler_params=pltpu.CompilerParams(
-            collective_id=collective_id, has_side_effects=True
-        ),
-    )(*shards)[:count]
 
 
 REDUCE_RECV = 27
@@ -582,62 +573,38 @@
 
                 lax.fori_loop(0, 4, step, 0)
 
-    def second(self):
+    def second(self, k):
         d, z, x, c, y = self.pos
+        zz = (z + 1 + k) % 4
+        q = zz * 2 + 1 - x
 
         @pl.when(self.away)
         def _():
-            def step(k, _):
-                zz = lax.rem(z + 1 + k, 4)
-                q = zz * 2 + 1 - x
-                self.came(q)
-                self.push(self.slot(q), 8 + zz, 16 + k, self.xn).start()
-                return 0
-
-            lax.fori_loop(0, 4, step, 0)
+            self.came(q)
+            self.push(self.slot(q), 8 + zz, 16 + k, self.xn).start()
 
         @pl.when(self.home)
         def _():
-            def over_x(k, _):
-                zz = lax.rem(z + 1 + k, 4)
-                q = zz * 2 + 1 - x
-                self.came(15 + q)
-                self.push(self.slot(15 + q), 23 + zz, 15 + k, self.xn).start()
-                return 0
-
-            lax.fori_loop(0, 4, over_x, 0)
-
-            def step(k, _):
-                zz = lax.rem(z + 1 + k, 4)
-                q = zz * 2 + 1 - x
-                b = 2 * q + c
-                self.came(q)
-                total = self.grad[b, :, self.cols].astype(F32) + self.value(q)
-                self.grad[b, :, self.cols] = total.astype(BF16)
-                self.push(self.rows(b), 8 + zz, 8 + k, self.xn).start()
-                return 0
-
-            lax.fori_loop(0, 4, step, 0)
-
-    def third(self):
+            self.came(15 + q)
+            self.push(self.slot(15 + q), 23 + zz, 15 + k, self.xn).start()
+            b = 2 * q + c
+            self.came(q)
+            total = self.grad[b, :, self.cols].astype(F32) + self.value(q)
+            self.grad[b, :, self.cols] = total.astype(BF16)
+            self.push(self.rows(b), 8 + zz, 8 + k, self.xn).start()
+
+    def third(self, k):
         d, z, x, c, y = self.pos
+        zz = (z + 1 + k) % 4
+        q = zz * 2 + x
 
         @pl.when(self.home)
         def _():
-            def far(k, _):
-                zz = lax.rem(z + 1 + k, 4)
-                q = zz * 2 + x
-                self.came(15 + q)
-                self.came(23 + zz)
-                self.land[15 + q] = (self.value(15 + q) + self.value(23 + zz)).astype(BF16)
-                self.push(self.slot(15 + q), 15 + zz, 19 + k, self.yn).start()
-                return 0
-
-            lax.fori_loop(0, 4, far, 0)
-
-            def step(k, _):
-                zz = lax.rem(z + 1 + k, 4)
-                q = zz * 2 + x
+            self.came(15 + q)
+            self.came(23 + zz)
+            self.land[15 + q] = (self.value(15 + q) + self.value(23 + zz)).astype(BF16)
+            self.push(self.slot(15 + q), 15 + zz, 19 + k, self.yn).start()
+            if k < 3:
                 b = 2 * q + c
                 self.came(q)
                 self.came(8 + zz)
@@ -645,27 +612,20 @@
                 total = total + self.value(q) + self.value(8 + zz)
                 self.grad[b, :, self.cols] = total.astype(BF16)
                 self.push(self.rows(b), 12 + k, 12 + k, (zz * 4 + x * 2 + c, y)).start()
-                return 0
-
-            lax.fori_loop(0, 3, step, 0)
-
-    def fourth(self):
+
+    def fourth(self, k):
         d, z, x, c, y = self.pos
+        zz = (z + 1 + k) % 4
+        q = zz * 2 + x
 
         @pl.when(self.away)
         def _():
-            def step(k, _):
-                zz = lax.rem(z + 1 + k, 4)
-                q = zz * 2 + x
-                self.came(q)
-                self.came(8 + zz)
-                self.came(15 + zz)
-                total = self.value(q) + self.value(8 + zz) + self.value(15 + zz)
-                self.land[q] = total.astype(BF16)
-                self.push(self.slot(q), 12 + k, 20 + k, (zz * 4 + x * 2 + c, y)).start()
-                return 0
-
-            lax.fori_loop(0, 3, step, 0)
+            self.came(q)
+            self.came(8 + zz)
+            self.came(15 + zz)
+            total = self.value(q) + self.value(8 + zz) + self.value(15 + zz)
+            self.land[q] = total.astype(BF16)
+            self.push(self.slot(q), 12 + k, 20 + k, (zz * 4 + x * 2 + c, y)).start()
 
     def fifth(self):
         d, z, x, c, y = self.pos
@@ -692,31 +652,22 @@
             self.push(block, 0, s, self.sib).wait_send()
 
 
-def reduce_events(parts):
+def reduce_events(parts, lead=1):
     n = len(parts)
-    stages = (Reduce.first, Reduce.second, Reduce.third, Reduce.fourth, Reduce.fifth)
-    events = [parts[0].first]
+    events = [p.first for p in parts[:lead]]
     for i in range(n + 3):
-        if i + 1 < n:
-            events.append(parts[i + 1].first)
-        for lag, stage in enumerate(stages[1:]):
-            if 0 <= i - lag < n:
-                events.append(functools.partial(stage, parts[i - lag]))
-    return events + [p.finish for p in parts]
-
-
-def reduce_kernel(chunks, count, *refs):
-    n = len(chunks)
-    grads, outs = refs[:count], refs[count : 2 * count]
-    lands, (recv, send) = refs[2 * count : 2 * count + n], refs[2 * count + n :]
-    pos = place()
-    greet(chip_peers(pos))
-    parts = [
-        Reduce(grads[g], lands[i], outs[g], recv.at[i], send.at[i], pos, cols)
-        for i, (g, cols) in enumerate(chunks)
-    ]
-    for event in reduce_events(parts):
-        event()
+        if i + lead < n:
+            events.append(parts[i + lead].first)
+        for k in range(4):
+            if i < n:
+                events.append(functools.partial(parts[i].second, k))
+            if 0 <= i - 1 < n:
+                events.append(functools.partial(parts[i - 1].third, k))
+            if 0 <= i - 2 < n and k < 3:
+                events.append(functools.partial(parts[i - 2].fourth, k))
+        if 0 <= i - 3 < n:
+            events.append(parts[i - 3].fifth)
+    return events
 
 
 def reduce_scratch(chunks):
@@ -727,139 +678,29 @@
     ]
 
 
-def reduce_grads(grads, chunks, collective_id):
-    count = len(grads)
-    vmem = pl.BlockSpec(memory_space=pltpu.VMEM)
-    return pl.pallas_call(
-        functools.partial(reduce_kernel, chunks, count),
-        out_shape=[jax.ShapeDtypeStruct(g.shape[1:], F32) for g in grads],
-        in_specs=[vmem] * count,
-        out_specs=[vmem] * count,
-        scratch_shapes=reduce_scratch(chunks),
-        compiler_params=pltpu.CompilerParams(
-            collective_id=collective_id, has_side_effects=True, vmem_limit_bytes=63000 * 1024
-        ),
-    )(*grads)
-
-
 class Pump:
     def __init__(self, events):
         self.events, self.next = list(events), 0
 
     def run(self, count=None):
-        stop = len(self.events) if count is None else min(len(self.events), self.next + count)
+        stop = len(self.events)
+        if count is not None:
+            stop = min(stop, self.next + max(0, count))
         for event in self.events[self.next : stop]:
             event()
         self.next = stop
 
-    def loop(self, steps, body, first=0, every=1, count=None):
-        todo = self.events[self.next :][: len(range(first, steps, every))]
-        todo = todo if count is None else todo[:count]
+    def loop(self, steps, body, count=0):
+        todo = self.events[self.next :][:count]
         self.next += len(todo)
 
         def step(i, _):
             for j, event in enumerate(todo):
-                pl.when(i == first + j * every)(event)
+                pl.when(i == j * steps // count)(event)
             body(i)
             return 0
 
         lax.fori_loop(0, steps, step, 0)
-
-
-def first_kernel(
-    chunks, piece_ref, w_ref, bias_ref, shard, mod_ref, silu_ref, full, relay,
-    part, land, mine, other, s1, r1, s2, r2, s3, recv, send,
-):
-    pos = place()
-    d, z, x, c, y = pos
-    sib, _, yn = neighbours(pos)
-    far = (z * 4 + x * 2 + 1 - c, 1 - y)
-    greet([((d + k) % 16, y) for k in range(1, 16)] + [yn, far])
-
-    def piece(k):
-        to = (d + k) % 16
-        return remote(piece_ref.at[to], silu_ref.at[d], s1.at[k], r1.at[d], (to, y))
-
-    def piece_in(k):
-        src = (d + k) % 16
-        return remote(piece_ref.at[src], silu_ref.at[src], s1.at[k], r1.at[src], (src, y))
-
-    for k in range(1, 16):
-        piece(k).start()
-    parts = gather_parts([shard], [full], [relay], chunks, recv, send, pos)
-    pump = Pump(gather_events(parts))
-    pump.run(2)
-    silu_ref[d] = piece_ref[d]
-    for k in range(1, 16):
-        piece_in(k).wait_recv()
-    rows = jnp.concatenate(
-        [silu_ref[2 * q + y].astype(F32)[0:1, :] for q in range(8)], axis=0
-    ).astype(BF16)[:, :72]
-    width = w_ref.shape[1] // 6
-    for j in range(6):
-        cols = slice(j * width, (j + 1) * width)
-        value = jnp.dot(rows, w_ref[:, cols], preferred_element_type=F32)
-        for q in range(8):
-            part[q, :, cols] = value[q : q + 1, :]
-    me = z * 2 + x
-
-    def send_part(k):
-        q = (me + k) % 8
-        return remote(part.at[q], land.at[me], s2.at[k], r2.at[me], (q * 2 + c, y))
-
-    def part_in(k):
-        q = (me + k) % 8
-        return remote(part.at[q], land.at[q], s2.at[k], r2.at[q], (q * 2 + c, y))
-
-    for k in range(1, 8):
-        send_part(k).start()
-    land[me] = part[me]
-    pump.run(6)
-    for k in range(1, 8):
-        part_in(k).wait_recv()
-    total = land[0]
-    for q in range(1, 8):
-        total = total + land[q]
-    mine[...] = total
-    swap = remote(mine, other, s3.at[0], s3.at[1], sib)
-    swap.start()
-    pump.run(3)
-    for k in range(1, 16):
-        piece(k).wait_send()
-    for k in range(1, 8):
-        send_part(k).wait_send()
-    swap.wait()
-    mod_ref[...] = mine[...] + other[...] + bias_ref[...]
-    pump.run()
-    for p in parts:
-        p.finish()
-
-
-def first_stage(pieces, w_mod, bias, shard, chunks, collective_id):
-    vmem, anywhere = pl.BlockSpec(memory_space=pltpu.VMEM), pl.BlockSpec(memory_space=pl.ANY)
-    n = w_mod.shape[1]
-    return pl.pallas_call(
-        functools.partial(first_kernel, chunks),
-        out_shape=[jax.ShapeDtypeStruct((1, n), F32), jax.ShapeDtypeStruct((16, 8, 128), BF16)]
-        + gather_shapes([shard]),
-        in_specs=[vmem] * 3 + [anywhere],
-        out_specs=[vmem] * 2 + [anywhere] * 2,
-        scratch_shapes=[
-            pltpu.VMEM((8, 1, n), F32),
-            pltpu.VMEM((8, 1, n), F32),
-            pltpu.VMEM((1, n), F32),
-            pltpu.VMEM((1, n), F32),
-            pltpu.SemaphoreType.DMA((16,)),
-            pltpu.SemaphoreType.DMA((16,)),
-            pltpu.SemaphoreType.DMA((8,)),
-            pltpu.SemaphoreType.DMA((8,)),
-            pltpu.SemaphoreType.DMA((2,)),
-        ]
-        + gather_sems(chunks),
-        compiler_params=pltpu.CompilerParams(
-            collective_id=collective_id, has_side_effects=True, vmem_limit_bytes=40 * 2**20
-        ),
-    )(pieces, w_mod, bias, shard)[:3]
 
 
 def flat(value):
@@ -914,13 +755,11 @@
         grad[j] = value.reshape(grad.shape[1:]).astype(BF16)
         for i, reducer in enumerate(reducers):
             pl.when(j == i)(reducer.first)
-        pl.when(j == 2)(reducers[0].second)
         return 0
 
     lax.fori_loop(0, 3, weight_grad, 0)
     each3(lambda q, core: send3(q, core).start())
-    pump = Pump(reduce_events(reducers)[:-3])
-    pump.events = [e for e in pump.events if e not in [r.first for r in reducers]][1:]
+    pump = Pump(reduce_events(reducers, 3)[3:])
 
     tile = half // 2
     swap = remote(sent, got, s0.at[4], s0.at[5], sib)
@@ -1123,31 +962,168 @@
 
 
 def forward_kernel(
-    chunks, block, scale, qkv, tokens, vecs, fc1_bias, grad_m, s_proj, s_fc1, s_fc2,
-    out, lse, branch, resid, rows, act, slope, fc2_grad,
-    w_proj, w_fc1, w_fc2, relay_proj, relay_1, relay_2,
-    proj_here, fc1_here, sent, got, sems, recv, send,
+    chunks, block, scale,
+    piece_ref, w_mod, mod_bias, proj_bias, small_in, tokens_in, grad_in,
+    s_qkv, s_proj, s_fc1, s_fc2,
+    mod, silu_ref, fc2_bias_grad,
+    rows_a_out, qkv_out, attended_out, lse_out, branch_out, resid_out, rows_out, act_out,
+    slope_out, fc2_grad_out, grad_m_out, tokens_out, grad_out,
+    w_qkv, w_proj, w_fc1, w_fc2, relay_qkv, relay_proj, relay_1, relay_2,
+    part, land, mine, other, small, tokens, out_grad,
+    rows_a, qkv, out, lse, branch, resid, rows, act, slope, fc2_grad, grad_m,
+    qkv_here, proj_here, weight_here, sent, got,
+    s1, r1, s2, r2, sems, out_sems, recv, send,
 ):
     pos = place()
-    sib = neighbours(pos)[0]
+    d, z, x, c, y = pos
+    sib, _, yn = neighbours(pos)
+    far = (z * 4 + x * 2 + 1 - c, 1 - y)
     half, width = tokens.shape
-    greet(chip_peers(pos))
+    home, away = c == y, c != y
+    greet([((d + k) % 16, y) for k in range(1, 16)] + [yn, far])
+
+    stores = []
+
+    def store(src, dst):
+        copy = pltpu.make_async_copy(src, dst, out_sems.at[len(stores)])
+        copy.start()
+        stores.append(copy)
+
+    def swapped(src, dst, i):
+        there = remote(src, dst, sems.at[i], sems.at[i + 1], far)
+        here = pltpu.make_async_copy(src, dst, sems.at[i + 1])
+
+        def start():
+            pl.when(away)(lambda: there.start())
+            pl.when(home)(lambda: here.start())
+
+        def wait():
+            pl.when(away)(lambda: there.wait())
+            pl.when(home)(lambda: here.wait())
+
+        return start, wait
+
+    def piece(k):
+        to = (d + k) % 16
+        return remote(piece_ref.at[to], silu_ref.at[d], s1.at[k], r1.at[d], (to, y))
+
+    def piece_in(k):
+        src = (d + k) % 16
+        return remote(piece_ref.at[src], silu_ref.at[src], s1.at[k], r1.at[src], (src, y))
+
+    for k in range(1, 16):
+        piece(k).start()
+    small_start, small_wait = swapped(small_in, small, 7)
+    tokens_start, tokens_wait = swapped(tokens_in, tokens, 9)
+    grad_start, grad_wait = swapped(grad_in, out_grad, 11)
+    small_start()
+    tokens_start()
     parts = gather_parts(
-        [s_proj, s_fc1, s_fc2],
-        [w_proj, w_fc1, w_fc2],
-        [relay_proj, relay_1, relay_2],
+        [s_qkv, s_proj, s_fc1, s_fc2],
+        [w_qkv, w_proj, w_fc1, w_fc2],
+        [relay_qkv, relay_proj, relay_1, relay_2],
         chunks,
         recv,
         send,
         pos,
     )
-    first = [i for i, (g, _) in enumerate(chunks) if g < 2]
-    events = gather_events(parts, 3)
+    last_of = {g: parts[i].ready for i, (g, _, _) in enumerate(chunks)}
+    events = gather_events(parts)
     pump = Pump(events)
+
+    def until_ready(g):
+        pump.run(events.index(last_of[g]) + 1 - pump.next)
+
+    pump.run(2)
+    silu_ref[d] = piece_ref[d]
+    for k in range(1, 16):
+        piece_in(k).wait_recv()
+    some = jnp.concatenate(
+        [silu_ref[2 * q + y].astype(F32)[0:1, :] for q in range(8)], axis=0
+    ).astype(BF16)[:, :72]
+    for j in range(6):
+        cols = slice(j * width, (j + 1) * width)
+        value = jnp.dot(some, w_mod[:, cols], preferred_element_type=F32)
+        for q in range(8):
+            part[q, :, cols] = value[q : q + 1, :]
+    me = z * 2 + x
+
+    def send_part(k):
+        q = (me + k) % 8
+        return remote(part.at[q], land.at[me], s2.at[k], r2.at[me], (q * 2 + c, y))
+
+    def part_in(k):
+        q = (me + k) % 8
+        return remote(part.at[q], land.at[q], s2.at[k], r2.at[q], (q * 2 + c, y))
+
+    for k in range(1, 8):
+        send_part(k).start()
+    land[me] = part[me]
+    pump.run(4)
+    for k in range(1, 8):
+        part_in(k).wait_recv()
+    total = land[0]
+    for q in range(1, 8):
+        total = total + land[q]
+    mine[...] = total
+    swap = remote(mine, other, sems.at[13], sems.at[14], sib)
+    swap.start()
     pump.run(3)
+    for k in range(1, 16):
+        piece(k).wait_send()
+    for k in range(1, 8):
+        send_part(k).wait_send()
+    swap.wait()
+    mod[...] = mine[...] + other[...] + mod_bias[...]
+    shift_a, scale_a, gate_a, shift_m, scale_m, gate_m = [
+        mod[:, i * width : (i + 1) * width] for i in range(6)
+    ]
+    small_wait()
+    tokens_wait()
+
+    tall = half // 4
+
+    def norm_rows(value, shift, scale_up):
+        center = value - jnp.mean(value, axis=-1, keepdims=True)
+        spread = jnp.mean(center * center, axis=-1, keepdims=True)
+        normed = center * lax.rsqrt(spread + 1e-06) * (1.0 + scale_up) + shift
+        return normed.astype(BF16)
+
+    def first_norm(i, _):
+        own = pl.ds(pl.multiple_of(i * tall, tall), tall)
+        rows_a[own, :] = norm_rows(tokens[own, :].astype(F32), shift_a, scale_a)
+        return 0
+
+    lax.fori_loop(0, 4, first_norm, 0)
+    share = remote(rows_a.at[:half], rows_a.at[half:], sems.at[5], sems.at[6], sib)
+    share.start()
+    until_ready(0)
+    heads = qkv.shape[0] // 3
+    cols = heads * qkv.shape[1]
+    load = pltpu.make_async_copy(w_qkv, qkv_here, sems.at[0])
+    load.start()
+    grad_start()
+    pump.run(2)
+    load.wait()
+    share.wait()
+    store(rows_a, rows_a_out)
+    store(tokens, tokens_out)
+    row = lax.broadcasted_iota(jnp.int32, (8, 2 * half), 0)
+    for j in range(3):
+        weight = flat(qkv_here[:, :, j * cols : (j + 1) * cols])
+        value = product(weight, rows_a[...], 0, 1)
+        if j != 1:
+            pick = jnp.where(row == j // 2, 1.0, 0.0).astype(BF16)
+            value = value + product(small[:, :cols], pick, 0, 0)
+        value = value.reshape((heads,) + qkv.shape[1:])
+        qkv[pl.ds(j * heads, heads)] = value.astype(BF16)
+        pump.run(2)
+    store(qkv, qkv_out)
     steps, body = attention_step(qkv, out, lse, block, scale)
-    pump.loop(steps, body, first=2)
-    pump.run(events.index(parts[0].ready) + 1 - pump.next)
+    pump.loop(steps, body, 16)
+    store(out, attended_out)
+    store(lse, lse_out)
+    until_ready(1)
 
     load = pltpu.make_async_copy(w_proj, proj_here, sems.at[0])
     load.start()
@@ -1157,101 +1133,148 @@
 
     def project(i):
         cols = pl.ds(pl.multiple_of(i * tile, tile), tile)
-        heads = flat(out[:, :, cols])
-        return product(heads, flat(proj_here[...]), 0, 1)
+        return product(flat(out[:, :, cols]), flat(proj_here[...]), 0, 1)
 
     def other_rows(i, _):
         sent[pl.ds(pl.multiple_of(i * tile, tile), tile), :] = project(i + 2).astype(BF16)
         return 0
 
     def own_rows(i, _):
-        branch[pl.ds(pl.multiple_of(i * tile, tile), tile), :] = project(i) + vecs[3:4, :]
+        branch[pl.ds(pl.multiple_of(i * tile, tile), tile), :] = project(i) + proj_bias[...]
         return 0
 
     lax.fori_loop(0, 2, other_rows, 0)
     swap.start()
     lax.fori_loop(0, 2, own_rows, 0)
-    pump.run(4)
+    pump.run(2)
+    grad_wait()
+    store(out_grad, grad_out)
+
+    def gated(i, total):
+        own = pl.ds(pl.multiple_of(i * tall, tall), tall)
+        value = (out_grad[own, :].astype(F32) * gate_m).astype(BF16)
+        grad_m[own, :] = value
+        return total + jnp.sum(value.astype(F32), axis=0, keepdims=True)
+
+    fc2_bias_grad[...] = lax.fori_loop(0, 4, gated, jnp.zeros((1, width), F32))
+    share_m = remote(grad_m.at[:half], grad_m.at[half:], sems.at[15], sems.at[16], sib)
+    share_m.start()
     swap.wait()
     share = remote(rows.at[:half], rows.at[half:], sems.at[3], sems.at[4], sib)
-    piece = half // 4
 
     def norm(i, _):
-        part = pl.ds(pl.multiple_of(i * piece, piece), piece)
-        total = branch[part, :] + got[part, :].astype(F32)
-        branch[part, :] = total
-        mid = tokens[part, :].astype(F32) + vecs[0:1, :] * total
-        resid[part, :] = mid
-        center = mid - jnp.mean(mid, axis=-1, keepdims=True)
-        spread = jnp.mean(center * center, axis=-1, keepdims=True)
-        normed = center * lax.rsqrt(spread + 1e-06) * (1.0 + vecs[2:3, :]) + vecs[1:2, :]
-        rows[part, :] = normed.astype(BF16)
+        own = pl.ds(pl.multiple_of(i * tall, tall), tall)
+        total = branch[own, :] + got[own, :].astype(F32)
+        branch[own, :] = total
+        mid = tokens[own, :].astype(F32) + gate_a * total
+        resid[own, :] = mid
+        rows[own, :] = norm_rows(mid, shift_m, scale_m)
         return 0
 
     lax.fori_loop(0, 4, norm, 0)
     share.start()
-    pump.run(events.index(parts[first[-1]].ready) + 1 - pump.next)
-
-    load = pltpu.make_async_copy(w_fc1, fc1_here, sems.at[0])
+    store(branch, branch_out)
+    store(resid, resid_out)
+    until_ready(2)
+
+    load = pltpu.make_async_copy(w_fc1, weight_here, sems.at[0])
     load.start()
     load.wait()
     share.wait()
+    store(rows, rows_out)
     n = 256
+    hidden_steps = act.shape[1] // n
 
     def hidden(i):
         cols = pl.ds(pl.multiple_of(i * n, n), n)
-        weight = flat(fc1_here[:, :, cols])
-        value, rate = gelu_and_slope(product(rows[...], weight, 1, 0) + fc1_bias[:, cols])
+        bias = small[:, cols].astype(F32)[2:3, :]
+        value, rate = gelu_and_slope(
+            product(rows[...], flat(weight_here[:, :, cols]), 1, 0) + bias
+        )
         act[:, cols] = value.astype(BF16)
         slope[:, cols] = rate.astype(BF16)
 
-    pump.loop(act.shape[1] // n, hidden)
+    pump.loop(hidden_steps, hidden, hidden_steps)
+    store(act, act_out)
+    store(slope, slope_out)
+    share_m.wait()
+    store(grad_m, grad_m_out)
 
     def weight_grad(i):
         cols = pl.ds(pl.multiple_of(i * n, n), n)
         value = product(grad_m[...], act[:, cols], 0, 0)
         fc2_grad[:, :, cols] = value.reshape(fc2_grad.shape[:2] + (n,)).astype(BF16)
 
-    pump.loop(act.shape[1] // n, weight_grad)
+    pump.loop(hidden_steps, weight_grad, hidden_steps)
+    store(fc2_grad, fc2_grad_out)
     pump.run()
     for p in parts:
         p.finish()
-
-
-def forward_stage(qkv, tokens, vecs, fc1_bias, grad_m, shards, chunks, collective_id, block=512):
-    heads, size, count = qkv.shape[0] // 3, qkv.shape[1], qkv.shape[2]
+    for copy in stores:
+        copy.wait()
+
+
+def forward_stage(
+    pieces, w_mod, mod_bias, proj_bias, small, tokens, out_grad, shards, size, chunks,
+    collective_id, block=512,
+):
     half, width = tokens.shape
-    owned, cols = shards[0].shape[1:]
-    hidden = shards[1].shape[2]
+    count = 2 * half
+    owned, cols = shards[1].shape[1:]
+    heads = cols // size
+    hidden = shards[2].shape[2]
+    n = w_mod.shape[1]
     vmem, anywhere = pl.BlockSpec(memory_space=pltpu.VMEM), pl.BlockSpec(memory_space=pl.ANY)
-    shape = jax.ShapeDtypeStruct
+    shape, dma = jax.ShapeDtypeStruct, pltpu.SemaphoreType.DMA
+    kept = [
+        ((count, width), BF16),
+        ((3 * heads, size, count), BF16),
+        ((heads, size, count), BF16),
+        ((heads, 1, count), F32),
+        ((half, width), F32),
+        ((half, width), F32),
+        ((count, width), BF16),
+        ((count, hidden), BF16),
+        ((count, hidden), BF16),
+        ((16, owned, hidden), BF16),
+        ((count, width), BF16),
+    ]
+    swap = ((half, width), BF16)
     return pl.pallas_call(
         functools.partial(forward_kernel, chunks, block, size**-0.5),
-        out_shape=[
-            shape((heads, size, count), BF16),
-            shape((heads, 1, count), F32),
-            shape((half, width), F32),
-            shape((half, width), F32),
-            shape((count, width), BF16),
-            shape((count, hidden), BF16),
-            shape((count, hidden), BF16),
-            shape((16, owned, hidden), BF16),
+        out_shape=[shape((1, n), F32), shape((16, 8, 128), BF16), shape((1, width), F32)]
+        + [shape(*k) for k in kept + [swap, swap]]
+        + gather_shapes(shards),
+        in_specs=[vmem] * 5 + [anywhere] * 6,
+        out_specs=[vmem] * 3 + [anywhere] * 21,
+        scratch_shapes=[
+            pltpu.VMEM((8, 1, n), F32),
+            pltpu.VMEM((8, 1, n), F32),
+            pltpu.VMEM((1, n), F32),
+            pltpu.VMEM((1, n), F32),
+            pltpu.VMEM(small.shape, BF16),
+            pltpu.VMEM(*swap),
+            pltpu.VMEM(*swap),
         ]
-        + gather_shapes(shards),
-        in_specs=[vmem] * 5 + [anywhere] * 3,
-        out_specs=[vmem] * 8 + [anywhere] * 6,
-        scratch_shapes=[
+        + [pltpu.VMEM(*k) for k in kept]
+        + [
+            pltpu.VMEM((16, owned, 3 * cols), BF16),
             pltpu.VMEM((16, owned, cols), BF16),
             pltpu.VMEM((16, owned, hidden), BF16),
-            pltpu.VMEM((half, width), BF16),
-            pltpu.VMEM((half, width), BF16),
-            pltpu.SemaphoreType.DMA((5,)),
+            pltpu.VMEM(*swap),
+            pltpu.VMEM(*swap),
+            dma((16,)),
+            dma((16,)),
+            dma((8,)),
+            dma((8,)),
+            dma((17,)),
+            dma((13,)),
         ]
         + gather_sems(chunks),
         compiler_params=pltpu.CompilerParams(
-            collective_id=collective_id, has_side_effects=True, vmem_limit_bytes=63000 * 1024
+            collective_id=collective_id, has_side_effects=True, vmem_limit_bytes=64500 * 1024
         ),
-    )(qkv, tokens, vecs, fc1_bias, grad_m, *shards)[:11]
+    )(pieces, w_mod, mod_bias, proj_bias, small, tokens, out_grad, *shards)[:20]
 
 
 def attention_back_step(qkv, grad, out, lse, result, key_sum, value_sum, block, scale):
@@ -1288,42 +1311,294 @@
     return heads * blocks, body
 
 
-def attention_backward_kernel(chunks, count, block, scale, qkv, grad, out, lse, *refs):
+def loader(sems):
+    count = iter(range(64))
+
+    def load(src, dst):
+        copy = pltpu.make_async_copy(src, dst, sems.at[next(count)])
+        copy.start()
+        return copy.wait
+
+    return load
+
+
+def hidden_back_kernel(
+    chunks, bias, grad_m_in, act_in, slope_in, rows_in, fc2_grad_in, w_fc2, w_fc1,
+    fc1_bias_grad, fc2_out, fc1_grad_out, branch_out, ngrad_out,
+    grad_m, act, slope, rows, fc2_grad, fc1_grad, branch, ngrad,
+    weight, pre_grad, sent1, got1, sent2, got2, *rest,
+):
     n = len(chunks)
-    grads, result, outs = refs[:count], refs[count], refs[count + 1 : 2 * count + 1]
-    key_sum, value_sum = refs[2 * count + 1 : 2 * count + 3]
-    rest = refs[2 * count + 3 :]
-    lands, (recv, send) = rest[:n], rest[n:]
+    lands, (sems, load_sems, recv, send) = rest[:n], rest[n:]
     pos = place()
+    sib = neighbours(pos)[0]
+    half, width = branch.shape
+    hidden = act.shape[1]
+    load = loader(load_sems)
+    grad_ready = load(fc2_grad_in, fc2_grad)
+    weight_ready = load(w_fc2, weight)
+    m_ready = load(grad_m_in, grad_m)
+    slope_ready = load(slope_in, slope)
+    act_ready = load(act_in, act)
+    rows_ready = load(rows_in, rows)
     greet(chip_peers(pos))
     parts = [
-        Reduce(grads[g], lands[i], outs[g], recv.at[i], send.at[i], pos, cols)
+        Reduce(fc2_grad, lands[i], fc2_out, recv.at[i], send.at[i], pos, cols)
+        for i, cols in enumerate(chunks)
+    ]
+    pump = Pump(reduce_events(parts))
+    grad_ready()
+    pump.run(2)
+    weight_ready()
+    m_ready()
+    slope_ready()
+    tile = 256
+
+    def into_hidden(i):
+        cols = pl.ds(pl.multiple_of(i * tile, tile), tile)
+        value = product(grad_m[...], flat(weight[:, :, cols]), 1, 0)
+        value = (value * slope[:, cols].astype(F32)).astype(BF16)
+        pre_grad[:, cols] = value
+        fc1_bias_grad[:, cols] = jnp.sum(value.astype(F32), axis=0, keepdims=True)
+
+    pump.loop(hidden // tile, into_hidden, 9)
+
+    def out_of_hidden(source, sent, own, extra):
+        def body(i):
+            turn = lax.rem(i + 2, 4)
+            part = pl.ds(pl.multiple_of(turn * tile, tile), tile)
+            value = product(source[part, :], flat(weight[...]), 1, 1)
+
+            @pl.when(i < 2)
+            def _():
+                sent[pl.ds(pl.multiple_of(i * tile, tile), tile), :] = value.astype(BF16)
+
+            @pl.when(i >= 2)
+            def _():
+                own[part, :] = value + extra
+
+        return body
+
+    swap1 = remote(sent1, got1, sems.at[1], sems.at[2], sib)
+    swap2 = remote(sent2, got2, sems.at[3], sems.at[4], sib)
+    act_ready()
+    pump.loop(4, out_of_hidden(act, sent1, branch, bias[...]), 8)
+    swap1.start()
+    weight_ready = load(w_fc1, weight)
+    pump.run(2)
+    weight_ready()
+    pump.loop(4, out_of_hidden(pre_grad, sent2, ngrad, 0.0), 8)
+    swap2.start()
+
+    def join(own, got):
+        def body(i, _):
+            part = pl.ds(pl.multiple_of(i * tile, tile), tile)
+            own[part, :] += got[part, :].astype(F32)
+            return 0
+
+        lax.fori_loop(0, half // tile, body, 0)
+
+    swap1.wait()
+    join(branch, got1)
+    stored = [load(branch, branch_out)]
+    rows_ready()
+
+    def weight_grad(i):
+        cols = pl.ds(pl.multiple_of(i * tile, tile), tile)
+        value = product(rows[...], pre_grad[:, cols], 0, 0)
+        fc1_grad[:, :, cols] = value.reshape(fc1_grad.shape[:2] + (tile,)).astype(BF16)
+
+    pump.loop(hidden // tile, weight_grad, 9)
+    stored.append(load(fc1_grad, fc1_grad_out))
+    swap2.wait()
+    join(ngrad, got2)
+    stored.append(load(ngrad, ngrad_out))
+    pump.run()
+    for p in parts:
+        p.finish()
+    for wait in stored:
+        wait()
+
+
+def hidden_back(bias, grad_m, act, slope, rows, fc2_grad, w_fc2, w_fc1, chunks, collective_id):
+    vmem, anywhere = pl.BlockSpec(memory_space=pltpu.VMEM), pl.BlockSpec(memory_space=pl.ANY)
+    shape = jax.ShapeDtypeStruct
+    count, width = grad_m.shape
+    half, hidden = count // 2, act.shape[1]
+    swap = pltpu.VMEM((half, width), BF16)
+    sums = pltpu.VMEM((half, width), F32)
+    land = reduce_scratch([(0, cols) for cols in chunks])
+    return pl.pallas_call(
+        functools.partial(hidden_back_kernel, chunks),
+        out_shape=[
+            shape((1, hidden), F32),
+            shape(fc2_grad.shape[1:], F32),
+            shape(fc2_grad.shape, BF16),
+            shape((half, width), F32),
+            shape((half, width), F32),
+        ],
+        in_specs=[vmem] + [anywhere] * 7,
+        out_specs=[vmem] * 2 + [anywhere] * 3,
+        scratch_shapes=[
+            pltpu.VMEM((count, width), BF16),
+            pltpu.VMEM((count, hidden), BF16),
+            pltpu.VMEM((count, hidden), BF16),
+            pltpu.VMEM((count, width), BF16),
+            pltpu.VMEM(fc2_grad.shape, BF16),
+            pltpu.VMEM(fc2_grad.shape, BF16),
+            sums,
+            sums,
+            pltpu.VMEM(fc2_grad.shape, BF16),
+            pltpu.VMEM((count, hidden), BF16),
+            swap,
+            swap,
+            swap,
+            swap,
+        ]
+        + land[: len(chunks)]
+        + [pltpu.SemaphoreType.DMA((5,)), pltpu.SemaphoreType.DMA((12,))]
+        + land[len(chunks) :],
+        compiler_params=pltpu.CompilerParams(
+            collective_id=collective_id, has_side_effects=True, vmem_limit_bytes=64500 * 1024
+        ),
+    )(bias, grad_m, act, slope, rows, fc2_grad, w_fc2, w_fc1)
+
+
+def norm_back_rows(value, g, scale_up):
+    center = value - jnp.mean(value, axis=-1, keepdims=True)
+    rate = lax.rsqrt(jnp.mean(center * center, axis=-1, keepdims=True) + 1e-06)
+    normed = center * rate
+    e = g * scale_up
+    inner = jnp.mean(e * normed, axis=-1, keepdims=True)
+    return rate * (e - jnp.mean(e, axis=-1, keepdims=True) - normed * inner), normed
+
+
+def row_sum(value):
+    return jnp.sum(value, axis=0, keepdims=True)
+
+
+def attention_back_kernel(
+    chunks, block, scale, vecs, resid_in, ngrad_in, out_grad_in, branch_in, w_proj_in, qkv_in,
+    out_in, lse_in, fc1_grad_in,
+    sums, fc1_out, proj_out, resid_grad_out, result_out,
+    resid, ngrad, out_grad, branch, w_proj, qkv, out, lse, fc1_grad, resid_grad, result,
+    rows, grad, proj_grad, key_sum, value_sum, *rest,
+):
+    n = len(chunks)
+    lands, (sems, load_sems, recv, send) = rest[:n], rest[n:]
+    pos = place()
+    sib = neighbours(pos)[0]
+    half, width = resid.shape
+    load = loader(load_sems)
+    first = [load(fc1_grad_in, fc1_grad)]
+    norm_ready = [
+        load(*pair)
+        for pair in ((ngrad_in, ngrad), (resid_in, resid), (out_grad_in, out_grad), (branch_in, branch))
+    ]
+    late = [load(w_proj_in, w_proj), load(out_in, out), load(qkv_in, qkv), load(lse_in, lse)]
+    greet(chip_peers(pos))
+    parts = [
+        Reduce(
+            (fc1_grad, proj_grad)[g],
+            lands[i],
+            (fc1_out, proj_out)[g],
+            recv.at[i],
+            send.at[i],
+            pos,
+            cols,
+        )
         for i, (g, cols) in enumerate(chunks)
     ]
+    pump = Pump(reduce_events(parts))
+    for wait in first:
+        wait()
+    pump.run(2)
+    for wait in norm_ready:
+        wait()
+    tall = half // 4
+    scale_up = 1.0 + vecs[1:2, :]
+
+    def norm(i, total):
+        part = pl.ds(pl.multiple_of(i * tall, tall), tall)
+        g = ngrad[part, :]
+        back, normed = norm_back_rows(resid[part, :], g, scale_up)
+        value = out_grad[part, :].astype(F32) + back
+        resid_grad[part, :] = value
+        low = (value * vecs[0:1, :]).astype(BF16)
+        rows[part, :] = low
+        terms = (g, g * normed, value * branch[part, :], low.astype(F32))
+        return tuple(t + row_sum(v) for t, v in zip(total, terms))
+
+    total = lax.fori_loop(0, 4, norm, (jnp.zeros((1, width), F32),) * 4)
+    share = remote(rows.at[:half], rows.at[half:], sems.at[0], sems.at[1], sib)
+    share.start()
+    stored = [load(resid_grad, resid_grad_out)]
+    for i in range(4):
+        sums[i : i + 1, :] = total[i]
+    pump.run(1)
+    for wait in late:
+        wait()
+    share.wait()
+    tile = 256
+
+    def attended(i):
+        cols = pl.ds(pl.multiple_of(i * tile, tile), tile)
+        value = product(flat(w_proj[...]), rows[cols, :], 0, 1)
+        grad[:, :, cols] = value.reshape(grad.shape[:2] + (tile,)).astype(BF16)
+
+    pump.loop(2 * half // tile, attended, 4)
+    value = product(rows[...], flat(out[...]), 0, 1)
+    proj_grad[...] = value.reshape(proj_grad.shape).astype(BF16)
     steps, body = attention_back_step(
         qkv, grad, out, lse, result, key_sum, value_sum, block, scale
     )
-    pump = Pump(reduce_events(parts))
-    pump.run(2)
-    pump.loop(steps, body, first=4, every=4)
+    pump.loop(steps, body, 28)
+    stored.append(load(result, result_out))
     pump.run()
-
-
-def attention_backward(qkv, grad, out, lse, grads, chunks, collective_id, block=512):
-    count = len(grads)
-    heads, size, tokens = qkv.shape[0] // 3, qkv.shape[1], qkv.shape[2]
-    vmem = pl.BlockSpec(memory_space=pltpu.VMEM)
+    for p in parts:
+        p.finish()
+    for wait in stored:
+        wait()
+
+
+def attention_back(
+    vecs, resid, ngrad, out_grad, branch, w_proj, qkv, out, lse, fc1_grad, chunks, collective_id,
+    block=512,
+):
+    heads, size, count = out.shape
+    half, width = resid.shape
+    owned, cols = w_proj.shape[1:]
+    vmem, anywhere = pl.BlockSpec(memory_space=pltpu.VMEM), pl.BlockSpec(memory_space=pl.ANY)
+    shape = jax.ShapeDtypeStruct
+    land = reduce_scratch(chunks)
+    arrays = (resid, ngrad, out_grad, branch, w_proj, qkv, out, lse, fc1_grad)
+    made = [((half, width), F32), (qkv.shape, BF16)]
     return pl.pallas_call(
-        functools.partial(attention_backward_kernel, chunks, count, block, size**-0.5),
-        out_shape=[jax.ShapeDtypeStruct(qkv.shape, BF16)]
-        + [jax.ShapeDtypeStruct(g.shape[1:], F32) for g in grads],
-        in_specs=[vmem] * (4 + count),
-        out_specs=[vmem] * (1 + count),
-        scratch_shapes=[pltpu.VMEM((size, tokens), F32)] * 2 + reduce_scratch(chunks),
+        functools.partial(attention_back_kernel, chunks, block, size**-0.5),
+        out_shape=[
+            shape((4, width), F32),
+            shape(fc1_grad.shape[1:], F32),
+            shape((owned, cols), F32),
+        ]
+        + [shape(*m) for m in made],
+        in_specs=[vmem] + [anywhere] * 9,
+        out_specs=[vmem] * 3 + [anywhere] * 2,
+        scratch_shapes=[pltpu.VMEM(a.shape, a.dtype) for a in arrays]
+        + [pltpu.VMEM(*m) for m in made]
+        + [
+            pltpu.VMEM((count, width), BF16),
+            pltpu.VMEM(out.shape, BF16),
+            pltpu.VMEM((16, owned, cols), BF16),
+            pltpu.VMEM((size, count), F32),
+            pltpu.VMEM((size, count), F32),
+        ]
+        + land[: len(chunks)]
+        + [pltpu.SemaphoreType.DMA((2,)), pltpu.SemaphoreType.DMA((12,))]
+        + land[len(chunks) :],
         compiler_params=pltpu.CompilerParams(
-            collective_id=collective_id, has_side_effects=True, vmem_limit_bytes=63000 * 1024
+            collective_id=collective_id, has_side_effects=True, vmem_limit_bytes=64500 * 1024
         ),
-    )(qkv, grad, out, lse, *grads)
+    )(vecs, *arrays)
 
 
 def index_of(z, x, c, y):
@@ -1397,36 +1672,28 @@
         silu_cond.astype(BF16).reshape(16, 1, owned), ((0, 0), (0, 7), (0, 128 - owned))
     )
     s_qkv = query_key_value_weight.reshape(1, owned, 3 * cols)
-    modulation, silu_owned, w_qkv = first_stage(
-        pieces, mod_weight, mod_bias.astype(F32)[None], s_qkv, [(0, p) for p in columns(3 * cols, 896)], 2
-    )
-    w_qkv = w_qkv.reshape(width, 3 * cols)
-    shift_a, scale_a, gate_a, shift_m, scale_m, gate_m = [
-        modulation[:, i * width : (i + 1) * width] for i in range(6)
+    small = jnp.stack(
+        [
+            jnp.pad(qkv_bias[0], (0, hidden - cols)),
+            jnp.pad(qkv_bias[1], (0, hidden - cols)),
+            first_hidden_bias,
+        ]
+    )
+    small = jnp.pad(small, ((0, 5), (0, 0)))
+    shards = [
+        s_qkv,
+        attention_out_weight.T.reshape(1, owned, cols),
+        first_hidden_weight.reshape(1, owned, hidden),
+        second_hidden_weight.T.reshape(1, owned, hidden),
     ]
-
-    bias_rows = jnp.concatenate([qkv_bias.reshape(-1), first_hidden_bias]).reshape(-1, width)
-    carried = trade(jnp.concatenate([tokens.reshape(half, width), bias_rows], axis=0))
-    tokens_here = carried[:half].astype(F32)
-    biases = carried[half:].reshape(-1)
-    q_bias, v_bias, fc1_bias = biases[:cols], biases[cols : 2 * cols], biases[2 * cols :]
-    grad_out = trade(out_grad.reshape(half, width)).astype(F32)
-
-    s_proj = attention_out_weight.T.reshape(1, owned, cols)
-    s_fc1 = first_hidden_weight.reshape(1, owned, hidden)
-    s_fc2 = second_hidden_weight.T.reshape(1, owned, hidden)
-    chunks = [(0, None)] + [(g, p) for g in (1, 2) for p in columns(hidden, 1152)]
-
-    normed_a = modulate(tokens_here, shift_a, scale_a)
-    rows_a = both_halves(normed_a.astype(BF16))
-    qkv_shift = jnp.concatenate([q_bias, jnp.zeros_like(q_bias), v_bias]).astype(F32)
-    qkv = product(w_qkv, rows_a, 0, 1) + qkv_shift[:, None]
-    qkv = qkv.astype(BF16).reshape(3 * heads_here, head_size, 2 * half)
-    grad_m_own = (grad_out * gate_m).astype(BF16)
-    fc2_bias_part = jnp.sum(grad_m_own, axis=0, dtype=F32)
-    grad_m = both_halves(grad_m_own)
-    vecs = jnp.concatenate([gate_a, shift_m, scale_m, attention_out_bias.astype(F32)[None]])
+    chunks = [(0, p, True) for p in columns(3 * cols, 896)] + [(1, None, False)]
+    chunks += [(g, p, False) for g in (2, 3) for p in columns(hidden, 1152)]
     (
+        modulation,
+        silu_owned,
+        fc2_bias_part,
+        rows_a,
+        qkv,
         attended,
         log_totals,
         branch_a,
@@ -1435,58 +1702,64 @@
         act_low,
         slope,
         fc2_grad,
+        grad_m,
+        tokens_here,
+        out_grad_here,
+        w_qkv,
         w_proj,
         w_fc1,
         w_fc2,
     ) = forward_stage(
+        pieces,
+        mod_weight,
+        mod_bias.astype(F32)[None],
+        attention_out_bias.astype(F32)[None],
+        small,
+        tokens.reshape(half, width),
+        out_grad.reshape(half, width),
+        shards,
+        head_size,
+        chunks,
+        2,
+    )
+    shift_a, scale_a, gate_a, shift_m, scale_m, gate_m = [
+        modulation[:, i * width : (i + 1) * width] for i in range(6)
+    ]
+    grad_out = out_grad_here.astype(F32)
+
+    fc1_bias_part, fc2_out, fc1_grad, branch_m, normed_m_grad = hidden_back(
+        second_hidden_bias.astype(F32)[None],
+        grad_m,
+        act_low,
+        slope,
+        rows_m,
+        fc2_grad,
+        w_fc2,
+        w_fc1,
+        columns(hidden, 768),
+        4,
+    )
+    output = (resid_mid + gate_m * branch_m).astype(BF16)
+    gate_m_grad = jnp.sum(grad_out * branch_m, axis=0)
+    sums, fc1_out, proj_out, resid_grad, qkv_grad = attention_back(
+        jnp.concatenate([gate_a, scale_m]),
+        resid_mid,
+        normed_m_grad,
+        out_grad_here,
+        branch_a,
+        w_proj,
         qkv,
-        carried[:half],
-        vecs,
-        fc1_bias.astype(F32)[None],
-        grad_m,
-        [s_proj, s_fc1, s_fc2],
-        chunks,
-        3,
-    )
-    w_proj, w_fc1, w_fc2 = (w.reshape(width, -1) for w in (w_proj, w_fc1, w_fc2))
-    attended_rows = attended.reshape(cols, 2 * half)
-    _, norm_m_back = jax.vjp(modulate, resid_mid, shift_m, scale_m)
-    branch_m = own_sum(
-        jnp.einsum("rf,df->rd", act_low, w_fc2, preferred_element_type=F32)
-    ) + second_hidden_bias.astype(F32)
-    output = (resid_mid + gate_m * branch_m).astype(BF16)
-
-    gate_m_grad = jnp.sum(grad_out * branch_m, axis=0)
-    act_grad = jnp.dot(grad_m, w_fc2, preferred_element_type=F32)
-    pre_grad = (act_grad * slope.astype(F32)).astype(BF16)
-    fc1_bias_part = jnp.sum(pre_grad, axis=0, dtype=F32)
-    fc1_grad = jnp.einsum("rd,rf->df", rows_m, pre_grad, preferred_element_type=F32).astype(BF16)
-    normed_m_grad = own_sum(
-        jnp.einsum("rf,df->rd", pre_grad, w_fc1, preferred_element_type=F32)
-    )
-    resid_part, shift_m_grad, scale_m_grad = norm_m_back(normed_m_grad)
-    resid_grad = grad_out + resid_part
-
-    gate_a_grad = jnp.sum(resid_grad * branch_a, axis=0)
-    grad_a_own = (resid_grad * gate_a).astype(BF16)
-    proj_bias_part = jnp.sum(grad_a_own, axis=0, dtype=F32)
-    grad_a = both_halves(grad_a_own)
-    proj_grad = product(grad_a, attended_rows, 0, 1).astype(BF16)
-    attended_grad = product(w_proj, grad_a, 0, 1).astype(BF16)
-    chunks = [(g, p) for g in (0, 1) for p in columns(hidden, 768)] + [(2, (0, cols))]
-    qkv_grad, fc2_out, fc1_out, proj_out = attention_backward(
-        qkv,
-        attended_grad.reshape(attended.shape),
         attended,
         log_totals,
-        [fc2_grad, fc1_grad.reshape(16, owned, -1), proj_grad.reshape(16, owned, -1)],
-        chunks,
-        4,
-    )
+        fc1_grad,
+        [(0, p) for p in columns(hidden, 768)] + [(1, (0, cols))],
+        5,
+    )
+    shift_m_grad, scale_m_grad, gate_a_grad, proj_bias_part = (sums[i] for i in range(4))
     qkv_bias_part = jnp.sum(qkv_grad, axis=2, dtype=F32)
     half_part = jnp.concatenate(
         [
-            fc1_bias_part,
+            fc1_bias_part[0],
             qkv_bias_part[:heads_here].reshape(-1),
             qkv_bias_part[2 * heads_here :].reshape(-1),
         ]
@@ -1500,12 +1773,12 @@
         ],
         axis=1,
     )
-    wide_part = jnp.concatenate([fc2_bias_part, proj_bias_part])[None]
+    wide_part = jnp.concatenate([fc2_bias_part[0], proj_bias_part])[None]
     tokens_grad, qkv_out, mod_weight_grad, mod_bias_grad, silu_grad, wide, narrow = last_stage(
         rows_a,
         qkv_grad,
-        w_qkv,
-        carried[:half],
+        w_qkv.reshape(width, 3 * cols),
+        tokens_here,
         resid_grad,
         scale_a,
         mod_part,

time: 548 us -> 471 us (0.86)
  matrix products: 46 us -> 0 us
  other arithmetic: 40 us -> 15.1 us
  starting transfers between devices: 16.8 us -> 5.56 us
  waiting for transfers between devices: 6.01 us -> 16 us
    pallas_call x2, Pallas kernels: 191 us -> 133 us  [the longest x1 73.6 us: attention_back(): pl.pallas_call(functools.partial(attention_back_kernel, chunks, block, si...]
    pallas_call x1, Pallas kernels: 140 us -> 196 us  [forward_stage(): pl.pallas_call(functools.partial(forward_kernel, chunks, block, size ** (...]
    dot_general x7 -> x0, matrix products: 46 us -> none  [the longest x3 14.5 us: product(): lax.dot_general(a, b, (((ca,), (cb,)), ((), ())), preferred_element_type=...]
    concatenate x6 -> x2, other arithmetic: 11.8 us -> 0.62 us  [the longest x1 0.61 us: on_device_chip(): jnp.concatenate([gate_a, scale_m])]
    ppermute x4 -> x2, starting transfers between devices: 15.7 us -> 5.56 us  [trade(): moved = lax.ppermute(value, AXES, latent_pairs())]
    ppermute x4 -> x2, waiting for transfers between devices: 6 us -> 16 us  [trade(): moved = lax.ppermute(value, AXES, latent_pairs())]
    reduce_sum x8 -> x0, other arithmetic: 8.97 us -> none  [the longest x1 3.8 us: on_device_chip(): fc2_bias_part = jnp.sum(grad_m_own, axis=0, dtype=F32)]
  transfers between devices with their start and end apart: 9 -> 2, of which waited for: 1 -> 2; matrix products, arithmetic and copies ran while one was open for 12% -> 2% of each run, Pallas kernels for 50% -> 0%
where the time goes in v4:
time: 471 us; the launch traced here: 466 us
  Pallas kernels  409 us (87%)
  local copies, waits for them, and re-layouts  19.9 us (4%)
  waiting for transfers between devices  16 us (3%)
  other arithmetic  15.1 us (3%)
  starting transfers between devices  5.56 us (1%)
    pallas_call x1, Pallas kernels, forward_stage(): pl.pallas_call(functools.partial(forward_kernel, chunks, block, size ** (...  196 us
    pallas_call x1, Pallas kernels, last_stage(): pl.pallas_call(last_kernel, out_shape=[shape((half, width), BF16), shape(...  79.5 us
    pallas_call x1, Pallas kernels, attention_back(): pl.pallas_call(functools.partial(attention_back_kernel, chunks, block, si...  73.6 us
    pallas_call x1, Pallas kernels, hidden_back(): pl.pallas_call(functools.partial(hidden_back_kernel, chunks), out_shape=[...  59.7 us
    ppermute x2, waiting for transfers between devices, trade(): moved = lax.ppermute(value, AXES, latent_pairs())  16 us
  transfers between devices with their start and end apart: 2, of which 2 were waited for; matrix products, arithmetic and copies ran while one was open for 2% of the time, Pallas kernels for 0%

profile of v4, /device:TPU:1, one launch (start us, length us, event | category | flops | bytes accessed | tf_op | source)
XLA Modules:
  0.0 466.4 jit_solution(18203132034590346862)
XLA Ops:
  0.6 0.8 slice_reduce_fusion.8
  1.5 1.3 reshape.79.proj_bias
  2.7 1.3 reshape.80.bias
  4.0 0.7 convert_reduce_fusion.1
  4.8 0.1 reshape.81
  4.9 0.7 stack.14
  5.6 0.6 pad.15.piece_ref
  6.2 1.3 reshape.78.mod_bias
  7.5 1.1 copy.28
  8.6 0.9 reshape.68.s_qkv
  9.6 0.7 fusion.4.small_in
  10.2 195.9 %shard_map.228 = (f32[1,6912]{1,0:T(1,128)}, bf16[16,8,128]{2,1,0:T(8,128)(2,1)}, f32[1,1152]{1,0:T(1,128)}, bf16[1024,1152]{1,0:T(8,128)(2,1)}, bf16[24,72,1024...) custom-call(bf16[16,8,128]{2,1,0:T(8,128)(2,1)} %pad.15.piece_ref, ...), custom_call_target="tpu_custom_call" | custom-call | tf_op jit(solution)/shard_map/pallas_call | solution.py:1243
  206.2 1.3 fusion.7
  207.5 59.7 %shard_map.229 = (f32[1,2304]{1,0:T(1,128)}, f32[72,2304]{1,0:T(8,128)}, bf16[16,72,2304]{2,1,0:T(8,128)(2,1)}, f32[512,1152]{1,0:T(8,128)}, f32[512,1152]{1,0:T(8,128)}) custom-call(f32[1,1152]{1,0:T(1,128)} %reshape.80.bias, bf16[1024,1152]{1,0:T(8,128)(2,1)} %get-tuple-element.52.grad_m_in, bf16[1024,2304]{1,0:T(8,128)(2,1)} %get-tuple-element.53.act_in, ...), custom_call_target="tpu_custom_call" | custom-call | tf_op jit(solution)/shard_map/pallas_call | solution.py:1431
  267.3 4.2 multiply_reduce_fusion
  271.5 0.6 pad_maximum_fusion.2.vecs
  272.1 73.6 %shard_map.230 = (f32[4,1152]{1,0:T(4,128)}, f32[72,2304]{1,0:T(8,128)}, f32[72,576]{1,0:T(8,128)}, f32[512,1152]{1,0:T(8,128)}, bf16[24,72,1024]{2,1,0:T(8,128)(2,1)}) custom-call(f32[2,1152]{1,0:T(2,128)} %pad_maximum_fusion.2.vecs, f32[512,1152]{1,0:T(8,128)} %get-tuple-element.50.resid_in, f32[512,1152]{1,0:T(8,128)} %get-tuple-element.61.ngrad_in, ...), custom_call_target="tpu_custom_call" | custom-call | tf_op jit(solution)/shard_map/pallas_call | solution.py:1576
  345.7 2.6 convert_reduce_fusion
  348.4 0.1 reshape.76
  348.4 0.1 reshape.75
  348.5 0.0 copy-done.9
  348.5 0.0 copy-done.8
  348.6 0.1 concatenate.15
  348.7 0.6 broadcast_in_dim.28.half_ref
  349.3 0.6 broadcast_in_dim.27.wide_ref
  349.9 0.6 pad_maximum_fusion.parts_ref
  350.6 79.5 %shard_map.231 = (bf16[512,1152]{1,0:T(8,128)(2,1)}, f32[3,72,576]{2,1,0:T(8,128)}, f32[72,6912]{1,0:T(8,128)}, f32[1,6912]{1,0:T(1,128)}, f32[16,8,128]{2,1,0:T...) custom-call(bf16[1024,1152]{1,0:T(8,128)(2,1)} %get-tuple-element.60.rows_ref, ...), custom_call_target="tpu_custom_call" | custom-call | tf_op jit(solution)/shard_map/pallas_call | solution.py:894
  430.1 2.3 collective-permute-start.1
  432.4 3.3 collective-permute-start
  435.7 0.9 slice_reduce_fusion.1
  436.5 1.4 slice_reduce_fusion.2
  437.9 0.1 reshape_squeeze.6
  438.0 0.7 reshape_squeeze.7
  438.7 1.4 reduce.8
  440.1 1.3 slice_reduce_fusion
  441.4 0.6 fusion.6
  442.0 5.9 %collective-permute-done.1 = bf16[512,1152]{1,0:T(8,128)(2,1)} collective-permute-done((bf16[512,1152]{1,0:T(8,128)(2,1)}, bf16[512,1152]{1,0:T(8,128)(2,1)}, u32[]{:S(2)}, u32[]{:S(2)}) %collective-permute-start.1) | collective-permute-done | bytes 1179680 | tf_op jit(solution)/shard_map/ppermute | solution.py:1630
  447.9 2.4 select_bitcast_fusion
  450.3 10.1 %collective-permute-done = bf16[512,1152]{1,0:T(8,128)(2,1)S(1)} collective-permute-done((bf16[512,1152]{1,0:T(8,128)(2,1)S(1)}, bf16[512,1152]{1,0:T(8,128)(2,1)S(1)}, u32[]{:S(2)}, u32[]{:S(2)}) %collective-permute-start) | collective-permute-done | bytes 1179680 | tf_op jit(solution)/shard_map/ppermute | solution.py:1630
  460.5 1.1 select_bitcast_fusion.1
  461.6 0.0 copy-done.1
  461.6 1.3 copy.34
  462.9 0.1 copy-done.4
  463.0 0.8 copy.35
  463.8 0.0 copy-done.5
  463.8 0.7 copy.36
  464.5 0.8 copy.37
  465.3 0.8 copy.38
  (25 shorter events, 0.2 us)
Async XLA Ops:
  345.7 2.8 copy-start.9
  345.7 2.8 copy-start.8
  345.7 3.6 copy-start.6
  350.6 81.8 %copy-start = (bf16[512,1152]{1,0:T(8,128)(2,1)S(1)}, bf16[512,1152]{1,0:T(8,128)(2,1)}, u32[]{:S(2)}) copy-start(bf16[512,1152]{1,0:T(8,128)(2,1)} %get-tuple-element.94) | copy-start | bytes 3538948
  350.6 90.9 %copy-start.7 = (bf16[1,1152]{1,0:T(2,128)(2,1)S(1)}, bf16[1,1152]{1,0:T(2,128)(2,1)}, u32[]{:S(2)}) copy-start(bf16[1,1152]{1,0:T(2,128)(2,1)} %param.14) | copy-start | bytes 6916
  430.1 17.8 %collective-permute-start.1 = (bf16[512,1152]{1,0:T(8,128)(2,1)}, bf16[512,1152]{1,0:T(8,128)(2,1)}, u32[]{:S(2)}, u32[]{:S(2)}) collective-permute-start(bf16[512,1152]{1,0:T(8,128)(2,1)} %get-tuple-element.77), channel_id=1, source_target_pairs={{1,2},{2,1},{5,6},{6,5},{9,10},{10,9},{13,14},{14,13},{17,18},{18,... | collective-permute-start | bytes 3538952 | tf_op jit(solution)/shard_map/ppermute | solution.py:1630
  432.4 28.1 %collective-permute-start = (bf16[512,1152]{1,0:T(8,128)(2,1)S(1)}, bf16[512,1152]{1,0:T(8,128)(2,1)S(1)}, u32[]{:S(2)}, u32[]{:S(2)}) collective-permute-start(bf16[512,1152]{1,0:T(8,128)(2,1)S(1)} %copy-done), channel_id=1, source_target_pairs={{1,2},{2,1},{5,6},{6,5},{9,10},{10,9},{13,14},{14,13},{17,18},{18,... | collective-permute-start | bytes 3538952 | tf_op jit(solution)/shard_map/ppermute | solution.py:1630
  450.3 11.3 %copy-start.1 = (f32[72,6912]{1,0:T(8,128)S(1)}, f32[72,6912]{1,0:T(8,128)}, u32[]{:S(2)}) copy-start(f32[72,6912]{1,0:T(8,128)} %get-tuple-element.122) | copy-start | bytes 5971972
  461.6 1.4 copy-start.4
  461.6 2.2 copy-start.5
  461.6 2.9 copy-start.3
  463.0 2.3 copy-start.2

commit v5 on v4

--- a/solution.py
+++ b/solution.py
@@ -322,6 +322,10 @@
     return (((z + k) % 4) * 4 + x * 2 + c, y)
 
 
+def z_order(z, k):
+    return (z, z + 1 - 2 * (z % 2), 2 - z // 2, 3 - 3 * (z // 2))[k]
+
+
 def greet(peers):
     sem = pltpu.get_barrier_semaphore()
     for peer in peers:
@@ -341,6 +345,7 @@
     )
 
 
+Z_SENDS = (1, 2, 3)
 GATHER_RECV = 24
 GATHER_SEND = 32
 
@@ -379,23 +384,25 @@
 
         @pl.when(self.home)
         def _():
-            for k in (2, 1, 3):
-                self.move(own, self.part(self.full, d), k, q, z_peer(self.pos, k)).start()
+            for k in Z_SENDS:
+                peer = (z_order(z, k) * 4 + x * 2 + c, y)
+                self.move(own, self.part(self.full, d), k, q, peer).start()
             self.move(own, self.part(self.full, d), 4, q, self.xn).start()
             self.move(own, self.part(self.full, d), 8, 8 + q, self.far).start()
             self.stay().start()
 
         @pl.when(self.away)
         def _():
-            for k in (2, 1, 3):
-                self.move(own, self.part(self.relay, q), k, q, z_peer(self.pos, k)).start()
+            for k in Z_SENDS:
+                peer = (z_order(z, k) * 4 + x * 2 + c, y)
+                self.move(own, self.part(self.relay, q), k, q, peer).start()
             self.move(own, self.part(self.full, d), 8, 16 + q, self.far).start()
             self.move(own, self.part(self.relay, q), 4, q, self.xn).start()
             self.move(own, self.part(self.full, d), 16, 8 + q, self.sib).start()
 
     def from_z(self, k):
         d, z, x, c, y = self.pos
-        q = ((z + k) % 4) * 2 + x
+        q = z_order(z, k) * 2 + x
         dst = self.part(self.full, 2 * q + c)
 
         @pl.when(self.home)
@@ -414,30 +421,33 @@
 
     def from_x(self, k):
         d, z, x, c, y = self.pos
-        q = ((z + k) % 4) * 2 + 1 - x
+        q = z_order(z, k) * 2 + 1 - x
         dst = self.part(self.full, 2 * q + c)
 
         @pl.when(self.home)
         def _():
             self.came(q)
-            if not self.wide:
+            if self.wide != 1:
                 self.move(dst, dst, 12 + k, 8 + q, self.far).start()
 
         @pl.when(self.away)
         def _():
             self.came(q)
+            if self.wide == 2:
+                self.move(self.part(self.relay, q), dst, 12 + k, 16 + q, self.far).start()
             self.move(self.part(self.relay, q), dst, 20 + k, 8 + q, self.sib).start()
 
     def from_y(self, k):
         d, z, x, c, y = self.pos
-        q = ((z + k) % 4) * 2 + x
+        q = z_order(z, k) * 2 + x
 
         @pl.when(self.away)
         def _():
             block = self.part(self.full, 2 * q + 1 - c)
-            self.came(16 + q)
-            self.move(block, block, 12 + k, 16 + q, self.xn).start()
-            if self.wide:
+            if self.wide != 2:
+                self.came(16 + q)
+                self.move(block, block, 12 + k, 16 + q, self.xn).start()
+            if self.wide == 1:
                 block = self.part(self.full, 2 * q + c)
                 self.came(8 + q)
                 self.move(block, block, 24 + k, 8 + q, self.xn).start()
@@ -457,8 +467,10 @@
                 q = ((z + k) % 4) * 2
                 self.came(16 + q + 1 - x)
                 self.came(8 + q + 1 - x)
-                if not self.wide:
+                if self.wide != 1:
                     self.came(8 + q + x)
+                if self.wide == 2:
+                    self.came(16 + q + x)
 
     def finish(self):
         block = self.part(self.full, 0)
@@ -467,13 +479,13 @@
 
         @pl.when(self.home)
         def _():
-            if not self.wide:
+            if self.wide != 1:
                 for s in range(12, 16):
                     self.move(block, block, s, 0, self.sib).wait_send()
 
         @pl.when(self.away)
         def _():
-            for s in range(12, 28 if self.wide else 24):
+            for s in range(12, 28 if self.wide == 1 else 24):
                 self.move(block, block, s, 0, self.sib).wait_send()
 
     def early(self):
@@ -711,27 +723,75 @@
     return lax.dot_general(a, b, (((ca,), (cb,)), ((), ())), preferred_element_type=F32)
 
 
+def loader(sems):
+    count = iter(range(64))
+
+    def load(src, dst):
+        copy = pltpu.make_async_copy(src, dst, sems.at[next(count)])
+        copy.start()
+        return copy.wait
+
+    return load
+
+
+def norm_back_rows(value, g, scale_up):
+    center = value - jnp.mean(value, axis=-1, keepdims=True)
+    rate = lax.rsqrt(jnp.mean(center * center, axis=-1, keepdims=True) + 1e-06)
+    normed = center * rate
+    e = g * scale_up
+    inner = jnp.mean(e * normed, axis=-1, keepdims=True)
+    return rate * (e - jnp.mean(e, axis=-1, keepdims=True) - normed * inner), normed
+
+
+def row_sum(value):
+    return jnp.sum(value, axis=0, keepdims=True)
+
+
 def last_kernel(
-    rows_ref, dqkv_ref, wqkv_ref, tokens_ref, resid_ref, scale_ref, parts_ref, wide_ref, half_ref,
-    silu_ref, w_ref,
-    tgrad_ref, qkv_out, mwg_ref, mbg_ref, sg_ref, wide_out, half_out,
-    grad, ngrad, sent, got, v1, v1_in, v2_in, mods, b2, b3, sgp, land0, land1, land2,
-    s0, s1, r1, s2, r2, s3, r3, s4, r4, recv, send,
+    mod_ref, sums_ref, fc2_bias_ref, fc1_bias_ref, w_ref,
+    rows_in, dqkv_in, wqkv_in, tokens_in, resid_in,
+    tgrad_ref, qkv_out, sg_ref, mods_a, mods_b, b2, b3,
+    rows_ref, dqkv_ref, wqkv_ref, tokens_ref, resid_ref, tsend, half_ref,
+    grad, ngrad, sent, got, v1, v1_in, v2, v2_in, sgp, land0, land1, land2,
+    load_sems, s0, s1, r1, s2, r2, s3, r3, s4, r4, s5, r5, recv, send,
 ):
     pos = place()
     d, z, x, c, y = pos
     sib = neighbours(pos)[0]
+    far = (z * 4 + x * 2 + 1 - c, 1 - y)
     lin = d * 2 + y
     half, width = tokens_ref.shape
     heads = dqkv_ref.shape[0] // 3
+    load = loader(load_sems)
+    ready = [load(dqkv_in, dqkv_ref), load(rows_in, rows_ref)]
+    ready_late = [
+        load(*pair)
+        for pair in ((wqkv_in, wqkv_ref), (tokens_in, tokens_ref), (resid_in, resid_ref))
+    ]
     greet([(((lin + k) % 32) // 2, (lin + k) % 2) for k in range(1, 32)])
     me = (z * 2 + x) * 2 + y
+    sgp[...] = jnp.zeros_like(sgp)
+    n = dqkv_ref.shape[1] * heads
+    hidden = fc1_bias_ref.shape[1]
+    for wait in ready:
+        wait()
+
+    half_ref[...] = jnp.zeros_like(half_ref)
+    half_ref[:, :hidden] = fc1_bias_ref[...]
+    ones = jnp.ones((8, 2 * half), BF16)
+    for j, at in ((0, hidden), (2, hidden + (n + 127) // 128 * 128)):
+        value = product(ones, flat(dqkv_ref[j * heads : (j + 1) * heads]), 1, 1)
+        half_ref[:, at : at + n] = value[0:1, :]
+
+    for i in range(6):
+        early = sums_ref[i : i + 1, :] if i < 5 else fc2_bias_ref[...]
+        v2[:, i * width : (i + 1) * width] = early
+    swap_early = remote(v2, v2_in, s0.at[2], s0.at[3], sib)
+    swap_early.start()
 
     @pl.when(y == c)
     def _():
         b3[me] = half_ref[...]
-
-    sgp[...] = jnp.zeros_like(sgp)
 
     def send3(q, core):
         s = q * 2 + core
@@ -744,7 +804,6 @@
                     functools.partial(action, q, core)
                 )
 
-    n = dqkv_ref.shape[1] * heads
     reducers = [
         Reduce(grad.at[j], land, qkv_out.at[j], recv.at[j], send.at[j], pos, (0, n))
         for j, land in enumerate((land0, land1, land2))
@@ -761,61 +820,6 @@
     each3(lambda q, core: send3(q, core).start())
     pump = Pump(reduce_events(reducers, 3)[3:])
 
-    tile = half // 2
-    swap = remote(sent, got, s0.at[4], s0.at[5], sib)
-
-    def into_norm(i):
-        cols = pl.ds(pl.multiple_of(i * tile, tile), tile)
-        return product(flat(dqkv_ref[:, :, cols]), wqkv_ref[...], 0, 1)
-
-    def other_rows(i, _):
-        sent[pl.ds(pl.multiple_of(i * tile, tile), tile), :] = into_norm(i + 2).astype(BF16)
-        return 0
-
-    def own_rows(i, _):
-        ngrad[pl.ds(pl.multiple_of(i * tile, tile), tile), :] = into_norm(i)
-        return 0
-
-    lax.fori_loop(0, 2, other_rows, 0)
-    swap.start()
-    pump.run(1)
-    lax.fori_loop(0, 2, own_rows, 0)
-    swap.wait()
-    piece = half // 4
-    scale = 1.0 + scale_ref[...]
-
-    def norm_back(i, sums):
-        part = pl.ds(pl.multiple_of(i * piece, piece), piece)
-        value = tokens_ref[part, :].astype(F32)
-        center = value - jnp.mean(value, axis=-1, keepdims=True)
-        rate = lax.rsqrt(jnp.mean(center * center, axis=-1, keepdims=True) + 1e-06)
-        normed = center * rate
-        g = ngrad[part, :] + got[part, :].astype(F32)
-        e = g * scale
-        inner = jnp.mean(e * normed, axis=-1, keepdims=True)
-        back = rate * (e - jnp.mean(e, axis=-1, keepdims=True) - normed * inner)
-        tgrad_ref[part, :] = (resid_ref[part, :] + back).astype(BF16)
-        return (
-            sums[0] + jnp.sum(g, axis=0, keepdims=True),
-            sums[1] + jnp.sum(g * normed, axis=0, keepdims=True),
-        )
-
-    zero = jnp.zeros((1, width), F32)
-    shift_sum, scale_sum = lax.fori_loop(0, 4, norm_back, (zero, zero))
-    v1[:, :width] = shift_sum
-    v1[:, width : 2 * width] = scale_sum
-    v1[:, 2 * width :] = parts_ref[...]
-
-    a = remote(v1, v1_in, s0.at[0], s0.at[1], sib)
-    b = remote(wide_ref, v2_in, s0.at[2], s0.at[3], sib)
-    a.start()
-    b.start()
-    pump.run(1)
-    a.wait()
-    b.wait()
-    mods[me] = (v1[...] + v1_in[...]).astype(BF16)
-    b2[me] = wide_ref[...] + v2_in[...]
-
     def chip(k):
         m = (me + k) % 16
         return m, ((m // 2) * 2 + c, m % 2)
@@ -827,17 +831,81 @@
         m, peer = chip(k)
         return remote(buf.at[m], buf.at[m], send.at[k], recv.at[m], peer)
 
-    both = ((mods, s1, r1), (b2, s2, r2))
+    last, wide, known = (mods_a, s1, r1), (b2, s2, r2), (mods_b, s5, r5)
+    swap_early.wait()
+    mods_b[me] = (v2[:, : 4 * width] + v2_in[:, : 4 * width]).astype(BF16)
+    b2[me] = v2[:, 4 * width :] + v2_in[:, 4 * width :]
     for k in range(1, 16):
-        for buf in both:
-            to_chip(*buf, k).start()
-    pump.run(3)
+        to_chip(*known, k).start()
+        to_chip(*wide, k).start()
+    for wait in ready_late:
+        wait()
+
+    tile = half // 2
+    swap = remote(sent, got, s0.at[4], s0.at[5], sib)
+
+    def into_norm(i):
+        cols = pl.ds(pl.multiple_of(i * tile, tile), tile)
+        return product(flat(dqkv_ref[:, :, cols]), flat(wqkv_ref[...]), 0, 1)
+
+    def other_rows(i):
+        sent[pl.ds(pl.multiple_of(i * tile, tile), tile), :] = into_norm(i + 2).astype(BF16)
+
+    def own_rows(i):
+        ngrad[pl.ds(pl.multiple_of(i * tile, tile), tile), :] = into_norm(i)
+
+    pump.loop(2, other_rows, 6)
+    swap.start()
+    pump.loop(2, own_rows, 6)
+    swap.wait()
+    piece = half // 4
+    scale = 1.0 + mod_ref[:, width : 2 * width]
+    v1[...] = jnp.zeros_like(v1)
+
+    def norm_back(i):
+        part = pl.ds(pl.multiple_of(i * piece, piece), piece)
+        g = ngrad[part, :] + got[part, :].astype(F32)
+        back, normed = norm_back_rows(tokens_ref[part, :].astype(F32), g, scale)
+        value = (resid_ref[part, :] + back).astype(BF16)
+
+        @pl.when(y == c)
+        def _():
+            tgrad_ref[part, :] = value
+
+        @pl.when(y != c)
+        def _():
+            tsend[part, :] = value
+
+        v1[:, :width] += row_sum(g)
+        v1[:, width : 2 * width] += row_sum(g * normed)
+
+    pump.loop(4, norm_back, 8)
+    trade = remote(tsend, tgrad_ref, s0.at[6], s0.at[7], far)
+    pl.when(y != c)(lambda: trade.start())
+
+    swap = remote(v1, v1_in, s0.at[0], s0.at[1], sib)
+    swap.start()
+    pump.run(2)
+    swap.wait()
+    mods_a[me] = (v1[...] + v1_in[...]).astype(BF16)
     for k in range(1, 16):
-        from_chip(*both[0], k).wait_recv()
-    every = jnp.concatenate([mods[i].astype(F32) for i in range(16)], axis=0)
-    mbg_ref[...] = jnp.sum(every, axis=0, keepdims=True)
-    every = every.astype(BF16)
-    back = product(every, w_ref[...], 1, 1)
+        to_chip(*last, k).start()
+
+    def rows_of(buf):
+        return jnp.concatenate([buf[i].astype(F32) for i in range(16)], axis=0)
+
+    def back_of(buf, at):
+        every = rows_of(buf).astype(BF16)
+        return product(every, w_ref[:, at : at + every.shape[1]], 1, 1)
+
+    pump.run(8)
+    for k in range(1, 16):
+        from_chip(*known, k).wait_recv()
+    back = back_of(mods_b, 2 * width)
+    pump.run(2)
+    for k in range(1, 16):
+        from_chip(*last, k).wait_recv()
+    back = back + back_of(mods_a, 0)
     for i in range(16):
         sgp[i, 0:1, :72] = back[i : i + 1, :]
 
@@ -848,86 +916,78 @@
     for k in range(1, 16):
         send4(k).start()
     sg_ref[d] = sgp[d]
-    pump.run(2)
-    owned = jnp.concatenate([silu_ref[i].astype(F32)[0:1, :] for i in range(16)], axis=0)
-    owned = owned.astype(BF16)[:, :72]
-    for j in range(6):
-        cols = slice(j * width, (j + 1) * width)
-        mwg_ref[:, cols] = product(owned, every[:, cols], 0, 0)
+    pump.run(4)
     for k in range(1, 16):
-        from_chip(*both[1], k).wait_recv()
-    total = b2[0]
-    for i in range(1, 16):
-        total = total + b2[i]
-    wide_out[...] = total
+        from_chip(*wide, k).wait_recv()
 
     def arrive3(i):
         remote(half_ref, b3.at[i], s3.at[0], r3.at[i], sib).wait_recv()
 
     for i in range(16):
         pl.when(jnp.logical_or(i != me, y != c))(functools.partial(arrive3, i))
-    total = b3[0]
-    for i in range(1, 16):
-        total = total + b3[i]
-    half_out[...] = total
     for k in range(1, 16):
         m = (d + k) % 16
         remote(sgp.at[m], sg_ref.at[m], s4.at[k], r4.at[m], (m, y)).wait_recv()
     pump.run()
     for reducer in reducers:
         reducer.finish()
+    pl.when(y != c)(lambda: trade.wait())
     each3(lambda q, core: send3(q, core).wait_send())
     for k in range(1, 16):
-        for buf in both:
+        for buf in (last, wide, known):
             to_chip(*buf, k).wait_send()
         send4(k).wait_send()
 
 
-def last_stage(rows, dqkv, w_qkv, tokens, resid, scale, parts, wide, halves, silu, w_mod, collective_id):
-    vmem = pl.BlockSpec(memory_space=pltpu.VMEM)
+def last_stage(
+    mod, sums, fc2_bias, fc1_bias, w_mod, rows, dqkv, w_qkv, tokens, resid, collective_id
+):
+    vmem, anywhere = pl.BlockSpec(memory_space=pltpu.VMEM), pl.BlockSpec(memory_space=pl.ANY)
     n = w_mod.shape[1]
-    n2, n3 = wide.shape[1], halves.shape[1]
     half, width = tokens.shape
     cols = dqkv.shape[0] * dqkv.shape[1] // 3
+    n2, n3 = 2 * width, fc1_bias.shape[1] + 2 * ((cols + 127) // 128 * 128)
     dma = pltpu.SemaphoreType.DMA((16,))
     shape = jax.ShapeDtypeStruct
+    loaded = (rows, dqkv, w_qkv, tokens, resid)
     return pl.pallas_call(
         last_kernel,
         out_shape=[
             shape((half, width), BF16),
             shape((3, 72, cols), F32),
-            shape((72, n), F32),
-            shape((1, n), F32),
             shape((16, 8, 128), F32),
-            shape((1, n2), F32),
-            shape((1, n3), F32),
+            shape((16, 1, n // 3), BF16),
+            shape((16, 1, n - n // 3), BF16),
+            shape((16, 1, n2), F32),
+            shape((16, 1, n3), F32),
         ],
-        in_specs=[vmem] * 11,
+        in_specs=[vmem] * 5 + [anywhere] * 5,
         out_specs=[vmem] * 7,
-        scratch_shapes=[
+        scratch_shapes=[pltpu.VMEM(a.shape, a.dtype) for a in loaded]
+        + [
+            pltpu.VMEM((half, width), BF16),
+            pltpu.VMEM((1, n3), F32),
             pltpu.VMEM((3, 16, 72, cols), BF16),
             pltpu.VMEM((half, width), F32),
             pltpu.VMEM((half, width), BF16),
             pltpu.VMEM((half, width), BF16),
+            pltpu.VMEM((1, n // 3), F32),
+            pltpu.VMEM((1, n // 3), F32),
             pltpu.VMEM((1, n), F32),
             pltpu.VMEM((1, n), F32),
-            pltpu.VMEM((1, n2), F32),
-            pltpu.VMEM((16, 1, n), BF16),
-            pltpu.VMEM((16, 1, n2), F32),
-            pltpu.VMEM((16, 1, n3), F32),
             pltpu.VMEM((16, 8, 128), F32),
         ]
         + [pltpu.VMEM((27, 72, cols), BF16)] * 3
-        + [pltpu.SemaphoreType.DMA((6,))]
-        + [dma] * 8
+        + [pltpu.SemaphoreType.DMA((8,)), pltpu.SemaphoreType.DMA((8,))]
+        + [dma] * 10
         + [
             pltpu.SemaphoreType.DMA((3, REDUCE_RECV)),
             pltpu.SemaphoreType.DMA((3, REDUCE_SEND)),
         ],
         compiler_params=pltpu.CompilerParams(
-            collective_id=collective_id, has_side_effects=True, vmem_limit_bytes=63000 * 1024
+            collective_id=collective_id, has_side_effects=True, vmem_limit_bytes=64500 * 1024
         ),
-    )(rows, dqkv, w_qkv, tokens, resid, scale, parts, wide, halves, silu, w_mod)
+    )(mod, sums, fc2_bias, fc1_bias, w_mod, *loaded)
 
 
 LOG2E = math.log2(math.e)
@@ -1034,7 +1094,7 @@
     def until_ready(g):
         pump.run(events.index(last_of[g]) + 1 - pump.next)
 
-    pump.run(2)
+    pump.run(6)
     silu_ref[d] = piece_ref[d]
     for k in range(1, 16):
         piece_in(k).wait_recv()
@@ -1059,7 +1119,7 @@
     for k in range(1, 8):
         send_part(k).start()
     land[me] = part[me]
-    pump.run(4)
+    pump.run(10)
     for k in range(1, 8):
         part_in(k).wait_recv()
     total = land[0]
@@ -1068,7 +1128,7 @@
     mine[...] = total
     swap = remote(mine, other, sems.at[13], sems.at[14], sib)
     swap.start()
-    pump.run(3)
+    pump.run(4)
     for k in range(1, 16):
         piece(k).wait_send()
     for k in range(1, 8):
@@ -1120,7 +1180,7 @@
         pump.run(2)
     store(qkv, qkv_out)
     steps, body = attention_step(qkv, out, lse, block, scale)
-    pump.loop(steps, body, 16)
+    pump.loop(steps, body, 22)
     store(out, attended_out)
     store(lse, lse_out)
     until_ready(1)
@@ -1311,17 +1371,6 @@
     return heads * blocks, body
 
 
-def loader(sems):
-    count = iter(range(64))
-
-    def load(src, dst):
-        copy = pltpu.make_async_copy(src, dst, sems.at[next(count)])
-        copy.start()
-        return copy.wait
-
-    return load
-
-
 def hidden_back_kernel(
     chunks, bias, grad_m_in, act_in, slope_in, rows_in, fc2_grad_in, w_fc2, w_fc1,
     fc1_bias_grad, fc2_out, fc1_grad_out, branch_out, ngrad_out,
@@ -1464,36 +1513,32 @@
     )(bias, grad_m, act, slope, rows, fc2_grad, w_fc2, w_fc1)
 
 
-def norm_back_rows(value, g, scale_up):
-    center = value - jnp.mean(value, axis=-1, keepdims=True)
-    rate = lax.rsqrt(jnp.mean(center * center, axis=-1, keepdims=True) + 1e-06)
-    normed = center * rate
-    e = g * scale_up
-    inner = jnp.mean(e * normed, axis=-1, keepdims=True)
-    return rate * (e - jnp.mean(e, axis=-1, keepdims=True) - normed * inner), normed
-
-
-def row_sum(value):
-    return jnp.sum(value, axis=0, keepdims=True)
-
-
 def attention_back_kernel(
-    chunks, block, scale, vecs, resid_in, ngrad_in, out_grad_in, branch_in, w_proj_in, qkv_in,
-    out_in, lse_in, fc1_grad_in,
-    sums, fc1_out, proj_out, resid_grad_out, result_out,
-    resid, ngrad, out_grad, branch, w_proj, qkv, out, lse, fc1_grad, resid_grad, result,
-    rows, grad, proj_grad, key_sum, value_sum, *rest,
+    chunks, block, scale, mod, resid_in, ngrad_in, out_grad_in, branch_in, branch_m_in, w_proj_in,
+    qkv_in, out_in, lse_in, fc1_grad_in,
+    sums, fc1_out, proj_out, output, resid_grad_out, result_out,
+    resid, ngrad, out_grad, branch, branch_m, w_proj, qkv, out, lse, fc1_grad, resid_grad, result,
+    rows, grad, proj_grad, key_sum, value_sum, given, *rest,
 ):
     n = len(chunks)
     lands, (sems, load_sems, recv, send) = rest[:n], rest[n:]
     pos = place()
     sib = neighbours(pos)[0]
     half, width = resid.shape
+    d, z, x, c, y = pos
+    home, away = c == y, c != y
+    far = (z * 4 + x * 2 + 1 - c, 1 - y)
     load = loader(load_sems)
     first = [load(fc1_grad_in, fc1_grad)]
     norm_ready = [
         load(*pair)
-        for pair in ((ngrad_in, ngrad), (resid_in, resid), (out_grad_in, out_grad), (branch_in, branch))
+        for pair in (
+            (ngrad_in, ngrad),
+            (resid_in, resid),
+            (out_grad_in, out_grad),
+            (branch_in, branch),
+            (branch_m_in, branch_m),
+        )
     ]
     late = [load(w_proj_in, w_proj), load(out_in, out), load(qkv_in, qkv), load(lse_in, lse)]
     greet(chip_peers(pos))
@@ -1516,24 +1561,46 @@
     for wait in norm_ready:
         wait()
     tall = half // 4
-    scale_up = 1.0 + vecs[1:2, :]
+    gate_a, scale_m, gate_m = (mod[:, i * width : (i + 1) * width] for i in (2, 4, 5))
+    scale_up = 1.0 + scale_m
 
     def norm(i, total):
         part = pl.ds(pl.multiple_of(i * tall, tall), tall)
         g = ngrad[part, :]
-        back, normed = norm_back_rows(resid[part, :], g, scale_up)
-        value = out_grad[part, :].astype(F32) + back
+        mid = resid[part, :]
+        back, normed = norm_back_rows(mid, g, scale_up)
+        grads = out_grad[part, :].astype(F32)
+        value = grads + back
         resid_grad[part, :] = value
-        low = (value * vecs[0:1, :]).astype(BF16)
+        low = (value * gate_a).astype(BF16)
         rows[part, :] = low
-        terms = (g, g * normed, value * branch[part, :], low.astype(F32))
+        made = (mid + gate_m * branch_m[part, :]).astype(BF16)
+
+        @pl.when(home)
+        def _():
+            output[part, :] = made
+
+        @pl.when(away)
+        def _():
+            given[part, :] = made
+
+        terms = (
+            value * branch[part, :],
+            g,
+            g * normed,
+            grads * branch_m[part, :],
+            low.astype(F32),
+        )
         return tuple(t + row_sum(v) for t, v in zip(total, terms))
 
-    total = lax.fori_loop(0, 4, norm, (jnp.zeros((1, width), F32),) * 4)
+    total = lax.fori_loop(0, 4, norm, (jnp.zeros((1, width), F32),) * 5)
     share = remote(rows.at[:half], rows.at[half:], sems.at[0], sems.at[1], sib)
     share.start()
     stored = [load(resid_grad, resid_grad_out)]
-    for i in range(4):
+    trade = remote(given, output, sems.at[2], sems.at[3], far)
+    pl.when(away)(lambda: trade.start())
+    sums[...] = jnp.zeros_like(sums)
+    for i in range(5):
         sums[i : i + 1, :] = total[i]
     pump.run(1)
     for wait in late:
@@ -1555,6 +1622,7 @@
     pump.loop(steps, body, 28)
     stored.append(load(result, result_out))
     pump.run()
+    pl.when(away)(lambda: trade.wait())
     for p in parts:
         p.finish()
     for wait in stored:
@@ -1562,8 +1630,8 @@
 
 
 def attention_back(
-    vecs, resid, ngrad, out_grad, branch, w_proj, qkv, out, lse, fc1_grad, chunks, collective_id,
-    block=512,
+    mod, resid, ngrad, out_grad, branch, branch_m, w_proj, qkv, out, lse, fc1_grad, chunks,
+    collective_id, block=512,
 ):
     heads, size, count = out.shape
     half, width = resid.shape
@@ -1571,18 +1639,19 @@
     vmem, anywhere = pl.BlockSpec(memory_space=pltpu.VMEM), pl.BlockSpec(memory_space=pl.ANY)
     shape = jax.ShapeDtypeStruct
     land = reduce_scratch(chunks)
-    arrays = (resid, ngrad, out_grad, branch, w_proj, qkv, out, lse, fc1_grad)
+    arrays = (resid, ngrad, out_grad, branch, branch_m, w_proj, qkv, out, lse, fc1_grad)
     made = [((half, width), F32), (qkv.shape, BF16)]
     return pl.pallas_call(
         functools.partial(attention_back_kernel, chunks, block, size**-0.5),
         out_shape=[
-            shape((4, width), F32),
+            shape((8, width), F32),
             shape(fc1_grad.shape[1:], F32),
             shape((owned, cols), F32),
+            shape((half, width), BF16),
         ]
         + [shape(*m) for m in made],
-        in_specs=[vmem] + [anywhere] * 9,
-        out_specs=[vmem] * 3 + [anywhere] * 2,
+        in_specs=[vmem] + [anywhere] * 10,
+        out_specs=[vmem] * 4 + [anywhere] * 2,
         scratch_shapes=[pltpu.VMEM(a.shape, a.dtype) for a in arrays]
         + [pltpu.VMEM(*m) for m in made]
         + [
@@ -1591,55 +1660,15 @@
             pltpu.VMEM((16, owned, cols), BF16),
             pltpu.VMEM((size, count), F32),
             pltpu.VMEM((size, count), F32),
+            pltpu.VMEM((half, width), BF16),
         ]
         + land[: len(chunks)]
-        + [pltpu.SemaphoreType.DMA((2,)), pltpu.SemaphoreType.DMA((12,))]
+        + [pltpu.SemaphoreType.DMA((4,)), pltpu.SemaphoreType.DMA((12,))]
         + land[len(chunks) :],
         compiler_params=pltpu.CompilerParams(
             collective_id=collective_id, has_side_effects=True, vmem_limit_bytes=64500 * 1024
         ),
-    )(vecs, *arrays)
-
-
-def index_of(z, x, c, y):
-    return ((z * 2 + x) * 2 + c) * 2 + y
-
-
-def core_pairs():
-    return [
-        (index_of(z, x, c, y), index_of(z, x, 1 - c, y))
-        for z in range(4)
-        for x in range(2)
-        for c in range(2)
-        for y in range(2)
-    ]
-
-
-def latent_pairs():
-    return [
-        (index_of(z, x, c, y), index_of(z, x, y, c))
-        for z in range(4)
-        for x in range(2)
-        for c in range(2)
-        for y in range(2)
-        if c != y
-    ]
-
-
-def trade(value):
-    moved = lax.ppermute(value, AXES, latent_pairs())
-    home = lax.axis_index("dp") % 2 == lax.axis_index("tensor")
-    return jnp.where(home, value, moved)
-
-
-def both_halves(value):
-    return jnp.concatenate([value, lax.ppermute(value, AXES, core_pairs())], axis=0)
-
-
-def own_sum(partial):
-    n = partial.shape[0] // 2
-    moved = lax.ppermute(partial[n:].astype(BF16), AXES, core_pairs())
-    return partial[:n] + moved.astype(F32)
+    )(mod, *arrays)
 
 
 def columns(n, step):
@@ -1686,7 +1715,7 @@
         first_hidden_weight.reshape(1, owned, hidden),
         second_hidden_weight.T.reshape(1, owned, hidden),
     ]
-    chunks = [(0, p, True) for p in columns(3 * cols, 896)] + [(1, None, False)]
+    chunks = [(0, p, False) for p in columns(3 * cols, 896)] + [(1, None, False)]
     chunks += [(g, p, False) for g in (2, 3) for p in columns(hidden, 1152)]
     (
         modulation,
@@ -1722,10 +1751,6 @@
         chunks,
         2,
     )
-    shift_a, scale_a, gate_a, shift_m, scale_m, gate_m = [
-        modulation[:, i * width : (i + 1) * width] for i in range(6)
-    ]
-    grad_out = out_grad_here.astype(F32)
 
     fc1_bias_part, fc2_out, fc1_grad, branch_m, normed_m_grad = hidden_back(
         second_hidden_bias.astype(F32)[None],
@@ -1739,14 +1764,13 @@
         columns(hidden, 768),
         4,
     )
-    output = (resid_mid + gate_m * branch_m).astype(BF16)
-    gate_m_grad = jnp.sum(grad_out * branch_m, axis=0)
-    sums, fc1_out, proj_out, resid_grad, qkv_grad = attention_back(
-        jnp.concatenate([gate_a, scale_m]),
+    sums, fc1_out, proj_out, output, resid_grad, qkv_grad = attention_back(
+        modulation,
         resid_mid,
         normed_m_grad,
         out_grad_here,
         branch_a,
+        branch_m,
         w_proj,
         qkv,
         attended,
@@ -1755,54 +1779,40 @@
         [(0, p) for p in columns(hidden, 768)] + [(1, (0, cols))],
         5,
     )
-    shift_m_grad, scale_m_grad, gate_a_grad, proj_bias_part = (sums[i] for i in range(4))
-    qkv_bias_part = jnp.sum(qkv_grad, axis=2, dtype=F32)
-    half_part = jnp.concatenate(
-        [
-            fc1_bias_part[0],
-            qkv_bias_part[:heads_here].reshape(-1),
-            qkv_bias_part[2 * heads_here :].reshape(-1),
-        ]
-    )[None]
-    mod_part = jnp.concatenate(
-        [
-            gate_a_grad.reshape(1, -1),
-            shift_m_grad.reshape(1, -1),
-            scale_m_grad.reshape(1, -1),
-            gate_m_grad.reshape(1, -1),
-        ],
-        axis=1,
-    )
-    wide_part = jnp.concatenate([fc2_bias_part[0], proj_bias_part])[None]
-    tokens_grad, qkv_out, mod_weight_grad, mod_bias_grad, silu_grad, wide, narrow = last_stage(
+    tokens_grad, qkv_out, silu_grad, mods_a, mods_b, wide, narrow = last_stage(
+        modulation,
+        sums,
+        fc2_bias_part,
+        fc1_bias_part,
+        mod_weight,
         rows_a,
         qkv_grad,
-        w_qkv.reshape(width, 3 * cols),
+        w_qkv,
         tokens_here,
         resid_grad,
-        scale_a,
-        mod_part,
-        wide_part,
-        half_part,
-        silu_owned,
-        mod_weight,
         6,
     )
+    mods = jnp.concatenate([mods_a[:, 0], mods_b[:, 0]], axis=1)
+    mod_weight_grad = product(silu_owned[:, 0, :owned], mods, 0, 0)
+    mod_bias_grad = jnp.sum(mods, axis=0, dtype=F32)
+    wide, narrow = jnp.sum(wide[:, 0], axis=0), jnp.sum(narrow[:, 0], axis=0)
+    step = (cols + 127) // 128 * 128
+    qkv_bias_grad = jnp.stack([narrow[hidden + i * step :][:cols] for i in range(2)])
     cond_grad = silu_back(silu_grad[:, 0, :owned].reshape(1, width))[0]
     return (
-        trade(output).reshape(half, 1, width),
-        trade(tokens_grad).reshape(half, 1, width),
+        output.reshape(half, 1, width),
+        tokens_grad.reshape(half, 1, width),
         cond_grad,
         mod_weight_grad,
-        mod_bias_grad[0],
+        mod_bias_grad,
         jnp.moveaxis(qkv_out, 0, 1),
-        narrow[0, hidden:].reshape(2, cols),
+        qkv_bias_grad,
         proj_out.T,
-        wide[0, width:],
+        wide[:width],
         fc1_out,
-        narrow[0, :hidden],
+        narrow[:hidden],
         fc2_out.T,
-        wide[0, :width],
+        wide[width:],
     )
 
 

time: 471 us -> 427 us (0.907)
  waiting for transfers between devices: 16 us -> 0 us
  Pallas kernels: 409 us -> 396 us
  other arithmetic: 15.1 us -> 5.37 us
  starting transfers between devices: 5.56 us -> 0 us
    pallas_call x1, Pallas kernels: 196 us -> 177 us  [forward_stage(): pl.pallas_call(functools.partial(forward_kernel, chunks, block, size ** (...]
    ppermute x2 -> x0, waiting for transfers between devices: 16 us -> none  [trade(): moved = lax.ppermute(value, AXES, latent_pairs())]
    pallas_call x1, Pallas kernels: 73.6 us -> 82.7 us  [attention_back(): pl.pallas_call(functools.partial(attention_back_kernel, chunks, block, si...]
    ppermute x2 -> x0, starting transfers between devices: 5.56 us -> none  [trade(): moved = lax.ppermute(value, AXES, latent_pairs())]
  transfers between devices with their start and end apart: 2 -> 0, of which waited for: 2 -> 0; matrix products, arithmetic and copies ran while one was open for 2% -> 0% of each run, Pallas kernels for 0% -> 0%
where the time goes in v5:
time: 427 us; the launch traced here: 423 us
  Pallas kernels  396 us (93%)
  local copies, waits for them, and re-layouts  18.3 us (4%)
  other arithmetic  5.37 us (1%)
    pallas_call x1, Pallas kernels, forward_stage(): pl.pallas_call(functools.partial(forward_kernel, chunks, block, size ** (...  177 us
    pallas_call x1, Pallas kernels, attention_back(): pl.pallas_call(functools.partial(attention_back_kernel, chunks, block, si...  82.7 us
    pallas_call x1, Pallas kernels, last_stage(): pl.pallas_call(last_kernel, out_shape=[shape((half, width), BF16), shape(...  76.6 us
    pallas_call x1, Pallas kernels, hidden_back(): pl.pallas_call(functools.partial(hidden_back_kernel, chunks), out_shape=[...  60.3 us

profile of v5, /device:TPU:1, one launch (start us, length us, event | category | flops | bytes accessed | tf_op | source)
XLA Modules:
  0.0 422.7 jit_solution(11857577192996005701)
XLA Ops:
  0.6 0.8 slice_reduce_fusion.2
  1.5 1.3 reshape.63.proj_bias
  2.7 1.3 reshape.64.bias
  4.0 0.7 convert_reduce_fusion.1
  4.8 0.1 reshape.65
  4.9 0.7 stack.23
  5.6 0.7 fusion.5.small_in
  6.2 0.6 pad.15.piece_ref
  6.9 1.3 reshape.62.mod_bias
  8.2 1.1 copy.28
  9.3 0.9 reshape.56.s_qkv
  10.2 176.7 %shard_map.228 = (f32[1,6912]{1,0:T(1,128)}, bf16[16,8,128]{2,1,0:T(8,128)(2,1)}, f32[1,1152]{1,0:T(1,128)}, bf16[1024,1152]{1,0:T(8,128)(2,1)}, bf16[24,72,1024...) custom-call(bf16[16,8,128]{2,1,0:T(8,128)(2,1)} %pad.15.piece_ref, ...), custom_call_target="tpu_custom_call" | custom-call | tf_op jit(solution)/shard_map/pallas_call | solution.py:1303
  186.9 0.8 slice.34
  187.7 60.3 %shard_map.229 = (f32[1,2304]{1,0:T(1,128)}, f32[72,2304]{1,0:T(8,128)}, bf16[16,72,2304]{2,1,0:T(8,128)(2,1)}, f32[512,1152]{1,0:T(8,128)}, f32[512,1152]{1,0:T(8,128)}) custom-call(f32[1,1152]{1,0:T(1,128)} %reshape.64.bias, bf16[1024,1152]{1,0:T(8,128)(2,1)} %get-tuple-element.53.grad_m_in, bf16[1024,2304]{1,0:T(8,128)(2,1)} %get-tuple-element.54.act_in, ...), custom_call_target="tpu_custom_call" | custom-call | tf_op jit(solution)/shard_map/pallas_call | solution.py:1480
  248.0 82.7 %shard_map.230 = (f32[8,1152]{1,0:T(8,128)}, f32[72,2304]{1,0:T(8,128)}, f32[72,576]{1,0:T(8,128)}, bf16[512,1152]{1,0:T(8,128)(2,1)}, f32[512,1152]{1,0:T(8,128)}, /*index=5*/bf16[24,72,1024]{2,1,0:T(8,128)(2,1)}) custom-call(f32[1,6912]{1,0:T(1,128)} %get-tuple-element.51.mod.mod_ref, f32[512,1152]{1,0:T(8,128)} %get-tuple-element.52.resid_in, ...), custom_call_target="tpu_custom_call" | custom-call | tf_op jit(solution)/shard_map/pallas_call | solution.py:1644
  330.7 0.0 copy-start.6
  330.7 76.6 %shard_map.231 = (bf16[512,1152]{1,0:T(8,128)(2,1)}, f32[3,72,576]{2,1,0:T(8,128)}, f32[16,8,128]{2,1,0:T(8,128)}, bf16[16,1,2304]{2,1,0:T(2,128)(2,1)}, bf16[16...) custom-call(f32[1,6912]{1,0:T(1,128)} %get-tuple-element.51.mod.mod_ref, ...), custom_call_target="tpu_custom_call" | custom-call | tf_op jit(solution)/shard_map/pallas_call | solution.py:953
  407.3 0.0 copy-start
  407.3 1.0 slice_reduce_fusion
  408.3 0.1 reshape_squeeze.3
  408.4 0.0 copy-done.6
  408.4 0.6 fusion.7
  409.0 1.0 reduce_sum.29
  410.0 1.1 reduce_sum.28
  411.1 0.6 fusion.12
  411.7 0.6 slice.43
  412.3 0.6 pad_maximum_fusion.2
  412.9 0.9 copy.39
  413.8 1.0 copy.38
  414.8 0.0 copy-start.1
  414.8 0.7 convert_reduce_fusion
  415.5 1.7 fusion
  417.2 0.0 copy-done
  417.2 0.0 copy-start.4
  417.2 0.0 copy-start.5
  417.2 1.0 copy.46
  418.2 0.0 copy-done.1
  418.3 0.0 copy-start.3
  418.3 0.0 copy-start.2
  418.3 1.0 copy.47
  419.3 0.0 copy-done.4
  419.3 0.8 copy.48
  420.1 0.0 copy-done.5
  420.1 0.7 copy.49
  420.8 0.0 copy-done.3
  420.8 0.8 copy.50
  421.6 0.0 copy-done.2
  421.6 0.8 copy.51
  (7 shorter events, 0.0 us)
Async XLA Ops:
  330.7 77.6 %copy-start.6 = (bf16[1,1152]{1,0:T(2,128)(2,1)S(1)}, bf16[1,1152]{1,0:T(2,128)(2,1)}, u32[]{:S(2)}) copy-start(bf16[1,1152]{1,0:T(2,128)(2,1)} %param.14) | copy-start | bytes 6916
  407.3 9.9 %copy-start = (bf16[512,1152]{1,0:T(8,128)(2,1)S(1)}, bf16[512,1152]{1,0:T(8,128)(2,1)}, u32[]{:S(2)}) copy-start(bf16[512,1152]{1,0:T(8,128)(2,1)} %get-tuple-element.69) | copy-start | bytes 3538948
  414.8 3.4 copy-start.1
  417.2 2.0 copy-start.4
  417.2 2.8 copy-start.5
  418.3 2.5 copy-start.3
  418.3 3.3 copy-start.2

commit v6 on v5

--- a/solution.py
+++ b/solution.py
@@ -350,6 +350,14 @@
 GATHER_SEND = 32
 
 
+def repeat(first, stop, action):
+    def step(i, _):
+        action(i)
+        return 0
+
+    lax.fori_loop(first, stop, step, 0)
+
+
 class Gather:
     def __init__(self, shard, full, relay, cols, wide, recv, send, pos):
         self.wide = wide
@@ -457,36 +465,31 @@
 
         @pl.when(self.home)
         def _():
-            for q in range(8):
-                self.came(8 + q)
+            repeat(0, 8, lambda q: self.came(8 + q))
             self.stay().wait()
 
         @pl.when(self.away)
         def _():
-            for k in range(4):
-                q = ((z + k) % 4) * 2
-                self.came(16 + q + 1 - x)
-                self.came(8 + q + 1 - x)
+            def other(k):
+                self.came(16 + 2 * k + 1 - x)
+                self.came(8 + 2 * k + 1 - x)
                 if self.wide != 1:
-                    self.came(8 + q + x)
+                    self.came(8 + 2 * k + x)
                 if self.wide == 2:
-                    self.came(16 + q + x)
+                    self.came(16 + 2 * k + x)
+
+            repeat(0, 4, other)
 
     def finish(self):
         block = self.part(self.full, 0)
-        for s in range(1, 12):
+
+        def sent(s):
             self.move(block, block, s, 0, self.sib).wait_send()
 
-        @pl.when(self.home)
-        def _():
-            if self.wide != 1:
-                for s in range(12, 16):
-                    self.move(block, block, s, 0, self.sib).wait_send()
-
-        @pl.when(self.away)
-        def _():
-            for s in range(12, 28 if self.wide == 1 else 24):
-                self.move(block, block, s, 0, self.sib).wait_send()
+        repeat(1, 12, sent)
+        if self.wide != 1:
+            pl.when(self.home)(lambda: repeat(12, 16, sent))
+        pl.when(self.away)(lambda: repeat(12, 28 if self.wide == 1 else 24, sent))
 
     def early(self):
         return [functools.partial(self.from_z, k) for k in (1, 2, 3)]
@@ -556,8 +559,15 @@
     def came(self, slot):
         self.push(self.slot(slot), slot, 0, self.sib).wait_recv()
 
-    def value(self, i):
-        return self.land[i].astype(F32)
+    def value(self, i, r):
+        return self.land[i, r].astype(F32)
+
+    def by_rows(self, body):
+        def step(i, _):
+            body(pl.ds(pl.multiple_of(i * 8, 8), 8))
+            return 0
+
+        lax.fori_loop(0, 9, step, 0)
 
     def first(self):
         d, z, x, c, y = self.pos
@@ -601,8 +611,12 @@
             self.push(self.slot(15 + q), 23 + zz, 15 + k, self.xn).start()
             b = 2 * q + c
             self.came(q)
-            total = self.grad[b, :, self.cols].astype(F32) + self.value(q)
-            self.grad[b, :, self.cols] = total.astype(BF16)
+
+            def add(r):
+                total = self.grad[b, r, self.cols].astype(F32) + self.value(q, r)
+                self.grad[b, r, self.cols] = total.astype(BF16)
+
+            self.by_rows(add)
             self.push(self.rows(b), 8 + zz, 8 + k, self.xn).start()
 
     def third(self, k):
@@ -614,15 +628,23 @@
         def _():
             self.came(15 + q)
             self.came(23 + zz)
-            self.land[15 + q] = (self.value(15 + q) + self.value(23 + zz)).astype(BF16)
+
+            def add(r):
+                self.land[15 + q, r] = (self.value(15 + q, r) + self.value(23 + zz, r)).astype(BF16)
+
+            self.by_rows(add)
             self.push(self.slot(15 + q), 15 + zz, 19 + k, self.yn).start()
             if k < 3:
                 b = 2 * q + c
                 self.came(q)
                 self.came(8 + zz)
-                total = self.grad[b, :, self.cols].astype(F32)
-                total = total + self.value(q) + self.value(8 + zz)
-                self.grad[b, :, self.cols] = total.astype(BF16)
+
+                def add_two(r):
+                    total = self.grad[b, r, self.cols].astype(F32)
+                    total = total + self.value(q, r) + self.value(8 + zz, r)
+                    self.grad[b, r, self.cols] = total.astype(BF16)
+
+                self.by_rows(add_two)
                 self.push(self.rows(b), 12 + k, 12 + k, (zz * 4 + x * 2 + c, y)).start()
 
     def fourth(self, k):
@@ -635,8 +657,12 @@
             self.came(q)
             self.came(8 + zz)
             self.came(15 + zz)
-            total = self.value(q) + self.value(8 + zz) + self.value(15 + zz)
-            self.land[q] = total.astype(BF16)
+
+            def add(r):
+                total = self.value(q, r) + self.value(8 + zz, r) + self.value(15 + zz, r)
+                self.land[q, r] = total.astype(BF16)
+
+            self.by_rows(add)
             self.push(self.slot(q), 12 + k, 20 + k, (zz * 4 + x * 2 + c, y)).start()
 
     def fifth(self):
@@ -646,22 +672,25 @@
         self.came(8 + z)
         for k in range(3):
             self.came(12 + k)
-        total = self.value(q) + self.value(8 + z)
-        total = total + self.value(12) + self.value(13) + self.value(14)
-
-        @pl.when(self.home)
-        def _():
-            self.out[:, self.cols] = total + self.grad[d, :, self.cols].astype(F32)
-
-        @pl.when(self.away)
-        def _():
-            self.came(15 + z)
-            self.out[:, self.cols] = total + self.value(15 + z)
+        pl.when(self.away)(lambda: self.came(15 + z))
+
+        def add(r):
+            total = self.value(q, r) + self.value(8 + z, r)
+            total = total + self.value(12, r) + self.value(13, r) + self.value(14, r)
+
+            @pl.when(self.home)
+            def _():
+                self.out[r, self.cols] = total + self.grad[d, r, self.cols].astype(F32)
+
+            @pl.when(self.away)
+            def _():
+                self.out[r, self.cols] = total + self.value(15 + z, r)
+
+        self.by_rows(add)
 
     def finish(self):
         block = self.slot(0)
-        for s in range(REDUCE_SEND):
-            self.push(block, 0, s, self.sib).wait_send()
+        repeat(0, REDUCE_SEND, lambda s: self.push(block, 0, s, self.sib).wait_send())
 
 
 def reduce_events(parts, lead=1):
@@ -845,20 +874,22 @@
     swap = remote(sent, got, s0.at[4], s0.at[5], sib)
 
     def into_norm(i):
-        cols = pl.ds(pl.multiple_of(i * tile, tile), tile)
-        return product(flat(dqkv_ref[:, :, cols]), flat(wqkv_ref[...]), 0, 1)
-
-    def other_rows(i):
-        sent[pl.ds(pl.multiple_of(i * tile, tile), tile), :] = into_norm(i + 2).astype(BF16)
-
-    def own_rows(i):
-        ngrad[pl.ds(pl.multiple_of(i * tile, tile), tile), :] = into_norm(i)
-
-    pump.loop(2, other_rows, 6)
-    swap.start()
-    pump.loop(2, own_rows, 6)
+        part = pl.ds(pl.multiple_of(lax.rem(i + 2, 4) * tile, tile), tile)
+        value = product(flat(dqkv_ref[:, :, part]), flat(wqkv_ref[...]), 0, 1)
+
+        @pl.when(i < 2)
+        def _():
+            sent[pl.ds(pl.multiple_of(i * tile, tile), tile), :] = value.astype(BF16)
+
+        @pl.when(i >= 2)
+        def _():
+            ngrad[part, :] = value
+
+        pl.when(i == 1)(lambda: swap.start())
+
+    pump.loop(4, into_norm, 12)
     swap.wait()
-    piece = half // 4
+    piece = half // 8
     scale = 1.0 + mod_ref[:, width : 2 * width]
     v1[...] = jnp.zeros_like(v1)
 
@@ -879,7 +910,7 @@
         v1[:, :width] += row_sum(g)
         v1[:, width : 2 * width] += row_sum(g * normed)
 
-    pump.loop(4, norm_back, 8)
+    pump.loop(8, norm_back, 8)
     trade = remote(tsend, tgrad_ref, s0.at[6], s0.at[7], far)
     pl.when(y != c)(lambda: trade.start())
 
@@ -1141,7 +1172,7 @@
     small_wait()
     tokens_wait()
 
-    tall = half // 4
+    tall = half // 8
 
     def norm_rows(value, shift, scale_up):
         center = value - jnp.mean(value, axis=-1, keepdims=True)
@@ -1154,7 +1185,7 @@
         rows_a[own, :] = norm_rows(tokens[own, :].astype(F32), shift_a, scale_a)
         return 0
 
-    lax.fori_loop(0, 4, first_norm, 0)
+    lax.fori_loop(0, 8, first_norm, 0)
     share = remote(rows_a.at[:half], rows_a.at[half:], sems.at[5], sems.at[6], sib)
     share.start()
     until_ready(0)
@@ -1191,21 +1222,22 @@
     tile = half // 2
     swap = remote(sent, got, sems.at[1], sems.at[2], sib)
 
-    def project(i):
-        cols = pl.ds(pl.multiple_of(i * tile, tile), tile)
-        return product(flat(out[:, :, cols]), flat(proj_here[...]), 0, 1)
-
-    def other_rows(i, _):
-        sent[pl.ds(pl.multiple_of(i * tile, tile), tile), :] = project(i + 2).astype(BF16)
+    def project(i, _):
+        part = pl.ds(pl.multiple_of(lax.rem(i + 2, 4) * tile, tile), tile)
+        value = product(flat(out[:, :, part]), flat(proj_here[...]), 0, 1)
+
+        @pl.when(i < 2)
+        def _():
+            sent[pl.ds(pl.multiple_of(i * tile, tile), tile), :] = value.astype(BF16)
+
+        @pl.when(i >= 2)
+        def _():
+            branch[part, :] = value + proj_bias[...]
+
+        pl.when(i == 1)(lambda: swap.start())
         return 0
 
-    def own_rows(i, _):
-        branch[pl.ds(pl.multiple_of(i * tile, tile), tile), :] = project(i) + proj_bias[...]
-        return 0
-
-    lax.fori_loop(0, 2, other_rows, 0)
-    swap.start()
-    lax.fori_loop(0, 2, own_rows, 0)
+    lax.fori_loop(0, 4, project, 0)
     pump.run(2)
     grad_wait()
     store(out_grad, grad_out)
@@ -1216,7 +1248,7 @@
         grad_m[own, :] = value
         return total + jnp.sum(value.astype(F32), axis=0, keepdims=True)
 
-    fc2_bias_grad[...] = lax.fori_loop(0, 4, gated, jnp.zeros((1, width), F32))
+    fc2_bias_grad[...] = lax.fori_loop(0, 8, gated, jnp.zeros((1, width), F32))
     share_m = remote(grad_m.at[:half], grad_m.at[half:], sems.at[15], sems.at[16], sib)
     share_m.start()
     swap.wait()
@@ -1231,7 +1263,7 @@
         rows[own, :] = norm_rows(mid, shift_m, scale_m)
         return 0
 
-    lax.fori_loop(0, 4, norm, 0)
+    lax.fori_loop(0, 8, norm, 0)
     share.start()
     store(branch, branch_out)
     store(resid, resid_out)
@@ -1560,7 +1592,7 @@
     pump.run(2)
     for wait in norm_ready:
         wait()
-    tall = half // 4
+    tall = half // 8
     gate_a, scale_m, gate_m = (mod[:, i * width : (i + 1) * width] for i in (2, 4, 5))
     scale_up = 1.0 + scale_m
 
@@ -1593,7 +1625,7 @@
         )
         return tuple(t + row_sum(v) for t, v in zip(total, terms))
 
-    total = lax.fori_loop(0, 4, norm, (jnp.zeros((1, width), F32),) * 5)
+    total = lax.fori_loop(0, 8, norm, (jnp.zeros((1, width), F32),) * 5)
     share = remote(rows.at[:half], rows.at[half:], sems.at[0], sems.at[1], sib)
     share.start()
     stored = [load(resid_grad, resid_grad_out)]

time: 427 us -> 426 us (level)
  no operation moved by 1% of the time
where the time goes in v6:
time: 426 us; the launch traced here: 425 us
  Pallas kernels  399 us (94%)
  local copies, waits for them, and re-layouts  18.3 us (4%)
  other arithmetic  5.37 us (1%)
    pallas_call x1, Pallas kernels, forward_stage(): pl.pallas_call(functools.partial(forward_kernel, chunks, block, size ** (...  177 us
    pallas_call x1, Pallas kernels, attention_back(): pl.pallas_call(functools.partial(attention_back_kernel, chunks, block, si...  83.7 us
    pallas_call x1, Pallas kernels, last_stage(): pl.pallas_call(last_kernel, out_shape=[shape((half, width), BF16), shape(...  76.8 us
    pallas_call x1, Pallas kernels, hidden_back(): pl.pallas_call(functools.partial(hidden_back_kernel, chunks), out_shape=[...  61.4 us

profile of v6, /device:TPU:1, one launch (start us, length us, event | category | flops | bytes accessed | tf_op | source)
XLA Modules:
  0.0 425.3 jit_solution(12140923667922629923)
XLA Ops:
  0.6 0.8 slice_reduce_fusion.2
  1.5 1.3 reshape.63.proj_bias
  2.7 1.3 reshape.64.bias
  4.0 0.7 convert_reduce_fusion.1
  4.8 0.1 reshape.65
  4.9 0.7 stack.23
  5.6 0.7 fusion.5.small_in
  6.2 0.6 pad.15.piece_ref
  6.9 1.3 reshape.62.mod_bias
  8.2 1.1 copy.28
  9.3 0.9 reshape.56.s_qkv
  10.2 177.2 %shard_map.228 = (f32[1,6912]{1,0:T(1,128)}, bf16[16,8,128]{2,1,0:T(8,128)(2,1)}, f32[1,1152]{1,0:T(1,128)}, bf16[1024,1152]{1,0:T(8,128)(2,1)}, bf16[24,72,1024...) custom-call(bf16[16,8,128]{2,1,0:T(8,128)(2,1)} %pad.15.piece_ref, ...), custom_call_target="tpu_custom_call" | custom-call | tf_op jit(solution)/shard_map/pallas_call | solution.py:1335
  187.5 0.8 slice.34
  188.2 61.4 %shard_map.229 = (f32[1,2304]{1,0:T(1,128)}, f32[72,2304]{1,0:T(8,128)}, bf16[16,72,2304]{2,1,0:T(8,128)(2,1)}, f32[512,1152]{1,0:T(8,128)}, f32[512,1152]{1,0:T(8,128)}) custom-call(f32[1,1152]{1,0:T(1,128)} %reshape.64.bias, bf16[1024,1152]{1,0:T(8,128)(2,1)} %get-tuple-element.53.grad_m_in, bf16[1024,2304]{1,0:T(8,128)(2,1)} %get-tuple-element.54.act_in, ...), custom_call_target="tpu_custom_call" | custom-call | tf_op jit(solution)/shard_map/pallas_call | solution.py:1512
  249.7 83.7 %shard_map.230 = (f32[8,1152]{1,0:T(8,128)}, f32[72,2304]{1,0:T(8,128)}, f32[72,576]{1,0:T(8,128)}, bf16[512,1152]{1,0:T(8,128)(2,1)}, f32[512,1152]{1,0:T(8,128)}, /*index=5*/bf16[24,72,1024]{2,1,0:T(8,128)(2,1)}) custom-call(f32[1,6912]{1,0:T(1,128)} %get-tuple-element.51.mod.mod_ref, f32[512,1152]{1,0:T(8,128)} %get-tuple-element.52.resid_in, ...), custom_call_target="tpu_custom_call" | custom-call | tf_op jit(solution)/shard_map/pallas_call | solution.py:1676
  333.4 0.0 copy-start.6
  333.4 76.8 %shard_map.231 = (bf16[512,1152]{1,0:T(8,128)(2,1)}, f32[3,72,576]{2,1,0:T(8,128)}, f32[16,8,128]{2,1,0:T(8,128)}, bf16[16,1,2304]{2,1,0:T(2,128)(2,1)}, bf16[16...) custom-call(f32[1,6912]{1,0:T(1,128)} %get-tuple-element.51.mod.mod_ref, ...), custom_call_target="tpu_custom_call" | custom-call | tf_op jit(solution)/shard_map/pallas_call | solution.py:984
  410.2 0.0 copy-start
  410.2 1.0 slice_reduce_fusion
  411.2 0.1 reshape_squeeze.3
  411.3 0.0 copy-done.6
  411.3 0.6 fusion.7
  411.9 1.0 reduce_sum.29
  412.9 1.1 reduce_sum.28
  414.0 0.6 fusion.12
  414.6 0.6 slice.43
  415.2 0.6 pad_maximum_fusion.2
  415.8 0.9 copy.39
  416.7 1.0 copy.38
  417.7 0.0 copy-start.1
  417.7 0.7 convert_reduce_fusion
  418.4 1.7 fusion
  420.1 0.0 copy-done
  420.1 0.0 copy-start.4
  420.1 0.0 copy-start.5
  420.1 1.0 copy.46
  421.1 0.0 copy-done.1
  421.1 0.0 copy-start.3
  421.1 0.0 copy-start.2
  421.1 1.0 copy.47
  422.2 0.0 copy-done.4
  422.2 0.8 copy.48
  423.0 0.0 copy-done.5
  423.0 0.7 copy.49
  423.6 0.0 copy-done.3
  423.6 0.8 copy.50
  424.5 0.0 copy-done.2
  424.5 0.8 copy.51
  (7 shorter events, 0.0 us)
Async XLA Ops:
  333.4 77.9 %copy-start.6 = (bf16[1,1152]{1,0:T(2,128)(2,1)S(1)}, bf16[1,1152]{1,0:T(2,128)(2,1)}, u32[]{:S(2)}) copy-start(bf16[1,1152]{1,0:T(2,128)(2,1)} %param.14) | copy-start | bytes 6916
  410.2 9.9 %copy-start = (bf16[512,1152]{1,0:T(8,128)(2,1)S(1)}, bf16[512,1152]{1,0:T(8,128)(2,1)}, u32[]{:S(2)}) copy-start(bf16[512,1152]{1,0:T(8,128)(2,1)} %get-tuple-element.69) | copy-start | bytes 3538948
  417.7 3.4 copy-start.1
  420.1 2.0 copy-start.4
  420.1 2.8 copy-start.5
  421.1 2.5 copy-start.3
  421.1 3.3 copy-start.2

commit v7 on v6

--- a/solution.py
+++ b/solution.py
@@ -1165,7 +1165,9 @@
     for k in range(1, 8):
         send_part(k).wait_send()
     swap.wait()
-    mod[...] = mine[...] + other[...] + mod_bias[...]
+    for i in range(6):
+        cols = slice(i * width, (i + 1) * width)
+        mod[:, cols] = mine[:, cols] + other[:, cols] + mod_bias[i : i + 1, :]
     shift_a, scale_a, gate_a, shift_m, scale_m, gate_m = [
         mod[:, i * width : (i + 1) * width] for i in range(6)
     ]
@@ -1232,7 +1234,7 @@
 
         @pl.when(i >= 2)
         def _():
-            branch[part, :] = value + proj_bias[...]
+            branch[part, :] = value + proj_bias[6:7, :]
 
         pl.when(i == 1)(lambda: swap.start())
         return 0
@@ -1463,7 +1465,7 @@
     swap1 = remote(sent1, got1, sems.at[1], sems.at[2], sib)
     swap2 = remote(sent2, got2, sems.at[3], sems.at[4], sib)
     act_ready()
-    pump.loop(4, out_of_hidden(act, sent1, branch, bias[...]), 8)
+    pump.loop(4, out_of_hidden(act, sent1, branch, bias[7:8, :]), 8)
     swap1.start()
     weight_ready = load(w_fc1, weight)
     pump.run(2)
@@ -1733,6 +1735,8 @@
         silu_cond.astype(BF16).reshape(16, 1, owned), ((0, 0), (0, 7), (0, 128 - owned))
     )
     s_qkv = query_key_value_weight.reshape(1, owned, 3 * cols)
+    biases = jnp.concatenate([mod_bias, attention_out_bias, second_hidden_bias])
+    biases = biases.astype(F32).reshape(8, width)
     small = jnp.stack(
         [
             jnp.pad(qkv_bias[0], (0, hidden - cols)),
@@ -1773,8 +1777,8 @@
     ) = forward_stage(
         pieces,
         mod_weight,
-        mod_bias.astype(F32)[None],
-        attention_out_bias.astype(F32)[None],
+        biases,
+        biases,
         small,
         tokens.reshape(half, width),
         out_grad.reshape(half, width),
@@ -1785,7 +1789,7 @@
     )
 
     fc1_bias_part, fc2_out, fc1_grad, branch_m, normed_m_grad = hidden_back(
-        second_hidden_bias.astype(F32)[None],
+        biases,
         grad_m,
         act_low,
         slope,

time: 426 us -> 424 us (level)
  no operation moved by 1% of the time
where the time goes in v7:
time: 424 us; the launch traced here: 423 us
  Pallas kernels  399 us (94%)
  local copies, waits for them, and re-layouts  15 us (4%)
  other arithmetic  6.13 us (1%)
    pallas_call x1, Pallas kernels, forward_stage(): pl.pallas_call(functools.partial(forward_kernel, chunks, block, size ** (...  177 us
    pallas_call x1, Pallas kernels, attention_back(): pl.pallas_call(functools.partial(attention_back_kernel, chunks, block, si...  83.7 us
    pallas_call x1, Pallas kernels, last_stage(): pl.pallas_call(last_kernel, out_shape=[shape((half, width), BF16), shape(...  76.8 us
    pallas_call x1, Pallas kernels, hidden_back(): pl.pallas_call(functools.partial(hidden_back_kernel, chunks), out_shape=[...  61.5 us

profile of v7, /device:TPU:1, one launch (start us, length us, event | category | flops | bytes accessed | tf_op | source)
XLA Modules:
  0.0 422.9 jit_solution(15991414198447837511)
XLA Ops:
  0.6 0.8 slice_reduce_fusion.2
  1.5 0.7 convert_reduce_fusion.1
  2.2 0.1 reshape.67
  2.3 0.7 stack.23
  3.0 0.7 fusion.5.small_in
  3.7 0.6 pad.15.piece_ref
  4.3 0.8 maximum_convert_fusion
  5.1 0.6 reshape.66.mod_bias.proj_bias.bias
  5.7 1.1 copy.28
  6.8 0.9 reshape.60.s_qkv
  7.7 177.2 %shard_map.228 = (f32[1,6912]{1,0:T(1,128)}, bf16[16,8,128]{2,1,0:T(8,128)(2,1)}, f32[1,1152]{1,0:T(1,128)}, bf16[1024,1152]{1,0:T(8,128)(2,1)}, bf16[24,72,1024...) custom-call(bf16[16,8,128]{2,1,0:T(8,128)(2,1)} %pad.15.piece_ref, ...), custom_call_target="tpu_custom_call" | custom-call | tf_op jit(solution)/shard_map/pallas_call | solution.py:1337
  185.0 0.8 slice.34
  185.7 61.5 %shard_map.229 = (f32[1,2304]{1,0:T(1,128)}, f32[72,2304]{1,0:T(8,128)}, bf16[16,72,2304]{2,1,0:T(8,128)(2,1)}, f32[512,1152]{1,0:T(8,128)}, f32[512,1152]{1,0:T(8,128)}) custom-call(f32[8,1152]{1,0:T(8,128)} %reshape.66.mod_bias.proj_bias.bias, bf16[1024,1152]{1,0:T(8,128)(2,1)} %get-tuple-element.53.grad_m_in, ...), custom_call_target="tpu_custom_call" | custom-call | tf_op jit(solution)/shard_map/pallas_call | solution.py:1514
  247.3 83.7 %shard_map.230 = (f32[8,1152]{1,0:T(8,128)}, f32[72,2304]{1,0:T(8,128)}, f32[72,576]{1,0:T(8,128)}, bf16[512,1152]{1,0:T(8,128)(2,1)}, f32[512,1152]{1,0:T(8,128)}, /*index=5*/bf16[24,72,1024]{2,1,0:T(8,128)(2,1)}) custom-call(f32[1,6912]{1,0:T(1,128)} %get-tuple-element.51.mod.mod_ref, f32[512,1152]{1,0:T(8,128)} %get-tuple-element.52.resid_in, ...), custom_call_target="tpu_custom_call" | custom-call | tf_op jit(solution)/shard_map/pallas_call | solution.py:1678
  331.0 0.0 copy-start.6
  331.0 76.8 %shard_map.231 = (bf16[512,1152]{1,0:T(8,128)(2,1)}, f32[3,72,576]{2,1,0:T(8,128)}, f32[16,8,128]{2,1,0:T(8,128)}, bf16[16,1,2304]{2,1,0:T(2,128)(2,1)}, bf16[16...) custom-call(f32[1,6912]{1,0:T(1,128)} %get-tuple-element.51.mod.mod_ref, ...), custom_call_target="tpu_custom_call" | custom-call | tf_op jit(solution)/shard_map/pallas_call | solution.py:984
  407.8 0.0 copy-start
  407.8 1.0 slice_reduce_fusion
  408.8 0.1 reshape_squeeze.3
  408.9 0.0 copy-done.6
  408.9 0.6 fusion.7
  409.5 1.0 reduce_sum.29
  410.5 1.1 reduce_sum.28
  411.6 0.6 fusion.12
  412.2 0.6 slice.43
  412.8 0.6 pad_maximum_fusion.2
  413.4 0.9 copy.39
  414.3 1.0 copy.38
  415.3 0.0 copy-start.1
  415.3 0.7 convert_reduce_fusion
  416.0 1.7 fusion
  417.7 0.0 copy-done
  417.7 0.0 copy-start.4
  417.7 0.0 copy-start.5
  417.7 1.0 copy.46
  418.7 0.0 copy-done.1
  418.7 0.0 copy-start.3
  418.7 0.0 copy-start.2
  418.7 1.0 copy.47
  419.8 0.0 copy-done.4
  419.8 0.8 copy.48
  420.6 0.0 copy-done.5
  420.6 0.7 copy.49
  421.2 0.0 copy-done.3
  421.2 0.8 copy.50
  422.1 0.0 copy-done.2
  422.1 0.8 copy.51
  (7 shorter events, 0.0 us)
Async XLA Ops:
  331.0 77.9 %copy-start.6 = (bf16[1,1152]{1,0:T(2,128)(2,1)S(1)}, bf16[1,1152]{1,0:T(2,128)(2,1)}, u32[]{:S(2)}) copy-start(bf16[1,1152]{1,0:T(2,128)(2,1)} %param.14) | copy-start | bytes 6916
  407.8 9.9 %copy-start = (bf16[512,1152]{1,0:T(8,128)(2,1)S(1)}, bf16[512,1152]{1,0:T(8,128)(2,1)}, u32[]{:S(2)}) copy-start(bf16[512,1152]{1,0:T(8,128)(2,1)} %get-tuple-element.69) | copy-start | bytes 3538948
  415.3 3.4 copy-start.1
  417.7 2.0 copy-start.4
  417.7 2.8 copy-start.5
  418.7 2.5 copy-start.3
  418.7 3.3 copy-start.2
